TPU v7x, 768 devices: a whole 4x8x12 slice. The times are simulated.
768 devices in a mesh: dp: 128 (over z_hi, y, x), tensor: 6 (over z_lo, core).
Axes of the slice: x: 4, y: 8, z: 12 (z_hi: 4, z_lo: 3; z = z_hi * 3 + z_lo), core: 2. Of those that a mesh axis runs over, the one named last changes fastest.
Arguments:
- normed: bfloat16 [65536, 8192], P('dp'), may hold values from -12 to 12
- key_cot: bfloat16 [65536, 768], P('dp', 'tensor'), may hold values from -6 to 6
- key_weight: bfloat16 [8192, 768], P(None, 'tensor'), may hold values from -0.0625 to 0.0625
- norm_gain: bfloat16 [8192], replicated, may hold values from 0.5 to 1.5
- weight_master: float32 [8192, 768], P('dp', 'tensor'), may hold values from -0.0625 to 0.0625
- weight_moment: float32 [8192, 768], P('dp', 'tensor'), may hold values from -0.00239208 to 0.00239208
- weight_second: float32 [8192, 768], P('dp', 'tensor'), may hold values from 3.1789146e-08 to 7.947286e-07
- gain_master: float32 [8192], P('dp'), may hold values from 0.5 to 1.5
- gain_moment: float32 [8192], P('dp'), may hold values from -0.00239208 to 0.00239208
- gain_second: float32 [8192], P('dp'), may hold values from 3.1789146e-08 to 7.947286e-07
- next_input: bfloat16 [8192, 8192], P('dp'), may hold values from -6 to 6
Outputs:
- next_keys: bfloat16 [8192, 768], P('dp', 'tensor')
- weight_master_new: float32 [8192, 768], P('dp', 'tensor')
- weight_moment_new: float32 [8192, 768], P('dp', 'tensor')
- weight_second_new: float32 [8192, 768], P('dp', 'tensor')
- gain_master_new: float32 [8192], P('dp')
- gain_moment_new: float32 [8192], P('dp')
- gain_second_new: float32 [8192], P('dp')
All inputs are finite; a program needn't handle non-finite values.
Results may differ from a plain program's by a relative error of at most 0.001.
The roundings to bfloat16 on the way count: a program that leaves them out, or rounds other values in their place, can miss the bound.
Values may be sent and summed in bfloat16 or wider, within the bound.
No kernel may reach another device: no remote copies, remote signals or barrier semaphores. Data moves between devices by JAX's collectives and lax.ppermute only.
A program may use at most 64 MiB of HBM per device.

v0:
```python
import jax
import jax.numpy as jnp
from jax import lax
from jax.sharding import PartitionSpec as P

beta_one = 0.9
beta_two = 0.95
adam_eps = 1e-08
learn_rate = 0.001
rms_eps = 1e-05
step_count = 10


def adam_update(grad, master, moment, second, decay):
    moment_new = beta_one * moment + (1.0 - beta_one) * grad
    second_new = beta_two * second + (1.0 - beta_two) * grad * grad
    corr_one = 1.0 - beta_one**step_count
    corr_two = 1.0 - beta_two**step_count
    update = moment_new / corr_one / (jnp.sqrt(second_new / corr_two) + adam_eps) + decay * master
    return (master - learn_rate * update, moment_new, second_new)


def bucket_terms(scaled, normed, key_cot, key_weight):
    weight_term = jnp.einsum("td,tc->dc", scaled, key_cot, preferred_element_type=jnp.float32)
    inner = jnp.einsum("td,tc->dc", normed, key_cot, preferred_element_type=jnp.float32)
    gain_term = jnp.sum(key_weight.astype(jnp.float32) * inner, axis=1)
    return (weight_term, gain_term)


def local(
    normed,
    key_cot,
    key_weight,
    norm_gain,
    weight_master,
    weight_moment,
    weight_second,
    gain_master,
    gain_moment,
    gain_second,
    next_input,
):
    heads = lax.axis_size("tensor")
    scaled = (normed.astype(jnp.float32) * norm_gain.astype(jnp.float32)[None, :]).astype(
        jnp.bfloat16
    )
    weight_term, gain_term = bucket_terms(scaled, normed, key_cot, key_weight)
    key_grad, gain_part = (
        lax.psum_scatter(weight_term, "dp", scatter_dimension=0, tiled=True),
        lax.psum_scatter(gain_term, "dp", scatter_dimension=0, tiled=True),
    )
    gain_grad = lax.psum(gain_part, "tensor")
    local_sum = jnp.sum(key_grad * key_grad) + jnp.sum(gain_grad * gain_grad) / heads
    total = lax.psum(local_sum, ("dp", "tensor"))
    clip = jnp.minimum(1.0, 1.0 / (jnp.sqrt(total) + 1e-06))
    weight_new, weight_moment_new, weight_second_new = adam_update(
        clip * key_grad, weight_master, weight_moment, weight_second, 0.1
    )
    gain_new, gain_moment_new, gain_second_new = adam_update(
        clip * gain_grad, gain_master, gain_moment, gain_second, 0.0
    )
    weight_param = weight_new.astype(jnp.bfloat16)
    gain_param = gain_new.astype(jnp.bfloat16)
    hidden = next_input.astype(jnp.float32)
    inverse = lax.rsqrt(jnp.mean(hidden * hidden, axis=1, keepdims=True) + rms_eps)
    rescaled = hidden * inverse
    weight_piece = lax.all_gather(weight_param, "dp", axis=0, tiled=True)
    gain_piece = lax.all_gather(gain_param, "dp", axis=0, tiled=True)
    mixed = (rescaled * gain_piece.astype(jnp.float32)[None, :]).astype(jnp.bfloat16)
    next_keys = jnp.dot(mixed, weight_piece, preferred_element_type=jnp.float32)
    return (
        next_keys.astype(jnp.bfloat16),
        weight_new,
        weight_moment_new,
        weight_second_new,
        gain_new,
        gain_moment_new,
        gain_second_new,
    )


def solution(mesh):
    return jax.shard_map(
        local,
        mesh=mesh,
        in_specs=(
            P("dp", None),
            P("dp", "tensor"),
            P(None, "tensor"),
            P(),
            P("dp", "tensor"),
            P("dp", "tensor"),
            P("dp", "tensor"),
            P("dp"),
            P("dp"),
            P("dp"),
            P("dp", None),
        ),
        out_specs=(
            P("dp", "tensor"),
            P("dp", "tensor"),
            P("dp", "tensor"),
            P("dp", "tensor"),
            P("dp"),
            P("dp"),
            P("dp"),
        ),
        check_vma=False,
    )
```

profile of v0, /device:TPU:128, one launch (start us, length us, event | category | flops | bytes accessed | tf_op | source)
XLA Modules:
  0.0 1778.3 jit_solution(16000040584866139262)
XLA Ops:
  7.2 0.0 copy-start
  7.2 0.0 reduce-scatter.2.cloned.1.call-start
  7.2 0.8 convert_element_type.32
  8.0 0.1 copy-done
  8.1 7.8 fusion
  15.9 0.0 copy-start.1
  15.9 0.0 reduce-scatter.2.cloned.1.call-update
  15.9 0.0 all-gather.2.cloned.1.call-start
  16.0 1.5 copy-done.1
  17.5 3.0 copy.19
  20.5 1.3 fusion.15
  22.5 0.0 copy-start.3
  22.5 0.0 copy-start.4
  22.5 0.0 copy-start.5
  22.5 0.0 copy-start.2
  22.5 0.0 copy-start.6
  22.5 0.0 copy-start.7
  22.6 0.0 copy-start.8
  22.6 5.8 fusion.5
  28.3 815.2 %all-reduce.1 = f32[8192]{0:T(1024)S(1)} all-reduce(f32[8192]{0:T(1024)S(1)} %fusion.5), channel_id=3, replica_groups=mesh['dp'=128,'tensor'=6] {'dp'}, use_global_device_ids=true, to_apply=%region_4.0.clone | all-reduce | flops 8192 | bytes 65536
  843.5 0.1 dynamic-slice.2
  843.6 8.7 psum.14
  852.3 0.6 multiply_reduce_fusion.1
  853.5 0.0 reduce-scatter.2.cloned.1.call-done
  853.5 1.4 multiply_reduce_fusion
  855.6 103.2 %psum.15 = f32[]{:T(128)} all-reduce(f32[]{:T(128)S(6)} %add.57), channel_id=1, replica_groups=mesh['dp'=128,'tensor'=6] {'dp','tensor'}, use_global_device_ids=true, to_apply=%region_7.0 | all-reduce | flops 1 | bytes 8 | tf_op jit(solution)/shard_map/psum | solution.py:54
  959.5 0.0 copy-done.3
  959.5 0.0 copy-done.4
  959.5 0.0 copy-done.5
  959.5 1.4 fusion.13
  961.0 0.0 all-gather.2.cloned.1.call-update
  961.6 0.0 copy-done.2
  961.6 0.3 fusion.2
  962.0 0.0 copy-done.6
  962.0 0.0 copy-done.7
  962.0 0.0 copy-done.8
  962.0 0.5 fusion.11
  962.5 0.2 dynamic-update-slice
  962.7 806.0 %all-reduce = bf16[8192]{0:T(1024)(128)(2,1)S(1)} all-reduce(bf16[8192]{0:T(1024)(128)(2,1)S(1)} %dynamic-update-slice), channel_id=1, replica_groups=mesh['dp'=128,'tensor'=6] {'dp'}, use_global_device_ids=true, to_apply=%add | all-reduce | flops 8192 | bytes 32768
  1768.7 0.0 all-gather.2.cloned.1.call-done
  1768.7 2.7 convolution_convert_fusion
  (3 shorter events, 0.0 us)
Async XLA Ops:
  7.2 0.9 copy-start
  7.2 846.4 %reduce-scatter.2.cloned.1.call-start = ((), (), s32[]{:S(2)}) async-start(), calls=%async_computation.1 | async-start | bytes 4227072 | tf_op jit(solution)/shard_map/reduce_scatter | solution.py:49
  15.9 1.6 copy-start.1
  15.9 1752.8 %all-gather.2.cloned.1.call-start = ((), (), s32[]{:S(2)}) async-start(), calls=%async_computation.2 | async-start | bytes 2113536 | tf_op jit(solution)/shard_map/all_gather | solution.py:67
  22.5 937.0 %copy-start.3 = (f32[64,128]{1,0:T(8,128)S(1)}, f32[64,128]{1,0:T(8,128)}, u32[]{:S(2)}) copy-start(f32[64,128]{1,0:T(8,128)} %param.15) | copy-start | bytes 98308
  22.5 937.0 %copy-start.4 = (f32[64,128]{1,0:T(8,128)S(1)}, f32[64,128]{1,0:T(8,128)}, u32[]{:S(2)}) copy-start(f32[64,128]{1,0:T(8,128)} %param.16) | copy-start | bytes 98308
  22.5 937.0 %copy-start.5 = (f32[64,128]{1,0:T(8,128)S(1)}, f32[64,128]{1,0:T(8,128)}, u32[]{:S(2)}) copy-start(f32[64,128]{1,0:T(8,128)} %param.17) | copy-start | bytes 98308
  22.5 939.1 %copy-start.2 = (bf16[64,8192]{1,0:T(8,128)(2,1)S(1)}, bf16[64,8192]{1,0:T(8,128)(2,1)}, u32[]{:S(2)}) copy-start(bf16[64,8192]{1,0:T(8,128)(2,1)} %param.21) | copy-start | bytes 3145732
  22.5 939.4 %copy-start.6 = (f32[64]{0:T(128)S(1)}, f32[64]{0:T(128)}, u32[]{:S(2)}) copy-start(f32[64]{0:T(128)} %param.18) | copy-start | bytes 772
  22.5 939.4 %copy-start.7 = (f32[64]{0:T(128)S(1)}, f32[64]{0:T(128)}, u32[]{:S(2)}) copy-start(f32[64]{0:T(128)} %param.19) | copy-start | bytes 772
  22.6 939.4 %copy-start.8 = (f32[64]{0:T(128)S(1)}, f32[64]{0:T(128)}, u32[]{:S(2)}) copy-start(f32[64]{0:T(128)} %param.20) | copy-start | bytes 772
Sparse Core Ops, SparseCore 0:
  16.1 829.5 reduce-scatter.1
  961.1 130.8 all-gather.1
where the time goes:
time: 1780 us
  blocking collectives  1730 us (97%)
    unnamed x2, blocking collectives  1620 us
    psum x1, blocking collectives, local(): total = lax.psum(local_sum, ('dp', 'tensor'))  103 us
  transfers between devices with their start and end apart: 2, of which 0 were waited for; matrix products, arithmetic and copies ran while one was open for 1% of the time, Pallas kernels for 0%

commit v1 on v0

v1 whole, which is shorter than its diff:
```python
import jax
import jax.numpy as jnp
from jax import lax
from jax.sharding import Mesh, PartitionSpec as P

beta_one = 0.9
beta_two = 0.95
adam_eps = 1e-08
learn_rate = 0.001
rms_eps = 1e-05
step_count = 10

ZH, Y, X, ZL, CORE = 4, 8, 4, 3, 2
AXES = ("zh", "y", "x", "zl", "core")
DP = ("zh", "y", "x")
TENSOR = ("zl", "core")
ROWS = 64
GROUP = ZH * ROWS


def adam_update(grad, master, moment, second, decay):
    moment_new = beta_one * moment + (1.0 - beta_one) * grad
    second_new = beta_two * second + (1.0 - beta_two) * grad * grad
    corr_one = 1.0 - beta_one**step_count
    corr_two = 1.0 - beta_two**step_count
    update = moment_new / corr_one / (jnp.sqrt(second_new / corr_two) + adam_eps) + decay * master
    return (master - learn_rate * update, moment_new, second_new)


def pack(rows, gains, pad):
    zeros = jnp.zeros(gains.shape[:-2] + (pad - 2, 128), gains.dtype)
    return jnp.concatenate([rows, gains, zeros], axis=-2)


def spread(array, axes, size):
    copies = jnp.broadcast_to(array[None], (size,) + array.shape)
    return lax.all_to_all(copies, axes, 0, 0, tiled=True)


def local(
    normed,
    key_cot,
    key_weight,
    norm_gain,
    weight_master,
    weight_moment,
    weight_second,
    gain_master,
    gain_moment,
    gain_second,
    next_input,
):
    f32 = jnp.float32
    zh = lax.axis_index("zh")
    state = jnp.stack([weight_master, weight_moment, weight_second])
    gain_state = jnp.stack([gain_master, gain_moment, gain_second])
    gain_state = jnp.pad(gain_state[:, None, :], ((0, 0), (0, 7), (0, 64)))
    state = jnp.concatenate([state, gain_state], axis=1)
    states = lax.all_gather(state, "zh", axis=0, tiled=False)
    wide = jnp.transpose(states[:, :, :ROWS], (1, 0, 2, 3)).reshape(3, GROUP, 128)
    gain_wide = jnp.transpose(states[:, :, ROWS, :ROWS], (1, 0, 2)).reshape(3, 2, 128)

    scaled = (normed.astype(f32) * norm_gain.astype(f32)[None, :]).astype(jnp.bfloat16)
    weight_term = jnp.einsum("td,tc->dc", scaled, key_cot, preferred_element_type=f32)
    inner = jnp.einsum("td,tc->dc", normed, key_cot, preferred_element_type=f32)
    gain_term = jnp.sum(key_weight.astype(f32) * inner, axis=1)
    weight_term = jnp.transpose(weight_term.reshape(ZH, Y, X, ROWS, 128), (2, 1, 0, 3, 4))
    gain_term = jnp.transpose(gain_term.reshape(ZH, Y, X, ROWS), (2, 1, 0, 3))
    grads = pack(weight_term.reshape(X, Y, GROUP, 128), gain_term.reshape(X, Y, 2, 128), 8)

    grads = jnp.sum(lax.all_to_all(grads, "x", 0, 0, tiled=True), axis=0)
    grads = jnp.sum(lax.all_to_all(grads, "y", 0, 0, tiled=True), axis=0)
    grads = jnp.sum(lax.all_gather(grads, "zh", axis=0, tiled=False), axis=0)
    key_grad = grads[:GROUP]

    squares = jnp.sum((key_grad * key_grad).reshape(-1, 8, 128), axis=0)
    shared = jnp.concatenate([grads[GROUP:], squares], axis=0)
    shared = jnp.sum(spread(shared, TENSOR, ZL * CORE), axis=0)
    gain_grad = shared[:2]
    total = jnp.sum(shared[8:]) + jnp.sum(gain_grad * gain_grad)
    total = spread(jnp.broadcast_to(total, (8, 128)), ("y", "x"), Y * X)
    total = jnp.sum(total[:, 0, 0])
    clip = jnp.minimum(1.0, 1.0 / (jnp.sqrt(total) + 1e-06))

    weight_new, weight_moment_new, weight_second_new = adam_update(
        clip * key_grad, wide[0], wide[1], wide[2], 0.1
    )
    gain_new, gain_moment_new, gain_second_new = adam_update(
        clip * gain_grad, gain_wide[0], gain_wide[1], gain_wide[2], 0.0
    )
    param = pack(weight_new.astype(jnp.bfloat16), gain_new.astype(jnp.bfloat16), 16)

    param = lax.all_gather(param, "y", axis=0, tiled=False)
    params = spread(param, "x", X)
    weight_piece = params[:, :, :GROUP].reshape(X, Y, ZH, ROWS, 128)
    weight_piece = jnp.transpose(weight_piece, (2, 1, 0, 3, 4)).reshape(-1, 128)
    gain_piece = params[:, :, GROUP : GROUP + 2].reshape(X, Y, ZH, ROWS)
    gain_piece = jnp.transpose(gain_piece, (2, 1, 0, 3)).reshape(-1)

    hidden = next_input.astype(f32)
    inverse = lax.rsqrt(jnp.mean(hidden * hidden, axis=1, keepdims=True) + rms_eps)
    rescaled = hidden * inverse
    mixed = (rescaled * gain_piece.astype(f32)[None, :]).astype(jnp.bfloat16)
    next_keys = jnp.dot(mixed, weight_piece, preferred_element_type=f32)

    def own(array):
        return lax.dynamic_slice_in_dim(array, zh * ROWS, ROWS, 0)

    return (
        next_keys.astype(jnp.bfloat16),
        own(weight_new),
        own(weight_moment_new),
        own(weight_second_new),
        own(gain_new.reshape(GROUP)),
        own(gain_moment_new.reshape(GROUP)),
        own(gain_second_new.reshape(GROUP)),
    )


def solution(mesh):
    folded = Mesh(mesh.devices.reshape(ZH, Y, X, ZL, CORE), AXES)
    return jax.shard_map(
        local,
        mesh=folded,
        in_specs=(
            P(DP, None),
            P(DP, TENSOR),
            P(None, TENSOR),
            P(),
            P(DP, TENSOR),
            P(DP, TENSOR),
            P(DP, TENSOR),
            P(DP),
            P(DP),
            P(DP),
            P(DP, None),
        ),
        out_specs=(
            P(DP, TENSOR),
            P(DP, TENSOR),
            P(DP, TENSOR),
            P(DP, TENSOR),
            P(DP),
            P(DP),
            P(DP),
        ),
        check_vma=False,
    )
```

time: 1780 us -> 233 us (0.13)
  the two profiles are of different devices: /device:TPU:128 before, /device:TPU:192 now
where the time goes in v1:
time: 233 us; the launch traced here: 232 us
  blocking collectives  135 us (58%)
  waiting for transfers between devices  35.7 us (15%)
  starting transfers between devices  19.2 us (8%)
  local copies, waits for them, and re-layouts  15.1 us (6%)
  matrix products  14.3 us (6%)
  other arithmetic  10.2 us (4%)
  between operations  2.93 us (1%)
    all_to_all x1, blocking collectives, local(): grads = jnp.sum(lax.all_to_all(grads, 'x', 0, 0, tiled=True), axis=0)  54.4 us
    all_to_all x3, waiting for transfers between devices, spread(): return lax.all_to_all(copies, axes, 0, 0, tiled=True)  33.1 us
    all_gather x1, blocking collectives, local(): grads = jnp.sum(lax.all_gather(grads, 'zh', axis=0, tiled=False), axis=0)  29.2 us
    all_gather x1, blocking collectives, local(): param = lax.all_gather(param, 'y', axis=0, tiled=False)  25.6 us
    all_gather x1, blocking collectives, local(): states = lax.all_gather(state, 'zh', axis=0, tiled=False)  25.6 us
    all_to_all x3, starting transfers between devices, spread(): return lax.all_to_all(copies, axes, 0, 0, tiled=True)  12.1 us
    all_to_all x1, starting transfers between devices, local(): grads = jnp.sum(lax.all_to_all(grads, 'y', 0, 0, tiled=True), axis=0)  7.1 us
    dot_general x1, matrix products, local(): jnp.einsum('td,tc->dc', scaled, key_cot, preferred_element_type=f32)  5.9 us
  transfers between devices with their start and end apart: 4, of which 4 were waited for; matrix products, arithmetic and copies ran while one was open for 2% of the time, Pallas kernels for 0%

profile of v1, /device:TPU:192, one launch (start us, length us, event | category | flops | bytes accessed | tf_op | source)
XLA Modules:
  0.0 232.1 jit_solution(1266572875907456224)
XLA Ops:
  0.6 0.0 copy-start
  0.6 0.8 convert_element_type.47
  1.4 0.2 copy-done
  1.6 5.9 %fusion = f32[8192,128]{1,0:T(8,128)S(1)} fusion(bf16[512,128]{1,0:T(8,128)(2,1)S(1)} %copy-done, bf16[512,8192]{1,0:T(8,128)(2,1)} %param.11, f32[8192]{0:T(1024)S(1)} %convert_element_type.47), kind=kOutput, calls=%fused_computation.2 | convolution fusion | flops 1086324736 | bytes 12746752 | tf_op jit(solution)/shard_map/td,tc->dc/dot_general | solution.py:64
  7.5 2.5 %copy.59 = f32[4,8,4,64,128]{4,3,0,1,2:T(8,128)} copy(f32[4,8,4,64,128]{4,3,2,1,0:T(8,128)S(1)} %bitcast.57) | data formatting | bytes 8388608 | tf_op jit(solution)/shard_map/reshape | solution.py:67
  9.9 3.0 %copy.60 = bf16[8192,128]{0,1:T(8,128)(2,1)} copy(bf16[8192,128]{1,0:T(8,128)(2,1)S(1)} %copy-done.1) | data formatting | bytes 4194304 | tf_op args[2]
  12.9 5.7 %fusion.5 = f32[8192]{0:T(1024)S(1)} fusion(bf16[512,8192]{1,0:T(8,128)(2,1)} %param.11, bf16[512,128]{1,0:T(8,128)(2,1)S(1)} %copy-done, bf16[8192,128]{0,1:T(8,128)(2,1)} %copy.60), kind=kOutput, calls=%fused_computation.10 | convolution fusion | flops 1076879360 | bytes 10649600 | tf_op jit(solution)/shard_map/td,tc->dc/dot_general | solution.py:65
  18.6 0.1 reshape.90
  18.7 0.1 reshape.91
  18.9 0.1 pad.12.clone
  18.9 2.6 %maximum_maximum_fusion = f32[4,8,264,128]{3,2,1,0:T(8,128)S(1)} fusion(f32[4,8,2,128]{3,2,1,0:T(2,128)S(1)} %reshape.91, f32[4,8,256,128]{3,2,1,0:T(8,128)} %bitcast.55, f32[264]{0:T(512)S(1)} %pad.12.clone), kind=kLoop, calls=%fused_computation.4 | loop fusion | flops 2162688 | bytes 8553504 | tf_op jit(solution)/shard_map/concatenate | solution.py:32
  21.5 54.4 %all_to_all.25 = f32[4,8,264,128]{3,2,1,0:T(8,128)} all-to-all(f32[4,8,264,128]{3,2,1,0:T(8,128)S(1)} %maximum_maximum_fusion), channel_id=1, replica_groups=mesh['zh'=4,'y'=8,'x'=4,'zl'=3,'core'=2] {'x'}, dimensions={0} | all-to-all | bytes 8650752 | tf_op jit(solution)/shard_map/all_to_all | solution.py:71
  76.0 3.5 %reduce_sum.92 = f32[8,264,128]{2,1,0:T(8,128)} reduce(f32[4,8,264,128]{3,2,1,0:T(8,128)} %all_to_all.25, f32[]{:T(128)} %constant.19.clone.1), dimensions={0}, to_apply=%region_2.3 | reduce | flops 811008 | bytes 5406724 | tf_op jit(solution)/shard_map/reduce_sum | solution.py:71
  79.5 7.1 %all-to-all-start.1 = ((f32[8,264,128]{2,1,0:T(8,128)}), f32[8,264,128]{2,1,0:T(8,128)S(1)}, u32[]{:S(2)}, u32[]{:S(2)}) async-start(f32[8,264,128]{2,1,0:T(8,128)} %reduce_sum.92), calls=%async_computation.1 | async-start | bytes 2162688 | tf_op jit(solution)/shard_map/all_to_all | solution.py:72
  86.7 25.6 %all-gather = f32[12,72,128]{2,1,0:T(8,128)S(1)} all-gather(f32[3,72,128]{2,1,0:T(8,128)S(1)} %select_maximum_fusion), channel_id=2, replica_groups=mesh['zh'=4,'y'=8,'x'=4,'zl'=3,'core'=2] {'zh'}, dimensions={0}, use_global_device_ids=true | all-gather | bytes 552960 | tf_op jit(solution)/shard_map/all_gather | solution.py:59
  112.3 2.6 %all-to-all-done.1 = f32[8,264,128]{2,1,0:T(8,128)S(1)} async-done(((f32[8,264,128]{2,1,0:T(8,128)}), f32[8,264,128]{2,1,0:T(8,128)S(1)}, u32[]{:S(2)}, u32[]{:S(2)}) %all-to-all-start.1) | async-done | bytes 1081376 | tf_op jit(solution)/shard_map/all_to_all | solution.py:72
  114.9 0.1 reduce_sum.93
  114.9 29.2 %all-gather.1 = f32[1056,128]{1,0:T(8,128)S(1)} all-gather(f32[264,128]{1,0:T(8,128)S(1)} %reduce_sum.93), channel_id=3, replica_groups=mesh['zh'=4,'y'=8,'x'=4,'zl'=3,'core'=2] {'zh'}, dimensions={0}, use_global_device_ids=true | all-gather | bytes 675840 | tf_op jit(solution)/shard_map/all_gather | solution.py:73
  144.2 0.6 broadcast_in_dim.12
  144.9 4.6 %all-to-all-start.2 = ((f32[6,16,128]{2,1,0:T(8,128)}), f32[6,16,128]{2,1,0:T(8,128)S(1)}, u32[]{:S(2)}, u32[]{:S(2)}) async-start(f32[6,16,128]{2,1,0:T(8,128)} %broadcast_in_dim.12), calls=%async_computation.2 | async-start | bytes 98304 | tf_op jit(solution)/shard_map/all_to_all | solution.py:37
  149.5 6.2 %all-to-all-done.2 = f32[6,16,128]{2,1,0:T(8,128)S(1)} async-done(((f32[6,16,128]{2,1,0:T(8,128)}), f32[6,16,128]{2,1,0:T(8,128)S(1)}, u32[]{:S(2)}, u32[]{:S(2)}) %all-to-all-start.2) | async-done | bytes 49184 | tf_op jit(solution)/shard_map/all_to_all | solution.py:37
  155.7 0.6 multiply_reduce_fusion
  156.3 0.6 slice_reduce_fusion.1
  158.2 0.6 broadcast_in_dim_broadcast_in_dim_broadcast_in_dim.3
  158.9 3.9 %all-to-all-start.3 = ((f32[32,8,128]{2,1,0:T(8,128)}), f32[32,8,128]{2,1,0:T(8,128)S(1)}, u32[]{:S(2)}, u32[]{:S(2)}) async-start(f32[32,8,128]{2,1,0:T(8,128)} %broadcast_in_dim_broadcast_in_dim_broadcast_in_dim.3), calls=%async_computation.3 | async-start | bytes 262144 | tf_op jit(solution)/shard_map/all_to_all | solution.py:37
  162.8 0.1 mul.165
  162.8 0.1 mul.172
  162.9 0.1 squeeze.16
  163.0 0.1 pad.7.clone
  163.1 10.3 %all-to-all-done.3 = f32[32,8,128]{2,1,0:T(8,128)S(1)} async-done(((f32[32,8,128]{2,1,0:T(8,128)}), f32[32,8,128]{2,1,0:T(8,128)S(1)}, u32[]{:S(2)}, u32[]{:S(2)}) %all-to-all-start.3) | async-done | bytes 131104 | tf_op jit(solution)/shard_map/all_to_all | solution.py:37
  173.4 0.6 slice_reduce_fusion
  174.8 0.8 fusion.15
  175.6 0.1 maximum_maximum_fusion.1
  175.7 25.6 %all-gather.2 = bf16[2176,128]{1,0:T(8,128)(2,1)S(1)} all-gather(bf16[272,128]{1,0:T(8,128)(2,1)S(1)} %maximum_maximum_fusion.1), channel_id=4, replica_groups=mesh['zh'=4,'y'=8,'x'=4,'zl'=3,'core'=2] {'y'}, dimensions={0}, use_global_device_ids=true | all-gather | bytes 626688 | tf_op jit(solution)/shard_map/all_gather | solution.py:93
  201.3 1.7 broadcast_in_dim.28
  203.0 3.6 %all-to-all-start.4 = ((bf16[4,8,272,128]{3,2,1,0:T(8,128)(2,1)}), bf16[4,8,272,128]{3,2,1,0:T(8,128)(2,1)S(1)}, u32[]{:S(2)}, u32[]{:S(2)}) async-start(bf16[4,8,272,128]{3,2,1,0:T(8,128)(2,1)} %broadcast_in_dim.28), calls=%async_computation.4 | async-start | bytes 4456448 | tf_op jit(solution)/shard_map/all_to_all | solution.py:37
  206.6 0.3 fusion.2
  206.9 0.6 dynamic_slice.21
  207.5 0.6 dynamic_slice.22
  208.1 0.6 dynamic_slice.23
  208.7 0.6 constant_dynamic-slice_fusion.2
  209.3 1.4 constant_dynamic-slice_fusion
  210.7 16.7 %all-to-all-done.4 = bf16[4,8,272,128]{3,2,1,0:T(8,128)(2,1)S(1)} async-done(((bf16[4,8,272,128]{3,2,1,0:T(8,128)(2,1)}), bf16[4,8,272,128]{3,2,1,0:T(8,128)(2,1)S(1)}, u32[]{:S(2)}, u32[]{:S(2)}) %all-to-all-start.4) | async-done | bytes 2228256 | tf_op jit(solution)/shard_map/all_to_all | solution.py:37
  227.4 0.3 slice.80
  227.7 1.5 copy.65
  229.2 0.1 reshape.99
  229.4 0.1 reshape.98
  229.5 2.7 %convolution_convert_fusion = bf16[64,128]{1,0:T(8,128)(2,1)} fusion(bf16[8192,128]{1,0:T(8,128)(2,1)} %bitcast.60, bf16[64,8192]{1,0:T(8,128)(2,1)S(1)} %copy-done.2, f32[8192]{0:T(1024)S(1)} %reshape.98, f32[64]{0:T(128)S(1)} %add_rsqrt_fusion), kind=kOutput, calls=%fused_computation.11 | convolution fusion | flops 136323072 | bytes 3195136 | tf_op jit(solution)/shard_map/dot_general | solution.py:104
  (36 shorter events, 0.3 us)
Async XLA Ops:
  0.6 0.9 copy-start
  7.5 2.5 %copy-start.1 = (bf16[8192,128]{1,0:T(8,128)(2,1)S(1)}, bf16[8192,128]{1,0:T(8,128)(2,1)}, u32[]{:S(2)}) copy-start(bf16[8192,128]{1,0:T(8,128)(2,1)} %param.13) | copy-start | bytes 6291460
  76.0 10.7 %copy-start.6 = (f32[64]{0:T(128)S(1)}, f32[64]{0:T(128)}, u32[]{:S(2)}) copy-start(f32[64]{0:T(128)} %param.20) | copy-start | bytes 772
  76.0 10.7 %copy-start.7 = (f32[64]{0:T(128)S(1)}, f32[64]{0:T(128)}, u32[]{:S(2)}) copy-start(f32[64]{0:T(128)} %param.19) | copy-start | bytes 772
  76.0 10.7 %copy-start.8 = (f32[64]{0:T(128)S(1)}, f32[64]{0:T(128)}, u32[]{:S(2)}) copy-start(f32[64]{0:T(128)} %param.18) | copy-start | bytes 772
  76.0 10.7 %copy-start.3 = (f32[64,128]{1,0:T(8,128)S(1)}, f32[64,128]{1,0:T(8,128)}, u32[]{:S(2)}) copy-start(f32[64,128]{1,0:T(8,128)} %param.17) | copy-start | bytes 98308
  76.0 10.7 %copy-start.4 = (f32[64,128]{1,0:T(8,128)S(1)}, f32[64,128]{1,0:T(8,128)}, u32[]{:S(2)}) copy-start(f32[64,128]{1,0:T(8,128)} %param.16) | copy-start | bytes 98308
  76.0 10.7 %copy-start.5 = (f32[64,128]{1,0:T(8,128)S(1)}, f32[64,128]{1,0:T(8,128)}, u32[]{:S(2)}) copy-start(f32[64,128]{1,0:T(8,128)} %param.15) | copy-start | bytes 98308
  79.5 35.3 %all-to-all-start.1 = ((f32[8,264,128]{2,1,0:T(8,128)}), f32[8,264,128]{2,1,0:T(8,128)S(1)}, u32[]{:S(2)}, u32[]{:S(2)}) async-start(f32[8,264,128]{2,1,0:T(8,128)} %reduce_sum.92), calls=%async_computation.1 | async-start | bytes 2162688 | tf_op jit(solution)/shard_map/all_to_all | solution.py:72
  144.9 10.9 %all-to-all-start.2 = ((f32[6,16,128]{2,1,0:T(8,128)}), f32[6,16,128]{2,1,0:T(8,128)S(1)}, u32[]{:S(2)}, u32[]{:S(2)}) async-start(f32[6,16,128]{2,1,0:T(8,128)} %broadcast_in_dim.12), calls=%async_computation.2 | async-start | bytes 98304 | tf_op jit(solution)/shard_map/all_to_all | solution.py:37
  158.9 14.5 %all-to-all-start.3 = ((f32[32,8,128]{2,1,0:T(8,128)}), f32[32,8,128]{2,1,0:T(8,128)S(1)}, u32[]{:S(2)}, u32[]{:S(2)}) async-start(f32[32,8,128]{2,1,0:T(8,128)} %broadcast_in_dim_broadcast_in_dim_broadcast_in_dim.3), calls=%async_computation.3 | async-start | bytes 262144 | tf_op jit(solution)/shard_map/all_to_all | solution.py:37
  175.6 31.0 %copy-start.2 = (bf16[64,8192]{1,0:T(8,128)(2,1)S(1)}, bf16[64,8192]{1,0:T(8,128)(2,1)}, u32[]{:S(2)}) copy-start(bf16[64,8192]{1,0:T(8,128)(2,1)} %param.21) | copy-start | bytes 3145732
  203.0 24.4 %all-to-all-start.4 = ((bf16[4,8,272,128]{3,2,1,0:T(8,128)(2,1)}), bf16[4,8,272,128]{3,2,1,0:T(8,128)(2,1)S(1)}, u32[]{:S(2)}, u32[]{:S(2)}) async-start(bf16[4,8,272,128]{3,2,1,0:T(8,128)(2,1)} %broadcast_in_dim.28), calls=%async_computation.4 | async-start | bytes 4456448 | tf_op jit(solution)/shard_map/all_to_all | solution.py:37

commit v2 on v1

v2 whole, which is shorter than its diff:
```python
import jax
import jax.numpy as jnp
from jax import lax
from jax.experimental import pallas as pl
from jax.experimental.pallas import tpu as pltpu
from jax.sharding import Mesh, PartitionSpec as P

beta_one = 0.9
beta_two = 0.95
adam_eps = 1e-08
learn_rate = 0.001
rms_eps = 1e-05
step_count = 10

ZH, Y, X, ZL, CORE = 4, 8, 4, 3, 2
AXES = ("zh", "y", "x", "zl", "core")
DP = ("zh", "y", "x")
TENSOR = ("zl", "core")
ROWS = 64
GROUP = ZH * ROWS
PADDED = GROUP + 16
SUMMED = GROUP + 8
GAIN_SCALE = 2.0**-6
SUM_SCALE = 2.0**-2
F32 = jnp.float32
BF16 = jnp.bfloat16
F16 = jnp.float16


def adam_update(grad, master, moment, second, decay):
    moment_new = beta_one * moment + (1.0 - beta_one) * grad
    second_new = beta_two * second + (1.0 - beta_two) * grad * grad
    corr_one = 1.0 - beta_one**step_count
    corr_two = 1.0 - beta_two**step_count
    update = moment_new / corr_one / (jnp.sqrt(second_new / corr_two) + adam_eps) + decay * master
    return (master - learn_rate * update, moment_new, second_new)


def gradient_kernel(*refs):
    normed, gain, weight = refs[0:4], refs[4:8], refs[8:12]
    cot, out = refs[12][...], refs[13]
    gains = []
    for z in range(ZH):
        saved = normed[z][...].astype(F32)
        scaled = (saved * gain[z][...].astype(F32)).astype(BF16)
        term = lax.dot_general(cot, scaled, (((0,), (0,)), ((), ())), preferred_element_type=F32)
        term = term.T
        for x in range(X):
            out[x, 0, z * ROWS : (z + 1) * ROWS, :] = term[x * ROWS : (x + 1) * ROWS]
        mixed = lax.dot_general(
            cot, weight[z][...], (((1,), (1,)), ((), ())), preferred_element_type=F32
        )
        gains.append(jnp.sum(saved * mixed, axis=0, keepdims=True))
    for x in range(X):
        part = [g[:, x * ROWS : (x + 1) * ROWS] for g in gains]
        pairs = [jnp.concatenate(part[i : i + 2], axis=1) for i in (0, 2)]
        rows = jnp.concatenate([*pairs, jnp.zeros((6, 128), F32)], axis=0)
        out[x, 0, GROUP:, :] = rows * GAIN_SCALE


def gradients(normed, key_cot, key_weight, norm_gain):
    tokens = normed.shape[0]
    gain = norm_gain.reshape(1, -1)
    return pl.pallas_call(
        gradient_kernel,
        grid=(Y,),
        in_specs=[
            *[pl.BlockSpec((tokens, GROUP), lambda y, z=z: (0, z * Y + y)) for z in range(ZH)],
            *[pl.BlockSpec((1, GROUP), lambda y, z=z: (0, z * Y + y)) for z in range(ZH)],
            *[pl.BlockSpec((GROUP, 128), lambda y, z=z: (z * Y + y, 0)) for z in range(ZH)],
            pl.BlockSpec((tokens, 128), lambda y: (0, 0)),
        ],
        out_specs=pl.BlockSpec((X, 1, SUMMED, 128), lambda y: (0, y, 0, 0)),
        out_shape=jax.ShapeDtypeStruct((X, Y, SUMMED, 128), F32),
        compiler_params=pltpu.CompilerParams(vmem_limit_bytes=56 << 20),
        cost_estimate=pl.CostEstimate(
            flops=2 * 2 * tokens * 8192 * 128, bytes_accessed=14 << 20, transcendentals=0
        ),
        name="gradients",
    )(*[normed] * ZH, *[gain] * ZH, *[key_weight] * ZH, key_cot)


def whole(kernel, *shapes, name, size=1 << 20):
    return pl.pallas_call(
        kernel,
        out_shape=[jax.ShapeDtypeStruct(shape, dtype) for shape, dtype in shapes],
        compiler_params=pltpu.CompilerParams(vmem_limit_bytes=12 << 20),
        cost_estimate=pl.CostEstimate(flops=size, bytes_accessed=size, transcendentals=0),
        name=name,
    )


def sum_zh_kernel(parts, grad, shared):
    total = parts[0]
    for z in range(1, ZH):
        total += parts[z]
    weight = total[:GROUP] * (1.0 / SUM_SCALE)
    gain = total[GROUP:] * (1.0 / (SUM_SCALE * GAIN_SCALE))
    grad[...] = weight
    squares = jnp.sum((weight * weight).reshape(-1, 8, 128), axis=0)
    for t in range(ZL * CORE):
        shared[t, :8] = gain
        shared[t, 8:] = squares


def sum_heads_kernel(parts, gain, norm):
    total = parts[0]
    for t in range(1, ZL * CORE):
        total += parts[t]
    gain[...] = total[:8]
    square = jnp.sum(total[:8] * total[:8] + total[8:])
    norm[...] = jnp.broadcast_to(square, norm.shape)


def update_kernel(norm, grad, gain, states, param, *outs):
    total = jnp.sum(norm[...], axis=0)
    clip = jnp.minimum(1.0, 1.0 / (jnp.sqrt(total) + 1e-06))
    wide = jnp.broadcast_to(clip[None], (ROWS // 8, 8, 128)).reshape(ROWS, 128)
    for z in range(ZH):
        span = slice(z * ROWS, (z + 1) * ROWS)
        new = adam_update(wide * grad[span], *[states[z, i, :ROWS] for i in range(3)], 0.1)
        param[span] = new[0].astype(BF16)
        for i in range(3):
            outs[i][span] = new[i]
    state = []
    for i in range(3):
        part = [states[z, i, ROWS : ROWS + 1, :ROWS] for z in range(ZH)]
        pairs = [jnp.concatenate(part[j : j + 2], axis=1) for j in (0, 2)]
        state.append(jnp.concatenate(pairs, axis=0))
    new = adam_update(clip[:2] * gain[:2], *state, 0.0)
    param[GROUP:] = jnp.concatenate([new[0], jnp.zeros((14, 128), F32)], axis=0).astype(BF16)
    for i in range(3):
        outs[3 + i][...] = new[i]


def exchange(array, axes):
    return lax.all_to_all(array, axes, 0, 0, tiled=True)


def local(
    normed,
    key_cot,
    key_weight,
    norm_gain,
    weight_master,
    weight_moment,
    weight_second,
    gain_master,
    gain_moment,
    gain_second,
    next_input,
):
    zh = lax.axis_index("zh")
    state = jnp.stack([weight_master, weight_moment, weight_second])
    gain_state = jnp.stack([gain_master, gain_moment, gain_second])
    gain_state = jnp.pad(gain_state[:, None, :], ((0, 0), (0, 7), (0, 128 - ROWS)))
    state = jnp.concatenate([state, gain_state], axis=1)
    states = lax.all_gather(state, "zh", axis=0, tiled=False)

    grads = gradients(normed, key_cot, key_weight, norm_gain)
    grads = exchange(grads.astype(F16), "x")
    grads, states = lax.optimization_barrier((grads, states))
    grads = (jnp.sum(grads.astype(F32), axis=0) * SUM_SCALE).astype(F16)
    grads = jnp.sum(exchange(grads, "y").astype(F32), axis=0)
    grads = lax.all_gather(grads, "zh", axis=0, tiled=False)
    heads = ZL * CORE
    key_grad, shared = whole(
        sum_zh_kernel, ((GROUP, 128), F32), ((heads, 16, 128), F32), name="sum_zh"
    )(grads)

    gain_grad, norm = whole(
        sum_heads_kernel, ((8, 128), F32), ((Y * X, 8, 128), F32), name="sum_heads"
    )(exchange(shared, TENSOR))
    norm = exchange(norm, ("y", "x"))
    param, *news = whole(
        update_kernel,
        ((PADDED, 128), BF16),
        *[((GROUP, 128), F32)] * 3,
        *[((2, 128), F32)] * 3,
        name="update",
    )(norm, key_grad, gain_grad, states)

    param = lax.all_gather(param, "y", axis=0, tiled=False)
    params = exchange(jnp.broadcast_to(param[None], (X,) + param.shape), "x")
    weight_piece = params[:, :, :GROUP].reshape(X, Y, ZH, ROWS, 128)
    weight_piece = jnp.transpose(weight_piece, (2, 1, 0, 3, 4)).reshape(-1, 128)
    gain_piece = params[:, :, GROUP : GROUP + 2].reshape(X, Y, ZH, ROWS)
    gain_piece = jnp.transpose(gain_piece, (2, 1, 0, 3)).reshape(-1)

    hidden = next_input.astype(F32)
    inverse = lax.rsqrt(jnp.mean(hidden * hidden, axis=1, keepdims=True) + rms_eps)
    rescaled = hidden * inverse
    mixed = (rescaled * gain_piece.astype(F32)[None, :]).astype(BF16)
    next_keys = jnp.dot(mixed, weight_piece, preferred_element_type=F32)

    def own(array):
        return lax.dynamic_slice_in_dim(array, zh * ROWS, ROWS, 0)

    return (
        next_keys.astype(BF16),
        *[own(new) for new in news[:3]],
        *[own(new.reshape(GROUP)) for new in news[3:]],
    )


def solution(mesh):
    folded = Mesh(mesh.devices.reshape(ZH, Y, X, ZL, CORE), AXES)
    shard, vector = P(DP, TENSOR), P(DP)
    return jax.shard_map(
        local,
        mesh=folded,
        in_specs=(
            P(DP, None),
            shard,
            P(None, TENSOR),
            P(),
            *[shard] * 3,
            *[vector] * 3,
            P(DP, None),
        ),
        out_specs=(shard, *[shard] * 3, *[vector] * 3),
        check_vma=False,
    )
```

time: 233 us -> 181 us (0.78)
  the two profiles are of different devices: /device:TPU:192 before, /device:TPU:64 now
where the time goes in v2:
time: 181 us; the launch traced here: 180 us
  blocking collectives  126 us (70%)
  waiting for transfers between devices  17.5 us (10%)
  Pallas kernels  10.9 us (6%)
  local copies, waits for them, and re-layouts  8.06 us (4%)
  starting transfers between devices  8.06 us (4%)
  other arithmetic  5.95 us (3%)
  matrix products  3.03 us (2%)
    all_to_all x3, blocking collectives, exchange(): return lax.all_to_all(array, axes, 0, 0, tiled=True)  44.9 us
    all_gather x1, blocking collectives, local(): grads = lax.all_gather(grads, 'zh', axis=0, tiled=False)  28.9 us
    all_gather x1, blocking collectives, local(): states = lax.all_gather(state, 'zh', axis=0, tiled=False)  26.6 us
    all_gather x1, blocking collectives, local(): param = lax.all_gather(param, 'y', axis=0, tiled=False)  25.5 us
    all_to_all x2, waiting for transfers between devices, exchange(): return lax.all_to_all(array, axes, 0, 0, tiled=True)  17.5 us
    pallas_call x1, Pallas kernels, gradients(): pl.pallas_call(gradient_kernel, grid=(Y,), in_specs=[*[pl.BlockSpec((toke...  10.5 us
    all_to_all x2, starting transfers between devices, exchange(): return lax.all_to_all(array, axes, 0, 0, tiled=True)  8.06 us
    convert_element_type x1, other arithmetic, local(): grads = exchange(grads.astype(F16), 'x')  3.88 us
  transfers between devices with their start and end apart: 2, of which 2 were waited for; matrix products, arithmetic and copies ran while one was open for 3% of the time, Pallas kernels for 0%

profile of v2, /device:TPU:64, one launch (start us, length us, event | category | flops | bytes accessed | tf_op | source)
XLA Modules:
  0.0 180.1 jit_solution(6017590879676752327)
XLA Ops:
  0.6 1.4 reshape.52.refs_4_.refs_5_.refs_6_.refs_7_
  2.0 10.5 %gradients.1 = f32[4,8,264,128]{3,2,1,0:T(8,128)} custom-call(bf16[512,8192]{1,0:T(8,128)(2,1)} %refs_3_.1, bf16[512,8192]{1,0:T(8,128)(2,1)} %refs_3_.1, bf16[512,8192]{1,0:T(8,128)(2,1)} %refs_3_.1, bf16[512,8192]{1,0:T(8,128)(2,1)} %refs_3_.1, bf16[1,8192]{1,0:T(2,128)(2,1)} %reshape.52.refs_4_.refs_5_.refs_6_.refs_7_, ...), custom_call_target="tpu_custom_call" | custom-call | flops 2147483648 | bytes 14680064 | tf_op jit(solution)/shard_map/gradients/pallas_call | solution.py:64
  12.5 3.9 %convert_element_type.40 = f16[4,8,264,128]{3,2,1,0:T(8,128)(2,1)} convert(f32[4,8,264,128]{3,2,1,0:T(8,128)} %gradients.1) | non-fusion elementwise | flops 1081344 | bytes 6488064 | tf_op jit(solution)/shard_map/convert_element_type | solution.py:161
  16.4 0.0 copy-start.3
  16.4 0.0 copy-start.4
  16.4 0.0 copy-start.5
  16.4 0.0 copy-start
  16.4 0.0 copy-start.1
  16.4 0.0 copy-start.2
  16.4 4.4 %all-to-all-start = ((f16[4,8,264,128]{3,2,1,0:T(8,128)(2,1)}), f16[4,8,264,128]{3,2,1,0:T(8,128)(2,1)S(1)}, u32[]{:S(2)}, u32[]{:S(2)}) async-start(f16[4,8,264,128]{3,2,1,0:T(8,128)(2,1)} %convert_element_type.40), calls=%async_computation | async-start | bytes 4325376 | tf_op jit(solution)/shard_map/all_to_all | solution.py:137
  20.9 0.0 copy-done.3
  20.9 0.0 copy-done.4
  20.9 0.0 copy-done.5
  20.9 0.0 copy-done
  20.9 0.0 copy-done.1
  20.9 0.0 copy-done.2
  21.0 26.6 %all-gather = f32[12,72,128]{2,1,0:T(8,128)S(1)} all-gather(f32[3,72,128]{2,1,0:T(8,128)S(1)} %select_maximum_fusion), channel_id=2, replica_groups=mesh['zh'=4,'y'=8,'x'=4,'zl'=3,'core'=2] {'zh'}, dimensions={0}, use_global_device_ids=true | all-gather | bytes 552960 | tf_op jit(solution)/shard_map/all_gather | solution.py:158
  47.6 0.3 all-to-all-done
  47.9 0.3 convert_reduce_fusion
  48.2 0.1 multiply_convert_fusion
  48.3 24.4 %all_to_all.25 = f16[8,264,128]{2,1,0:T(8,128)(2,1)S(1)} all-to-all(f16[8,264,128]{2,1,0:T(8,128)(2,1)S(1)} %multiply_convert_fusion), channel_id=1, replica_groups=mesh['zh'=4,'y'=8,'x'=4,'zl'=3,'core'=2] {'y'}, dimensions={0} | all-to-all | bytes 1081344 | tf_op jit(solution)/shard_map/all_to_all | solution.py:137
  72.7 0.1 convert_reduce_fusion.1
  72.8 28.9 %all-gather.1 = f32[1056,128]{1,0:T(8,128)S(1)} all-gather(f32[264,128]{1,0:T(8,128)S(1)} %convert_reduce_fusion.1), channel_id=3, replica_groups=mesh['zh'=4,'y'=8,'x'=4,'zl'=3,'core'=2] {'zh'}, dimensions={0}, use_global_device_ids=true | all-gather | bytes 675840 | tf_op jit(solution)/shard_map/all_gather | solution.py:165
  101.8 6.4 %all_to_all.26.parts = f32[6,16,128]{2,1,0:T(8,128)S(1)} all-to-all(f32[6,16,128]{2,1,0:T(8,128)S(1)} %get-tuple-element.21), channel_id=1, replica_groups=mesh['zh'=4,'y'=8,'x'=4,'zl'=3,'core'=2] {'zl','core'}, dimensions={0} | all-to-all | bytes 98304 | tf_op jit(solution)/shard_map/all_to_all | solution.py:137
  108.1 0.1 sum_heads.1
  108.3 14.1 %all_to_all.27.norm = f32[32,8,128]{2,1,0:T(8,128)S(1)} all-to-all(f32[32,8,128]{2,1,0:T(8,128)S(1)} %get-tuple-element.22), channel_id=1, replica_groups=mesh['zh'=4,'y'=8,'x'=4,'zl'=3,'core'=2] {'y','x'}, dimensions={0} | all-to-all | bytes 262144 | tf_op jit(solution)/shard_map/all_to_all | solution.py:137
  122.4 0.2 update.1
  122.5 25.5 %all-gather.2 = bf16[2176,128]{1,0:T(8,128)(2,1)S(1)} all-gather(bf16[272,128]{1,0:T(8,128)(2,1)S(1)} %get-tuple-element.26), channel_id=4, replica_groups=mesh['zh'=4,'y'=8,'x'=4,'zl'=3,'core'=2] {'y'}, dimensions={0}, use_global_device_ids=true | all-gather | bytes 626688 | tf_op jit(solution)/shard_map/all_gather | solution.py:183
  148.0 1.7 broadcast_in_dim.5
  149.7 3.6 %all-to-all-start.4 = ((bf16[4,8,272,128]{3,2,1,0:T(8,128)(2,1)}), bf16[4,8,272,128]{3,2,1,0:T(8,128)(2,1)S(1)}, u32[]{:S(2)}, u32[]{:S(2)}) async-start(bf16[4,8,272,128]{3,2,1,0:T(8,128)(2,1)} %broadcast_in_dim.5), calls=%async_computation.4 | async-start | bytes 4456448 | tf_op jit(solution)/shard_map/all_to_all | solution.py:137
  153.3 1.5 fusion
  154.9 0.6 dynamic_slice.21
  155.4 0.6 dynamic_slice.22
  156.0 0.6 dynamic_slice.23
  156.6 0.6 constant_dynamic-slice_fusion.2
  157.2 0.6 constant_dynamic-slice_fusion
  157.9 17.1 %all-to-all-done.4 = bf16[4,8,272,128]{3,2,1,0:T(8,128)(2,1)S(1)} async-done(((bf16[4,8,272,128]{3,2,1,0:T(8,128)(2,1)}), bf16[4,8,272,128]{3,2,1,0:T(8,128)(2,1)S(1)}, u32[]{:S(2)}, u32[]{:S(2)}) %all-to-all-start.4) | async-done | bytes 2228256 | tf_op jit(solution)/shard_map/all_to_all | solution.py:137
  175.0 0.3 slice.9
  175.3 1.5 copy.28
  176.8 0.1 reshape.59
  177.0 0.1 reshape.58
  177.1 3.0 %convolution_convert_fusion = bf16[64,128]{1,0:T(8,128)(2,1)} fusion(bf16[8192,128]{1,0:T(8,128)(2,1)} %bitcast.27, bf16[64,8192]{1,0:T(8,128)(2,1)} %param.21, f32[8192]{0:T(1024)S(1)} %reshape.58, f32[64]{0:T(128)S(1)} %add_rsqrt_fusion), kind=kOutput, calls=%fused_computation.6 | convolution fusion | flops 136323072 | bytes 3195136 | tf_op jit(solution)/shard_map/dot_general | solution.py:194
  (7 shorter events, 0.1 us)
Async XLA Ops:
  16.4 4.5 %copy-start.3 = (f32[64]{0:T(128)S(1)}, f32[64]{0:T(128)}, u32[]{:S(2)}) copy-start(f32[64]{0:T(128)} %param.20) | copy-start | bytes 772
  16.4 4.5 %copy-start.4 = (f32[64]{0:T(128)S(1)}, f32[64]{0:T(128)}, u32[]{:S(2)}) copy-start(f32[64]{0:T(128)} %param.19) | copy-start | bytes 772
  16.4 4.5 %copy-start.5 = (f32[64]{0:T(128)S(1)}, f32[64]{0:T(128)}, u32[]{:S(2)}) copy-start(f32[64]{0:T(128)} %param.18) | copy-start | bytes 772
  16.4 4.5 %copy-start = (f32[64,128]{1,0:T(8,128)S(1)}, f32[64,128]{1,0:T(8,128)}, u32[]{:S(2)}) copy-start(f32[64,128]{1,0:T(8,128)} %param.17) | copy-start | bytes 98308
  16.4 4.5 %copy-start.1 = (f32[64,128]{1,0:T(8,128)S(1)}, f32[64,128]{1,0:T(8,128)}, u32[]{:S(2)}) copy-start(f32[64,128]{1,0:T(8,128)} %param.16) | copy-start | bytes 98308
  16.4 4.5 %copy-start.2 = (f32[64,128]{1,0:T(8,128)S(1)}, f32[64,128]{1,0:T(8,128)}, u32[]{:S(2)}) copy-start(f32[64,128]{1,0:T(8,128)} %param.15) | copy-start | bytes 98308
  16.4 31.5 %all-to-all-start = ((f16[4,8,264,128]{3,2,1,0:T(8,128)(2,1)}), f16[4,8,264,128]{3,2,1,0:T(8,128)(2,1)S(1)}, u32[]{:S(2)}, u32[]{:S(2)}) async-start(f16[4,8,264,128]{3,2,1,0:T(8,128)(2,1)} %convert_element_type.40), calls=%async_computation | async-start | bytes 4325376 | tf_op jit(solution)/shard_map/all_to_all | solution.py:137
  149.7 25.3 %all-to-all-start.4 = ((bf16[4,8,272,128]{3,2,1,0:T(8,128)(2,1)}), bf16[4,8,272,128]{3,2,1,0:T(8,128)(2,1)S(1)}, u32[]{:S(2)}, u32[]{:S(2)}) async-start(bf16[4,8,272,128]{3,2,1,0:T(8,128)(2,1)} %broadcast_in_dim.5), calls=%async_computation.4 | async-start | bytes 4456448 | tf_op jit(solution)/shard_map/all_to_all | solution.py:137

commit v3 on v2

--- a/solution.py
+++ b/solution.py
@@ -22,6 +22,9 @@
 SUMMED = GROUP + 8
 GAIN_SCALE = 2.0**-6
 SUM_SCALE = 2.0**-2
+LAST_SCALE = 2.0**-3
+STATE = 512
+WIDTH = Y * GROUP
 F32 = jnp.float32
 BF16 = jnp.bfloat16
 F16 = jnp.float16
@@ -43,14 +46,15 @@
     for z in range(ZH):
         saved = normed[z][...].astype(F32)
         scaled = (saved * gain[z][...].astype(F32)).astype(BF16)
-        term = lax.dot_general(cot, scaled, (((0,), (0,)), ((), ())), preferred_element_type=F32)
+        both = [scaled, normed[z][...]]
+        term, inner = [
+            lax.dot_general(cot, rows, (((0,), (0,)), ((), ())), preferred_element_type=F32)
+            for rows in both
+        ]
         term = term.T
         for x in range(X):
             out[x, 0, z * ROWS : (z + 1) * ROWS, :] = term[x * ROWS : (x + 1) * ROWS]
-        mixed = lax.dot_general(
-            cot, weight[z][...], (((1,), (1,)), ((), ())), preferred_element_type=F32
-        )
-        gains.append(jnp.sum(saved * mixed, axis=0, keepdims=True))
+        gains.append(jnp.sum(weight[z][...].astype(F32).T * inner, axis=0, keepdims=True))
     for x in range(X):
         part = [g[:, x * ROWS : (x + 1) * ROWS] for g in gains]
         pairs = [jnp.concatenate(part[i : i + 2], axis=1) for i in (0, 2)]
@@ -80,13 +84,14 @@
     )(*[normed] * ZH, *[gain] * ZH, *[key_weight] * ZH, key_cot)
 
 
-def whole(kernel, *shapes, name, size=1 << 20):
+def whole(kernel, *shapes, name, size=1 << 20, **options):
     return pl.pallas_call(
         kernel,
         out_shape=[jax.ShapeDtypeStruct(shape, dtype) for shape, dtype in shapes],
         compiler_params=pltpu.CompilerParams(vmem_limit_bytes=12 << 20),
         cost_estimate=pl.CostEstimate(flops=size, bytes_accessed=size, transcendentals=0),
         name=name,
+        **options,
     )
 
 
@@ -94,8 +99,8 @@
     total = parts[0]
     for z in range(1, ZH):
         total += parts[z]
-    weight = total[:GROUP] * (1.0 / SUM_SCALE)
-    gain = total[GROUP:] * (1.0 / (SUM_SCALE * GAIN_SCALE))
+    weight = total[:GROUP] * (1.0 / (SUM_SCALE * LAST_SCALE))
+    gain = total[GROUP:] * (1.0 / (SUM_SCALE * LAST_SCALE * GAIN_SCALE))
     grad[...] = weight
     squares = jnp.sum((weight * weight).reshape(-1, 8, 128), axis=0)
     for t in range(ZL * CORE):
@@ -118,19 +123,58 @@
     wide = jnp.broadcast_to(clip[None], (ROWS // 8, 8, 128)).reshape(ROWS, 128)
     for z in range(ZH):
         span = slice(z * ROWS, (z + 1) * ROWS)
-        new = adam_update(wide * grad[span], *[states[z, i, :ROWS] for i in range(3)], 0.1)
+        new = adam_update(wide * grad[span], *[states[z, i * ROWS : (i + 1) * ROWS] for i in range(3)], 0.1)
         param[span] = new[0].astype(BF16)
         for i in range(3):
             outs[i][span] = new[i]
     state = []
     for i in range(3):
-        part = [states[z, i, ROWS : ROWS + 1, :ROWS] for z in range(ZH)]
+        row = 3 * ROWS + i
+        part = [states[z, row : row + 1, :ROWS] for z in range(ZH)]
         pairs = [jnp.concatenate(part[j : j + 2], axis=1) for j in (0, 2)]
         state.append(jnp.concatenate(pairs, axis=0))
     new = adam_update(clip[:2] * gain[:2], *state, 0.0)
     param[GROUP:] = jnp.concatenate([new[0], jnp.zeros((14, 128), F32)], axis=0).astype(BF16)
     for i in range(3):
         outs[3 + i][...] = new[i]
+
+
+def tokens_kernel(me, tokens, out):
+    total = jnp.zeros((ROWS, GROUP), F32)
+    for i in range(0, tokens.shape[1], GROUP):
+        part = tokens[:, i : i + GROUP].astype(F32)
+        total += part * part
+    mean = jnp.sum(total, axis=1, keepdims=True) * (1.0 / tokens.shape[1])
+    inverse = lax.rsqrt(mean + rms_eps)
+    high = inverse.astype(BF16).astype(F32)
+    middle = (inverse - high).astype(BF16).astype(F32)
+    low = inverse - high - middle
+    lane = lax.broadcasted_iota(jnp.int32, (ROWS, 128), 1)
+    parts = jnp.where(lane == 0, high, jnp.where(lane == 1, middle, jnp.where(lane == 2, low, 0.0)))
+    for x in range(X):
+        slot = lax.rem(x + X - me[0], X)
+        for y in range(Y):
+            pieces = []
+            for z in range(ZH):
+                start = ((z * Y + y) * X + x) * ROWS
+                pieces.append(tokens[:, start : start + ROWS])
+            out[slot, :, y * GROUP : (y + 1) * GROUP] = jnp.concatenate(pieces, axis=1)
+        out[slot, :, WIDTH:] = parts.astype(BF16)
+
+
+def keys_kernel(me, *refs):
+    tokens, param, out = refs[:X], refs[X], refs[X + 1]
+    for k in range(X):
+        parts = tokens[k][:, WIDTH:].astype(F32)
+        inverse = parts[:, 0:1] + parts[:, 1:2] + parts[:, 2:3]
+        total = jnp.zeros((ROWS, 128), F32)
+        for y in range(Y):
+            gain = param[y, GROUP : GROUP + 16].astype(F32)
+            gain = jnp.concatenate([gain[0:1], gain[1:2]], axis=1)
+            hidden = tokens[k][:, y * GROUP : (y + 1) * GROUP].astype(F32)
+            mixed = (hidden * inverse * gain).astype(BF16)
+            total += jnp.dot(mixed, param[y, :GROUP], preferred_element_type=F32)
+        out[lax.rem(me[0] + X - k, X)] = total
 
 
 def exchange(array, axes):
@@ -151,18 +195,27 @@
     next_input,
 ):
     zh = lax.axis_index("zh")
-    state = jnp.stack([weight_master, weight_moment, weight_second])
+    state = jnp.concatenate([weight_master, weight_moment, weight_second], axis=0)
     gain_state = jnp.stack([gain_master, gain_moment, gain_second])
-    gain_state = jnp.pad(gain_state[:, None, :], ((0, 0), (0, 7), (0, 128 - ROWS)))
-    state = jnp.concatenate([state, gain_state], axis=1)
-    states = lax.all_gather(state, "zh", axis=0, tiled=False)
+    gain_state = jnp.pad(gain_state, ((0, STATE - 3 * ROWS - 3), (0, 128 - ROWS)))
+    state = jnp.concatenate([state, gain_state], axis=0)
 
     grads = gradients(normed, key_cot, key_weight, norm_gain)
     grads = exchange(grads.astype(F16), "x")
-    grads, states = lax.optimization_barrier((grads, states))
+    me = lax.axis_index("x").astype(jnp.int32).reshape(1)
+    specs = [pl.BlockSpec(memory_space=pltpu.SMEM), pl.BlockSpec(memory_space=pltpu.VMEM)]
+    (tokens,) = whole(
+        tokens_kernel, ((X, ROWS, WIDTH + 128), BF16), name="tokens", in_specs=specs
+    )(me, next_input)
+    grads, tokens, state = lax.optimization_barrier((grads, tokens, state))
+    states = lax.all_gather(state, "zh", axis=0, tiled=False)
+    tokens = [tokens[0]] + [
+        lax.ppermute(tokens[k], "x", [(i, (i + k) % X) for i in range(X)]) for k in range(1, X)
+    ]
     grads = (jnp.sum(grads.astype(F32), axis=0) * SUM_SCALE).astype(F16)
-    grads = jnp.sum(exchange(grads, "y").astype(F32), axis=0)
-    grads = lax.all_gather(grads, "zh", axis=0, tiled=False)
+    grads, *tokens = lax.optimization_barrier((exchange(grads, "y"), *tokens))
+    grads = jnp.sum(grads.astype(F32), axis=0) * LAST_SCALE
+    grads = lax.all_gather(grads.astype(F16), "zh", axis=0, tiled=False).astype(F32)
     heads = ZL * CORE
     key_grad, shared = whole(
         sum_zh_kernel, ((GROUP, 128), F32), ((heads, 16, 128), F32), name="sum_zh"
@@ -181,17 +234,11 @@
     )(norm, key_grad, gain_grad, states)
 
     param = lax.all_gather(param, "y", axis=0, tiled=False)
-    params = exchange(jnp.broadcast_to(param[None], (X,) + param.shape), "x")
-    weight_piece = params[:, :, :GROUP].reshape(X, Y, ZH, ROWS, 128)
-    weight_piece = jnp.transpose(weight_piece, (2, 1, 0, 3, 4)).reshape(-1, 128)
-    gain_piece = params[:, :, GROUP : GROUP + 2].reshape(X, Y, ZH, ROWS)
-    gain_piece = jnp.transpose(gain_piece, (2, 1, 0, 3)).reshape(-1)
-
-    hidden = next_input.astype(F32)
-    inverse = lax.rsqrt(jnp.mean(hidden * hidden, axis=1, keepdims=True) + rms_eps)
-    rescaled = hidden * inverse
-    mixed = (rescaled * gain_piece.astype(F32)[None, :]).astype(BF16)
-    next_keys = jnp.dot(mixed, weight_piece, preferred_element_type=F32)
+    specs = [pl.BlockSpec(memory_space=pltpu.SMEM)] + [pl.BlockSpec(memory_space=pltpu.VMEM)] * (X + 1)
+    (keys,) = whole(keys_kernel, ((X, ROWS, 128), F32), name="keys", in_specs=specs)(
+        me, *tokens, param
+    )
+    next_keys = jnp.sum(exchange(keys, "x"), axis=0)
 
     def own(array):
         return lax.dynamic_slice_in_dim(array, zh * ROWS, ROWS, 0)

time: 181 us -> 198 us (1.094)
  the two profiles are of different devices: /device:TPU:64 before, /device:TPU:2 now
where the time goes in v3:
time: 198 us; the launch traced here: 197 us
  blocking collectives  71.9 us (36%)
  starting transfers between devices  48.9 us (25%)
  waiting for transfers between devices  35 us (18%)
  between operations  14.2 us (7%)
  Pallas kernels  12.8 us (6%)
  other arithmetic  8.35 us (4%)
  local copies, waits for them, and re-layouts  5.98 us (3%)
    all_to_all x4, starting transfers between devices, exchange(): return lax.all_to_all(array, axes, 0, 0, tiled=True)  39.1 us
    all_gather x1, blocking collectives, local(): lax.all_gather(grads.astype(F16), 'zh', axis=0, tiled=False).astype(F32)  39.1 us
    all_to_all x4, waiting for transfers between devices, exchange(): return lax.all_to_all(array, axes, 0, 0, tiled=True)  25.6 us
    all_gather x1, blocking collectives, local(): param = lax.all_gather(param, 'y', axis=0, tiled=False)  25.5 us
    pallas_call x1, Pallas kernels, gradients(): pl.pallas_call(gradient_kernel, grid=(Y,), in_specs=[*[pl.BlockSpec((toke...  10.1 us
    ppermute x3, starting transfers between devices, local(): lax.ppermute(tokens[k], 'x', [(i, (i + k) % X) for i in range(X)])  9.81 us
    ppermute x3, waiting for transfers between devices, local(): lax.ppermute(tokens[k], 'x', [(i, (i + k) % X) for i in range(X)])  8.71 us
    all_to_all x1, blocking collectives, exchange(): return lax.all_to_all(array, axes, 0, 0, tiled=True)  7.42 us
  transfers between devices with their start and end apart: 8, of which 6 were waited for; matrix products, arithmetic and copies ran while one was open for 2% of the time, Pallas kernels for 1%

profile of v3, /device:TPU:2, one launch (start us, length us, event | category | flops | bytes accessed | tf_op | source)
XLA Modules:
  0.0 197.2 jit_solution(3781442331613266004)
XLA Ops:
  7.2 1.4 reshape.43.refs_4_.refs_5_.refs_6_.refs_7_
  8.5 10.1 %gradients.1 = f32[4,8,264,128]{3,2,1,0:T(8,128)} custom-call(bf16[512,8192]{1,0:T(8,128)(2,1)} %refs_3_.1, bf16[512,8192]{1,0:T(8,128)(2,1)} %refs_3_.1, bf16[512,8192]{1,0:T(8,128)(2,1)} %refs_3_.1, bf16[512,8192]{1,0:T(8,128)(2,1)} %refs_3_.1, bf16[1,8192]{1,0:T(2,128)(2,1)} %reshape.43.refs_4_.refs_5_.refs_6_.refs_7_, ...), custom_call_target="tpu_custom_call" | custom-call | flops 2147483648 | bytes 14680064 | tf_op jit(solution)/shard_map/gradients/pallas_call | solution.py:68
  18.6 3.9 %convert_element_type.33 = f16[4,8,264,128]{3,2,1,0:T(8,128)(2,1)} convert(f32[4,8,264,128]{3,2,1,0:T(8,128)} %gradients.1) | non-fusion elementwise | flops 1081344 | bytes 6488064 | tf_op jit(solution)/shard_map/convert_element_type | solution.py:204
  22.5 14.1 %all-to-all-start = ((f16[4,8,264,128]{3,2,1,0:T(8,128)(2,1)}), f16[4,8,264,128]{3,2,1,0:T(8,128)(2,1)}, u32[]{:S(2)}, u32[]{:S(2)}) async-start(f16[4,8,264,128]{3,2,1,0:T(8,128)(2,1)} %convert_element_type.33), calls=%async_computation | async-start | bytes 4325376 | tf_op jit(solution)/shard_map/all_to_all | solution.py:181
  36.6 0.0 copy-done
  36.6 0.0 copy-start.2
  36.6 0.0 copy-start.3
  36.6 0.0 copy-start.4
  36.6 0.5 tokens.2
  37.1 0.1 copy-done.5
  37.2 0.0 copy-done.6
  37.3 0.0 copy-done.7
  37.3 0.1 copy-done.2
  37.4 0.0 copy-done.3
  37.4 0.0 copy-done.4
  37.4 0.7 pad_maximum_fusion
  38.1 15.2 %all-to-all-done = f16[4,8,264,128]{3,2,1,0:T(8,128)(2,1)} async-done(((f16[4,8,264,128]{3,2,1,0:T(8,128)(2,1)}), f16[4,8,264,128]{3,2,1,0:T(8,128)(2,1)}, u32[]{:S(2)}, u32[]{:S(2)}) %all-to-all-start) | async-done | bytes 2162720 | tf_op jit(solution)/shard_map/all_to_all | solution.py:181
  53.4 2.0 %convert_reduce_fusion = f32[8,264,128]{2,1,0:T(8,128)S(1)} fusion(f16[4,8,264,128]{3,2,1,0:T(8,128)(2,1)} %all-to-all-done), kind=kLoop, calls=%fused_computation | loop fusion | flops 1892352 | bytes 3244032 | tf_op jit(solution)/shard_map/reduce_sum | solution.py:215
  55.4 0.9 multiply_convert_fusion
  56.3 7.3 %all-to-all-start.1 = ((f16[8,264,128]{2,1,0:T(8,128)(2,1)}), f16[8,264,128]{2,1,0:T(8,128)(2,1)S(1)}, u32[]{:S(2)}, u32[]{:S(2)}) async-start(f16[8,264,128]{2,1,0:T(8,128)(2,1)} %multiply_convert_fusion), calls=%async_computation.1 | async-start | bytes 1081344 | tf_op jit(solution)/shard_map/all_to_all | solution.py:181
  63.6 0.0 all-gather.5.cloned.1.call-start
  63.7 0.7 all-gather.5.cloned.1.call-update
  64.4 0.1 slice_bitcast_fusion
  64.4 1.9 collective-permute-start
  66.4 5.4 %collective-permute-start.1 = (bf16[64,2176]{1,0:T(8,128)(2,1)S(1)}, bf16[64,2176]{1,0:T(8,128)(2,1)S(1)}, u32[]{:S(2)}, u32[]{:S(2)}) collective-permute-start(bf16[64,2176]{1,0:T(8,128)(2,1)S(1)} %get-tuple-element.46), channel_id=1, source_target_pairs={{0,12},{6,18},{12,0},{18,6},{1,13},{7,19},{13,1},{19,7},{2,14},{8,... | collective-permute-start | bytes 835592 | tf_op jit(solution)/shard_map/ppermute | solution.py:213
  71.8 2.5 %collective-permute-start.2 = (bf16[64,2176]{1,0:T(8,128)(2,1)S(1)}, bf16[64,2176]{1,0:T(8,128)(2,1)S(1)}, u32[]{:S(2)}, u32[]{:S(2)}) collective-permute-start(bf16[64,2176]{1,0:T(8,128)(2,1)S(1)} %get-tuple-element.45), channel_id=1, source_target_pairs={{0,18},{6,0},{12,6},{18,12},{1,19},{7,1},{13,7},{19,13},{2,20},{8,... | collective-permute-start | bytes 835592 | tf_op jit(solution)/shard_map/ppermute | solution.py:213
  74.3 1.5 collective-permute-done.refs_1_
  75.8 3.6 %collective-permute-done.1.refs_2_ = bf16[64,2176]{1,0:T(8,128)(2,1)S(1)} collective-permute-done((bf16[64,2176]{1,0:T(8,128)(2,1)S(1)}, bf16[64,2176]{1,0:T(8,128)(2,1)S(1)}, u32[]{:S(2)}, u32[]{:S(2)}) %collective-permute-start.1) | collective-permute-done | bytes 278560 | tf_op jit(solution)/shard_map/ppermute | solution.py:213
  79.4 3.6 %collective-permute-done.2.refs_3_ = bf16[64,2176]{1,0:T(8,128)(2,1)S(1)} collective-permute-done((bf16[64,2176]{1,0:T(8,128)(2,1)S(1)}, bf16[64,2176]{1,0:T(8,128)(2,1)S(1)}, u32[]{:S(2)}, u32[]{:S(2)}) %collective-permute-start.2) | collective-permute-done | bytes 278560 | tf_op jit(solution)/shard_map/ppermute | solution.py:213
  83.0 0.0 all-to-all-done.1
  83.0 0.1 convert_reduce_fusion.1
  83.1 39.1 %all-gather = f16[1056,128]{1,0:T(8,128)(2,1)S(1)} all-gather(f16[264,128]{1,0:T(8,128)(2,1)S(1)} %multiply_convert_fusion.1), channel_id=2, replica_groups=mesh['zh'=4,'y'=8,'x'=4,'zl'=3,'core'=2] {'zh'}, dimensions={0}, use_global_device_ids=true | all-gather | bytes 337920 | tf_op jit(solution)/shard_map/all_gather | solution.py:218
  122.2 7.4 %all_to_all.25.parts = f32[6,16,128]{2,1,0:T(8,128)S(1)} all-to-all(f32[6,16,128]{2,1,0:T(8,128)S(1)} %get-tuple-element.33), channel_id=1, replica_groups=mesh['zh'=4,'y'=8,'x'=4,'zl'=3,'core'=2] {'zl','core'}, dimensions={0} | all-to-all | bytes 98304 | tf_op jit(solution)/shard_map/all_to_all | solution.py:181
  129.7 0.8 sum_heads.1
  130.4 12.6 %all-to-all-start.3 = ((f32[32,8,128]{2,1,0:T(8,128)}), f32[32,8,128]{2,1,0:T(8,128)S(1)}, u32[]{:S(2)}, u32[]{:S(2)}) async-start(f32[32,8,128]{2,1,0:T(8,128)} %get-tuple-element.34), calls=%async_computation.3 | async-start | bytes 262144 | tf_op jit(solution)/shard_map/all_to_all | solution.py:181
  143.1 8.9 %all-to-all-done.3.norm = f32[32,8,128]{2,1,0:T(8,128)S(1)} async-done(((f32[32,8,128]{2,1,0:T(8,128)}), f32[32,8,128]{2,1,0:T(8,128)S(1)}, u32[]{:S(2)}, u32[]{:S(2)}) %all-to-all-start.3) | async-done | bytes 131104 | tf_op jit(solution)/shard_map/all_to_all | solution.py:181
  151.9 1.2 copy-done.1
  153.1 0.2 update.1
  153.3 25.5 %all-gather.2 = bf16[2176,128]{1,0:T(8,128)(2,1)S(1)} all-gather(bf16[272,128]{1,0:T(8,128)(2,1)S(1)} %get-tuple-element.38), channel_id=4, replica_groups=mesh['zh'=4,'y'=8,'x'=4,'zl'=3,'core'=2] {'y'}, dimensions={0}, use_global_device_ids=true | all-gather | bytes 626688 | tf_op jit(solution)/shard_map/all_gather | solution.py:236
  178.8 1.3 keys.1
  180.1 5.1 %all-to-all-start.4 = ((f32[4,64,128]{2,1,0:T(8,128)}), f32[4,64,128]{2,1,0:T(8,128)S(1)}, u32[]{:S(2)}, u32[]{:S(2)}) async-start(f32[4,64,128]{2,1,0:T(8,128)} %keys.1), calls=%async_computation.4 | async-start | bytes 262144 | tf_op jit(solution)/shard_map/all_to_all | solution.py:181
  185.2 0.6 dynamic_slice.21
  185.8 0.6 dynamic_slice.22
  186.4 0.6 dynamic_slice.23
  186.9 0.6 constant_dynamic-slice_fusion
  187.6 0.6 constant_dynamic-slice_fusion.2
  188.2 1.5 all-to-all-done.4
  189.7 0.6 reduce_sum.29
  (10 shorter events, 0.1 us)
Async XLA Ops:
  22.5 14.1 %copy-start = (bf16[64,8192]{1,0:T(8,128)(2,1)S(1)}, bf16[64,8192]{1,0:T(8,128)(2,1)}, u32[]{:S(2)}) copy-start(bf16[64,8192]{1,0:T(8,128)(2,1)} %tokens.3) | copy-start | bytes 3145732
  22.5 30.9 %all-to-all-start = ((f16[4,8,264,128]{3,2,1,0:T(8,128)(2,1)}), f16[4,8,264,128]{3,2,1,0:T(8,128)(2,1)}, u32[]{:S(2)}, u32[]{:S(2)}) async-start(f16[4,8,264,128]{3,2,1,0:T(8,128)(2,1)} %convert_element_type.33), calls=%async_computation | async-start | bytes 4325376 | tf_op jit(solution)/shard_map/all_to_all | solution.py:181
  36.6 0.7 copy-start.5
  36.6 0.7 copy-start.6
  36.6 0.7 copy-start.7
  36.6 0.8 copy-start.2
  36.6 0.8 copy-start.3
  36.6 0.8 copy-start.4
  56.3 26.6 %all-to-all-start.1 = ((f16[8,264,128]{2,1,0:T(8,128)(2,1)}), f16[8,264,128]{2,1,0:T(8,128)(2,1)S(1)}, u32[]{:S(2)}, u32[]{:S(2)}) async-start(f16[8,264,128]{2,1,0:T(8,128)(2,1)} %multiply_convert_fusion), calls=%async_computation.1 | async-start | bytes 1081344 | tf_op jit(solution)/shard_map/all_to_all | solution.py:181
  63.6 88.3 %all-gather.5.cloned.1.call-start = ((), (), s32[]{:S(2)}) async-start(), calls=%async_computation.5 | async-start | bytes 1310720 | tf_op jit(solution)/shard_map/all_gather | solution.py:211
  64.4 11.4 %collective-permute-start = (bf16[64,2176]{1,0:T(8,128)(2,1)S(1)}, bf16[64,2176]{1,0:T(8,128)(2,1)S(1)}, u32[]{:S(2)}, u32[]{:S(2)}) collective-permute-start(bf16[64,2176]{1,0:T(8,128)(2,1)S(1)} %get-tuple-element.47), channel_id=1, source_target_pairs={{0,6},{6,12},{12,18},{18,0},{1,7},{7,13},{13,19},{19,1},{2,8},{8,1... | collective-permute-start | bytes 835592 | tf_op jit(solution)/shard_map/ppermute | solution.py:213
  66.4 13.0 %collective-permute-start.1 = (bf16[64,2176]{1,0:T(8,128)(2,1)S(1)}, bf16[64,2176]{1,0:T(8,128)(2,1)S(1)}, u32[]{:S(2)}, u32[]{:S(2)}) collective-permute-start(bf16[64,2176]{1,0:T(8,128)(2,1)S(1)} %get-tuple-element.46), channel_id=1, source_target_pairs={{0,12},{6,18},{12,0},{18,6},{1,13},{7,19},{13,1},{19,7},{2,14},{8,... | collective-permute-start | bytes 835592 | tf_op jit(solution)/shard_map/ppermute | solution.py:213
  71.8 11.2 %collective-permute-start.2 = (bf16[64,2176]{1,0:T(8,128)(2,1)S(1)}, bf16[64,2176]{1,0:T(8,128)(2,1)S(1)}, u32[]{:S(2)}, u32[]{:S(2)}) collective-permute-start(bf16[64,2176]{1,0:T(8,128)(2,1)S(1)} %get-tuple-element.45), channel_id=1, source_target_pairs={{0,18},{6,0},{12,6},{18,12},{1,19},{7,1},{13,7},{19,13},{2,20},{8,... | collective-permute-start | bytes 835592 | tf_op jit(solution)/shard_map/ppermute | solution.py:213
  130.4 21.5 %all-to-all-start.3 = ((f32[32,8,128]{2,1,0:T(8,128)}), f32[32,8,128]{2,1,0:T(8,128)S(1)}, u32[]{:S(2)}, u32[]{:S(2)}) async-start(f32[32,8,128]{2,1,0:T(8,128)} %get-tuple-element.34), calls=%async_computation.3 | async-start | bytes 262144 | tf_op jit(solution)/shard_map/all_to_all | solution.py:181
  151.9 1.2 copy-start.1
  180.1 9.6 %all-to-all-start.4 = ((f32[4,64,128]{2,1,0:T(8,128)}), f32[4,64,128]{2,1,0:T(8,128)S(1)}, u32[]{:S(2)}, u32[]{:S(2)}) async-start(f32[4,64,128]{2,1,0:T(8,128)} %keys.1), calls=%async_computation.4 | async-start | bytes 262144 | tf_op jit(solution)/shard_map/all_to_all | solution.py:181
Sparse Core Ops, SparseCore 0:
  66.8 64.9 all-gather.4

commit v4 on v3

--- a/solution.py
+++ b/solution.py
@@ -23,7 +23,6 @@
 GAIN_SCALE = 2.0**-6
 SUM_SCALE = 2.0**-2
 LAST_SCALE = 2.0**-3
-STATE = 512
 WIDTH = Y * GROUP
 F32 = jnp.float32
 BF16 = jnp.bfloat16
@@ -197,8 +196,9 @@
     zh = lax.axis_index("zh")
     state = jnp.concatenate([weight_master, weight_moment, weight_second], axis=0)
     gain_state = jnp.stack([gain_master, gain_moment, gain_second])
-    gain_state = jnp.pad(gain_state, ((0, STATE - 3 * ROWS - 3), (0, 128 - ROWS)))
+    gain_state = jnp.pad(gain_state, ((0, 5), (0, 128 - ROWS)))
     state = jnp.concatenate([state, gain_state], axis=0)
+    states = lax.all_gather(state, "zh", axis=0, tiled=False)
 
     grads = gradients(normed, key_cot, key_weight, norm_gain)
     grads = exchange(grads.astype(F16), "x")
@@ -207,23 +207,23 @@
     (tokens,) = whole(
         tokens_kernel, ((X, ROWS, WIDTH + 128), BF16), name="tokens", in_specs=specs
     )(me, next_input)
-    grads, tokens, state = lax.optimization_barrier((grads, tokens, state))
-    states = lax.all_gather(state, "zh", axis=0, tiled=False)
+    grads, tokens, states = lax.optimization_barrier((grads, tokens, states))
     tokens = [tokens[0]] + [
         lax.ppermute(tokens[k], "x", [(i, (i + k) % X) for i in range(X)]) for k in range(1, X)
     ]
     grads = (jnp.sum(grads.astype(F32), axis=0) * SUM_SCALE).astype(F16)
-    grads, *tokens = lax.optimization_barrier((exchange(grads, "y"), *tokens))
-    grads = jnp.sum(grads.astype(F32), axis=0) * LAST_SCALE
-    grads = lax.all_gather(grads.astype(F16), "zh", axis=0, tiled=False).astype(F32)
+    grads = jnp.sum(exchange(grads, "y").astype(F32), axis=0) * LAST_SCALE
+    grads = jnp.broadcast_to(grads.astype(F16)[None], (ZH,) + grads.shape)
+    grads = exchange(grads, "zh").astype(F32)
     heads = ZL * CORE
     key_grad, shared = whole(
         sum_zh_kernel, ((GROUP, 128), F32), ((heads, 16, 128), F32), name="sum_zh"
     )(grads)
 
+    shared, *tokens = lax.optimization_barrier((exchange(shared, TENSOR), *tokens))
     gain_grad, norm = whole(
         sum_heads_kernel, ((8, 128), F32), ((Y * X, 8, 128), F32), name="sum_heads"
-    )(exchange(shared, TENSOR))
+    )(shared)
     norm = exchange(norm, ("y", "x"))
     param, *news = whole(
         update_kernel,

time: 198 us -> 165 us (0.83)
  waiting for transfers between devices: 35 us -> 19.4 us
  between operations: 14.2 us -> 0.78 us
  blocking collectives: 71.9 us -> 66.6 us
  starting transfers between devices: 48.9 us -> 51.2 us
    all_gather x1, blocking collectives: 39.1 us -> 18 us  [local(): states = lax.all_gather(state, 'zh', axis=0, tiled=False)]
    all_to_all x1, blocking collectives: 7.42 us -> 23.1 us  [exchange(): return lax.all_to_all(array, axes, 0, 0, tiled=True)]
    ppermute x3, waiting for transfers between devices: 8.71 us -> 0.01 us  [local(): lax.ppermute(tokens[k], 'x', [(i, (i + k) % X) for i in range(X)])]
    all_to_all x4 -> x5, waiting for transfers between devices: 25.6 us -> 19.3 us  [exchange(): return lax.all_to_all(array, axes, 0, 0, tiled=True)]
    all_to_all x4 -> x5, starting transfers between devices: 39.1 us -> 41.4 us  [exchange(): return lax.all_to_all(array, axes, 0, 0, tiled=True)]
  transfers between devices with their start and end apart: 8 -> 8, of which waited for: 6 -> 4; matrix products, arithmetic and copies ran while one was open for 2% -> 2% of each run, Pallas kernels for 1% -> 1%
where the time goes in v4:
time: 165 us; the launch traced here: 164 us
  blocking collectives  66.6 us (40%)
  starting transfers between devices  51.2 us (31%)
  waiting for transfers between devices  19.4 us (12%)
  Pallas kernels  13.4 us (8%)
  other arithmetic  6.8 us (4%)
  local copies, waits for them, and re-layouts  5.47 us (3%)
    all_to_all x5, starting transfers between devices, exchange(): return lax.all_to_all(array, axes, 0, 0, tiled=True)  41.4 us
    all_gather x1, blocking collectives, local(): param = lax.all_gather(param, 'y', axis=0, tiled=False)  25.6 us
    all_to_all x1, blocking collectives, exchange(): return lax.all_to_all(array, axes, 0, 0, tiled=True)  23.1 us
    all_to_all x5, waiting for transfers between devices, exchange(): return lax.all_to_all(array, axes, 0, 0, tiled=True)  19.3 us
    all_gather x1, blocking collectives, local(): states = lax.all_gather(state, 'zh', axis=0, tiled=False)  18 us
    pallas_call x1, Pallas kernels, gradients(): pl.pallas_call(gradient_kernel, grid=(Y,), in_specs=[*[pl.BlockSpec((toke...  10.1 us
    ppermute x3, starting transfers between devices, local(): lax.ppermute(tokens[k], 'x', [(i, (i + k) % X) for i in range(X)])  9.81 us
    convert_element_type x1, other arithmetic, local(): grads = exchange(grads.astype(F16), 'x')  3.88 us
  transfers between devices with their start and end apart: 8, of which 4 were waited for; matrix products, arithmetic and copies ran while one was open for 2% of the time, Pallas kernels for 1%

profile of v4, /device:TPU:2, one launch (start us, length us, event | category | flops | bytes accessed | tf_op | source)
XLA Modules:
  0.0 163.7 jit_solution(3927614089440636861)
XLA Ops:
  0.6 1.4 reshape.34.refs_4_.refs_5_.refs_6_.refs_7_
  2.0 10.1 %gradients.1 = f32[4,8,264,128]{3,2,1,0:T(8,128)} custom-call(bf16[512,8192]{1,0:T(8,128)(2,1)} %refs_3_.1, bf16[512,8192]{1,0:T(8,128)(2,1)} %refs_3_.1, bf16[512,8192]{1,0:T(8,128)(2,1)} %refs_3_.1, bf16[512,8192]{1,0:T(8,128)(2,1)} %refs_3_.1, bf16[1,8192]{1,0:T(2,128)(2,1)} %reshape.34.refs_4_.refs_5_.refs_6_.refs_7_, ...), custom_call_target="tpu_custom_call" | custom-call | flops 2147483648 | bytes 14680064 | tf_op jit(solution)/shard_map/gradients/pallas_call | solution.py:67
  12.1 3.9 %convert_element_type.27 = f16[4,8,264,128]{3,2,1,0:T(8,128)(2,1)} convert(f32[4,8,264,128]{3,2,1,0:T(8,128)} %gradients.1) | non-fusion elementwise | flops 1081344 | bytes 6488064 | tf_op jit(solution)/shard_map/convert_element_type | solution.py:204
  15.9 0.0 copy-start
  15.9 14.1 %all-to-all-start = ((f16[4,8,264,128]{3,2,1,0:T(8,128)(2,1)}), f16[4,8,264,128]{3,2,1,0:T(8,128)(2,1)}, u32[]{:S(2)}, u32[]{:S(2)}) async-start(f16[4,8,264,128]{3,2,1,0:T(8,128)(2,1)} %convert_element_type.27), calls=%async_computation | async-start | bytes 4325376 | tf_op jit(solution)/shard_map/all_to_all | solution.py:180
  30.0 0.0 copy-start.2
  30.0 0.0 copy-start.3
  30.1 0.0 copy-done
  30.1 0.5 tokens.2
  30.5 0.1 copy-done.4
  30.7 0.0 copy-done.5
  30.7 0.0 copy-done.6
  30.7 0.1 copy-done.1
  30.8 0.0 copy-done.2
  30.8 0.0 copy-done.3
  30.9 18.0 %all-gather = f32[800,128]{1,0:T(8,128)S(1)} all-gather(f32[200,128]{1,0:T(8,128)S(1)} %pad_maximum_fusion), channel_id=2, replica_groups=mesh['zh'=4,'y'=8,'x'=4,'zl'=3,'core'=2] {'zh'}, dimensions={0}, use_global_device_ids=true | all-gather | bytes 512000 | tf_op jit(solution)/shard_map/all_gather | solution.py:201
  48.9 0.0 all-to-all-done
  48.9 2.0 %convert_reduce_fusion = f32[8,264,128]{2,1,0:T(8,128)S(1)} fusion(f16[4,8,264,128]{3,2,1,0:T(8,128)(2,1)} %all-to-all-done), kind=kLoop, calls=%fused_computation | loop fusion | flops 1892352 | bytes 3244032 | tf_op jit(solution)/shard_map/reduce_sum | solution.py:214
  50.9 0.1 multiply_convert_fusion
  51.1 23.1 %all_to_all.30 = f16[8,264,128]{2,1,0:T(8,128)(2,1)S(1)} all-to-all(f16[8,264,128]{2,1,0:T(8,128)(2,1)S(1)} %multiply_convert_fusion), channel_id=1, replica_groups=mesh['zh'=4,'y'=8,'x'=4,'zl'=3,'core'=2] {'y'}, dimensions={0} | all-to-all | bytes 1081344 | tf_op jit(solution)/shard_map/all_to_all | solution.py:180
  74.1 0.1 convert_reduce_fusion.1
  74.2 0.7 broadcast_in_dim.2
  75.0 13.4 %all-to-all-start.2 = ((f16[4,264,128]{2,1,0:T(8,128)(2,1)}), f16[4,264,128]{2,1,0:T(8,128)(2,1)S(1)}, u32[]{:S(2)}, u32[]{:S(2)}) async-start(f16[4,264,128]{2,1,0:T(8,128)(2,1)} %broadcast_in_dim.2), calls=%async_computation.2 | async-start | bytes 540672 | tf_op jit(solution)/shard_map/all_to_all | solution.py:180
  88.3 0.1 slice_bitcast_fusion
  88.4 2.0 %collective-permute-start = (bf16[64,2176]{1,0:T(8,128)(2,1)S(1)}, bf16[64,2176]{1,0:T(8,128)(2,1)S(1)}, u32[]{:S(2)}, u32[]{:S(2)}) collective-permute-start(bf16[64,2176]{1,0:T(8,128)(2,1)S(1)} %get-tuple-element.47), channel_id=1, source_target_pairs={{0,6},{6,12},{12,18},{18,0},{1,7},{7,13},{13,19},{19,1},{2,8},{8,1... | collective-permute-start | bytes 835592 | tf_op jit(solution)/shard_map/ppermute | solution.py:212
  90.4 5.4 %collective-permute-start.1 = (bf16[64,2176]{1,0:T(8,128)(2,1)S(1)}, bf16[64,2176]{1,0:T(8,128)(2,1)S(1)}, u32[]{:S(2)}, u32[]{:S(2)}) collective-permute-start(bf16[64,2176]{1,0:T(8,128)(2,1)S(1)} %get-tuple-element.46), channel_id=1, source_target_pairs={{0,12},{6,18},{12,0},{18,6},{1,13},{7,19},{13,1},{19,7},{2,14},{8,... | collective-permute-start | bytes 835592 | tf_op jit(solution)/shard_map/ppermute | solution.py:212
  95.8 2.5 %collective-permute-start.2 = (bf16[64,2176]{1,0:T(8,128)(2,1)S(1)}, bf16[64,2176]{1,0:T(8,128)(2,1)S(1)}, u32[]{:S(2)}, u32[]{:S(2)}) collective-permute-start(bf16[64,2176]{1,0:T(8,128)(2,1)S(1)} %get-tuple-element.45), channel_id=1, source_target_pairs={{0,18},{6,0},{12,6},{18,12},{1,19},{7,1},{13,7},{19,13},{2,20},{8,... | collective-permute-start | bytes 835592 | tf_op jit(solution)/shard_map/ppermute | solution.py:212
  98.3 4.0 %all-to-all-done.2 = f16[4,264,128]{2,1,0:T(8,128)(2,1)S(1)} async-done(((f16[4,264,128]{2,1,0:T(8,128)(2,1)}), f16[4,264,128]{2,1,0:T(8,128)(2,1)S(1)}, u32[]{:S(2)}, u32[]{:S(2)}) %all-to-all-start.2) | async-done | bytes 270368 | tf_op jit(solution)/shard_map/all_to_all | solution.py:180
  102.3 0.7 sum_zh.1
  102.9 3.7 %all-to-all-start.3 = ((f32[6,16,128]{2,1,0:T(8,128)}), f32[6,16,128]{2,1,0:T(8,128)S(1)}, u32[]{:S(2)}, u32[]{:S(2)}) async-start(f32[6,16,128]{2,1,0:T(8,128)} %get-tuple-element.27), calls=%async_computation.3 | async-start | bytes 98304 | tf_op jit(solution)/shard_map/all_to_all | solution.py:180
  106.6 0.0 collective-permute-done.refs_1_
  106.6 0.0 collective-permute-done.1.refs_2_
  106.6 0.0 collective-permute-done.2.refs_3_
  106.6 5.0 %all-to-all-done.3.parts = f32[6,16,128]{2,1,0:T(8,128)S(1)} async-done(((f32[6,16,128]{2,1,0:T(8,128)}), f32[6,16,128]{2,1,0:T(8,128)S(1)}, u32[]{:S(2)}, u32[]{:S(2)}) %all-to-all-start.3) | async-done | bytes 49184 | tf_op jit(solution)/shard_map/all_to_all | solution.py:180
  111.6 0.8 sum_heads.1
  112.4 5.3 %all-to-all-start.4 = ((f32[32,8,128]{2,1,0:T(8,128)}), f32[32,8,128]{2,1,0:T(8,128)S(1)}, u32[]{:S(2)}, u32[]{:S(2)}) async-start(f32[32,8,128]{2,1,0:T(8,128)} %get-tuple-element.34), calls=%async_computation.4 | async-start | bytes 262144 | tf_op jit(solution)/shard_map/all_to_all | solution.py:180
  117.7 8.9 %all-to-all-done.4.norm = f32[32,8,128]{2,1,0:T(8,128)S(1)} async-done(((f32[32,8,128]{2,1,0:T(8,128)}), f32[32,8,128]{2,1,0:T(8,128)S(1)}, u32[]{:S(2)}, u32[]{:S(2)}) %all-to-all-start.4) | async-done | bytes 131104 | tf_op jit(solution)/shard_map/all_to_all | solution.py:180
  126.5 0.2 update.1
  126.7 25.6 %all-gather.1 = bf16[2176,128]{1,0:T(8,128)(2,1)S(1)} all-gather(bf16[272,128]{1,0:T(8,128)(2,1)S(1)} %get-tuple-element.38), channel_id=3, replica_groups=mesh['zh'=4,'y'=8,'x'=4,'zl'=3,'core'=2] {'y'}, dimensions={0}, use_global_device_ids=true | all-gather | bytes 626688 | tf_op jit(solution)/shard_map/all_gather | solution.py:236
  152.3 1.3 keys.1
  153.6 5.0 %all-to-all-start.5 = ((f32[4,64,128]{2,1,0:T(8,128)}), f32[4,64,128]{2,1,0:T(8,128)S(1)}, u32[]{:S(2)}, u32[]{:S(2)}) async-start(f32[4,64,128]{2,1,0:T(8,128)} %keys.1), calls=%async_computation.5 | async-start | bytes 262144 | tf_op jit(solution)/shard_map/all_to_all | solution.py:180
  158.6 0.6 dynamic_slice.21
  159.2 0.6 dynamic_slice.22
  159.8 0.6 dynamic_slice.23
  160.3 0.6 constant_dynamic-slice_fusion
  161.0 0.6 constant_dynamic-slice_fusion.2
  161.6 1.5 all-to-all-done.5
  163.1 0.6 reduce_sum.29
  (8 shorter events, 0.1 us)
Async XLA Ops:
  15.9 14.1 %copy-start = (bf16[64,8192]{1,0:T(8,128)(2,1)S(1)}, bf16[64,8192]{1,0:T(8,128)(2,1)}, u32[]{:S(2)}) copy-start(bf16[64,8192]{1,0:T(8,128)(2,1)} %tokens.3) | copy-start | bytes 3145732
  15.9 33.0 %all-to-all-start = ((f16[4,8,264,128]{3,2,1,0:T(8,128)(2,1)}), f16[4,8,264,128]{3,2,1,0:T(8,128)(2,1)}, u32[]{:S(2)}, u32[]{:S(2)}) async-start(f16[4,8,264,128]{3,2,1,0:T(8,128)(2,1)} %convert_element_type.27), calls=%async_computation | async-start | bytes 4325376 | tf_op jit(solution)/shard_map/all_to_all | solution.py:180
  30.0 0.7 copy-start.4
  30.0 0.7 copy-start.5
  30.0 0.7 copy-start.6
  30.0 0.8 copy-start.1
  30.0 0.8 copy-start.2
  30.0 0.8 copy-start.3
  75.0 27.3 %all-to-all-start.2 = ((f16[4,264,128]{2,1,0:T(8,128)(2,1)}), f16[4,264,128]{2,1,0:T(8,128)(2,1)S(1)}, u32[]{:S(2)}, u32[]{:S(2)}) async-start(f16[4,264,128]{2,1,0:T(8,128)(2,1)} %broadcast_in_dim.2), calls=%async_computation.2 | async-start | bytes 540672 | tf_op jit(solution)/shard_map/all_to_all | solution.py:180
  88.4 18.2 %collective-permute-start = (bf16[64,2176]{1,0:T(8,128)(2,1)S(1)}, bf16[64,2176]{1,0:T(8,128)(2,1)S(1)}, u32[]{:S(2)}, u32[]{:S(2)}) collective-permute-start(bf16[64,2176]{1,0:T(8,128)(2,1)S(1)} %get-tuple-element.47), channel_id=1, source_target_pairs={{0,6},{6,12},{12,18},{18,0},{1,7},{7,13},{13,19},{19,1},{2,8},{8,1... | collective-permute-start | bytes 835592 | tf_op jit(solution)/shard_map/ppermute | solution.py:212
  90.4 16.2 %collective-permute-start.1 = (bf16[64,2176]{1,0:T(8,128)(2,1)S(1)}, bf16[64,2176]{1,0:T(8,128)(2,1)S(1)}, u32[]{:S(2)}, u32[]{:S(2)}) collective-permute-start(bf16[64,2176]{1,0:T(8,128)(2,1)S(1)} %get-tuple-element.46), channel_id=1, source_target_pairs={{0,12},{6,18},{12,0},{18,6},{1,13},{7,19},{13,1},{19,7},{2,14},{8,... | collective-permute-start | bytes 835592 | tf_op jit(solution)/shard_map/ppermute | solution.py:212
  95.8 10.8 %collective-permute-start.2 = (bf16[64,2176]{1,0:T(8,128)(2,1)S(1)}, bf16[64,2176]{1,0:T(8,128)(2,1)S(1)}, u32[]{:S(2)}, u32[]{:S(2)}) collective-permute-start(bf16[64,2176]{1,0:T(8,128)(2,1)S(1)} %get-tuple-element.45), channel_id=1, source_target_pairs={{0,18},{6,0},{12,6},{18,12},{1,19},{7,1},{13,7},{19,13},{2,20},{8,... | collective-permute-start | bytes 835592 | tf_op jit(solution)/shard_map/ppermute | solution.py:212
  102.9 8.7 %all-to-all-start.3 = ((f32[6,16,128]{2,1,0:T(8,128)}), f32[6,16,128]{2,1,0:T(8,128)S(1)}, u32[]{:S(2)}, u32[]{:S(2)}) async-start(f32[6,16,128]{2,1,0:T(8,128)} %get-tuple-element.27), calls=%async_computation.3 | async-start | bytes 98304 | tf_op jit(solution)/shard_map/all_to_all | solution.py:180
  112.4 14.1 %all-to-all-start.4 = ((f32[32,8,128]{2,1,0:T(8,128)}), f32[32,8,128]{2,1,0:T(8,128)S(1)}, u32[]{:S(2)}, u32[]{:S(2)}) async-start(f32[32,8,128]{2,1,0:T(8,128)} %get-tuple-element.34), calls=%async_computation.4 | async-start | bytes 262144 | tf_op jit(solution)/shard_map/all_to_all | solution.py:180
  153.6 9.6 %all-to-all-start.5 = ((f32[4,64,128]{2,1,0:T(8,128)}), f32[4,64,128]{2,1,0:T(8,128)S(1)}, u32[]{:S(2)}, u32[]{:S(2)}) async-start(f32[4,64,128]{2,1,0:T(8,128)} %keys.1), calls=%async_computation.5 | async-start | bytes 262144 | tf_op jit(solution)/shard_map/all_to_all | solution.py:180

commit v5 on v4

--- a/solution.py
+++ b/solution.py
@@ -116,26 +116,37 @@
     norm[...] = jnp.broadcast_to(square, norm.shape)
 
 
-def update_kernel(norm, grad, gain, states, param, *outs):
+def update_kernel(me, norm, grad, gain, *refs):
+    states, param, own, gains = refs[:ZH], refs[ZH], refs[ZH + 1 : ZH + 4], refs[ZH + 4 :]
     total = jnp.sum(norm[...], axis=0)
     clip = jnp.minimum(1.0, 1.0 / (jnp.sqrt(total) + 1e-06))
-    wide = jnp.broadcast_to(clip[None], (ROWS // 8, 8, 128)).reshape(ROWS, 128)
-    for z in range(ZH):
-        span = slice(z * ROWS, (z + 1) * ROWS)
-        new = adam_update(wide * grad[span], *[states[z, i * ROWS : (i + 1) * ROWS] for i in range(3)], 0.1)
-        param[span] = new[0].astype(BF16)
-        for i in range(3):
-            outs[i][span] = new[i]
+    for k in range(ZH):
+        span = pl.ds(pl.multiple_of(lax.rem(me[0] + ZH - k, ZH) * ROWS, ROWS), ROWS)
+        parts = [states[k][i * ROWS : (i + 1) * ROWS] for i in range(3)]
+        new = adam_update(clip * grad[span], *parts, 0.1)
+        rounded = new[0].astype(BF16)
+        for y in range(Y):
+            param[y, span] = rounded
+        if k == 0:
+            for i in range(3):
+                own[i][...] = new[i]
     state = []
     for i in range(3):
-        row = 3 * ROWS + i
-        part = [states[z, row : row + 1, :ROWS] for z in range(ZH)]
+        rows = [states[k][3 * ROWS + i : 3 * ROWS + i + 1, :ROWS] for k in range(ZH)]
+        part = []
+        for z in range(ZH):
+            row = rows[0]
+            for k in range(1, ZH):
+                row = jnp.where(lax.rem(me[0] + ZH - k, ZH) == z, rows[k], row)
+            part.append(row)
         pairs = [jnp.concatenate(part[j : j + 2], axis=1) for j in (0, 2)]
         state.append(jnp.concatenate(pairs, axis=0))
-    new = adam_update(clip[:2] * gain[:2], *state, 0.0)
-    param[GROUP:] = jnp.concatenate([new[0], jnp.zeros((14, 128), F32)], axis=0).astype(BF16)
+    new = adam_update(clip * gain[:2], *state, 0.0)
+    tile = jnp.concatenate([new[0], jnp.zeros((14, 128), F32)], axis=0).astype(BF16)
+    for y in range(Y):
+        param[y, GROUP:] = tile
     for i in range(3):
-        outs[3 + i][...] = new[i]
+        gains[i][...] = new[i]
 
 
 def tokens_kernel(me, tokens, out):
@@ -180,6 +191,17 @@
     return lax.all_to_all(array, axes, 0, 0, tiled=True)
 
 
+def shifts(arrays, axis, size):
+    return [
+        lax.ppermute(
+            arrays[k] if isinstance(arrays, list) else arrays,
+            axis,
+            [(i, (i + k) % size) for i in range(size)],
+        )
+        for k in range(1, size)
+    ]
+
+
 def local(
     normed,
     key_cot,
@@ -198,21 +220,20 @@
     gain_state = jnp.stack([gain_master, gain_moment, gain_second])
     gain_state = jnp.pad(gain_state, ((0, 5), (0, 128 - ROWS)))
     state = jnp.concatenate([state, gain_state], axis=0)
-    states = lax.all_gather(state, "zh", axis=0, tiled=False)
 
     grads = gradients(normed, key_cot, key_weight, norm_gain)
     grads = exchange(grads.astype(F16), "x")
     me = lax.axis_index("x").astype(jnp.int32).reshape(1)
     specs = [pl.BlockSpec(memory_space=pltpu.SMEM), pl.BlockSpec(memory_space=pltpu.VMEM)]
+    grads, next_input, state = lax.optimization_barrier((grads, next_input, state))
+    states = [state, *shifts(state, "zh", ZH)]
     (tokens,) = whole(
         tokens_kernel, ((X, ROWS, WIDTH + 128), BF16), name="tokens", in_specs=specs
     )(me, next_input)
-    grads, tokens, states = lax.optimization_barrier((grads, tokens, states))
-    tokens = [tokens[0]] + [
-        lax.ppermute(tokens[k], "x", [(i, (i + k) % X) for i in range(X)]) for k in range(1, X)
-    ]
+    tokens = [tokens[0], *shifts([tokens[k] for k in range(X)], "x", X)]
     grads = (jnp.sum(grads.astype(F32), axis=0) * SUM_SCALE).astype(F16)
-    grads = jnp.sum(exchange(grads, "y").astype(F32), axis=0) * LAST_SCALE
+    grads, *states = lax.optimization_barrier((exchange(grads, "y"), *states))
+    grads = jnp.sum(grads.astype(F32), axis=0) * LAST_SCALE
     grads = jnp.broadcast_to(grads.astype(F16)[None], (ZH,) + grads.shape)
     grads = exchange(grads, "zh").astype(F32)
     heads = ZL * CORE
@@ -222,18 +243,20 @@
 
     shared, *tokens = lax.optimization_barrier((exchange(shared, TENSOR), *tokens))
     gain_grad, norm = whole(
-        sum_heads_kernel, ((8, 128), F32), ((Y * X, 8, 128), F32), name="sum_heads"
+        sum_heads_kernel, ((8, 128), F32), ((Y * X, 1, 128), F32), name="sum_heads"
     )(shared)
     norm = exchange(norm, ("y", "x"))
+    specs = [pl.BlockSpec(memory_space=pltpu.SMEM)] + [pl.BlockSpec(memory_space=pltpu.VMEM)] * (ZH + 3)
     param, *news = whole(
         update_kernel,
-        ((PADDED, 128), BF16),
-        *[((GROUP, 128), F32)] * 3,
+        ((Y, PADDED, 128), BF16),
+        *[((ROWS, 128), F32)] * 3,
         *[((2, 128), F32)] * 3,
         name="update",
-    )(norm, key_grad, gain_grad, states)
-
-    param = lax.all_gather(param, "y", axis=0, tiled=False)
+        in_specs=specs,
+    )(zh.astype(jnp.int32).reshape(1), norm, key_grad, gain_grad, *states)
+
+    param = exchange(param, "y")
     specs = [pl.BlockSpec(memory_space=pltpu.SMEM)] + [pl.BlockSpec(memory_space=pltpu.VMEM)] * (X + 1)
     (keys,) = whole(keys_kernel, ((X, ROWS, 128), F32), name="keys", in_specs=specs)(
         me, *tokens, param
@@ -245,7 +268,7 @@
 
     return (
         next_keys.astype(BF16),
-        *[own(new) for new in news[:3]],
+        *news[:3],
         *[own(new.reshape(GROUP)) for new in news[3:]],
     )
 

time: 165 us -> 169 us (1.024)
  the two profiles are of different devices: /device:TPU:2 before, /device:TPU:64 now
where the time goes in v5:
time: 169 us; the launch traced here: 168 us
  starting transfers between devices  65.5 us (39%)
  waiting for transfers between devices  57.2 us (34%)
  blocking collectives  19.6 us (12%)
  Pallas kernels  13.9 us (8%)
  other arithmetic  5.87 us (3%)
  local copies, waits for them, and re-layouts  4.66 us (3%)
    all_to_all x6, waiting for transfers between devices, exchange(): return lax.all_to_all(array, axes, 0, 0, tiled=True)  45.2 us
    all_to_all x6, starting transfers between devices, exchange(): return lax.all_to_all(array, axes, 0, 0, tiled=True)  34 us
    ppermute x6, starting transfers between devices, shifts(): lax.ppermute(arrays[k] if isinstance(arrays, list) else arrays, axis, [(i...  31.5 us
    all_to_all x1, blocking collectives, exchange(): return lax.all_to_all(array, axes, 0, 0, tiled=True)  19.6 us
    ppermute x6, waiting for transfers between devices, shifts(): lax.ppermute(arrays[k] if isinstance(arrays, list) else arrays, axis, [(i...  12 us
    pallas_call x1, Pallas kernels, gradients(): pl.pallas_call(gradient_kernel, grid=(Y,), in_specs=[*[pl.BlockSpec((toke...  10 us
    convert_element_type x1, other arithmetic, local(): grads = exchange(grads.astype(F16), 'x')  3.89 us
  transfers between devices with their start and end apart: 12, of which 9 were waited for; matrix products, arithmetic and copies ran while one was open for 2% of the time, Pallas kernels for 1%

profile of v5, /device:TPU:64, one launch (start us, length us, event | category | flops | bytes accessed | tf_op | source)
XLA Modules:
  0.0 167.6 jit_solution(5682076680922136588)
XLA Ops:
  0.6 1.4 reshape.37.refs_4_.refs_5_.refs_6_.refs_7_
  2.0 10.0 %gradients.1 = f32[4,8,264,128]{3,2,1,0:T(8,128)} custom-call(bf16[512,8192]{1,0:T(8,128)(2,1)} %refs_3_.1, bf16[512,8192]{1,0:T(8,128)(2,1)} %refs_3_.1, bf16[512,8192]{1,0:T(8,128)(2,1)} %refs_3_.1, bf16[512,8192]{1,0:T(8,128)(2,1)} %refs_3_.1, bf16[1,8192]{1,0:T(2,128)(2,1)} %reshape.37.refs_4_.refs_5_.refs_6_.refs_7_, ...), custom_call_target="tpu_custom_call" | custom-call | flops 2147483648 | bytes 14680064 | tf_op jit(solution)/shard_map/gradients/pallas_call | solution.py:67
  12.0 3.9 %convert_element_type.27 = f16[4,8,264,128]{3,2,1,0:T(8,128)(2,1)} convert(f32[4,8,264,128]{3,2,1,0:T(8,128)} %gradients.1) | non-fusion elementwise | flops 1081344 | bytes 6488064 | tf_op jit(solution)/shard_map/convert_element_type | solution.py:225
  15.9 0.0 copy-start.2
  15.9 0.0 copy-start.3
  16.0 4.4 %all-to-all-start = ((f16[4,8,264,128]{3,2,1,0:T(8,128)(2,1)}), f16[4,8,264,128]{3,2,1,0:T(8,128)(2,1)S(1)}, u32[]{:S(2)}, u32[]{:S(2)}) async-start(f16[4,8,264,128]{3,2,1,0:T(8,128)(2,1)} %convert_element_type.27), calls=%async_computation | async-start | bytes 4325376 | tf_op jit(solution)/shard_map/all_to_all | solution.py:191
  20.4 0.0 copy-done.4
  20.4 0.0 copy-done.5
  20.4 0.0 copy-done.6
  20.5 27.0 %all-to-all-done = f16[4,8,264,128]{3,2,1,0:T(8,128)(2,1)S(1)} async-done(((f16[4,8,264,128]{3,2,1,0:T(8,128)(2,1)}), f16[4,8,264,128]{3,2,1,0:T(8,128)(2,1)S(1)}, u32[]{:S(2)}, u32[]{:S(2)}) %all-to-all-start) | async-done | bytes 2162720 | tf_op jit(solution)/shard_map/all_to_all | solution.py:191
  47.4 0.3 convert_reduce_fusion
  47.7 0.0 copy-start
  47.7 0.9 multiply_convert_fusion
  48.7 7.1 %all-to-all-start.1 = ((f16[8,264,128]{2,1,0:T(8,128)(2,1)}), f16[8,264,128]{2,1,0:T(8,128)(2,1)S(1)}, u32[]{:S(2)}, u32[]{:S(2)}) async-start(f16[8,264,128]{2,1,0:T(8,128)(2,1)} %multiply_convert_fusion), calls=%async_computation.1 | async-start | bytes 1081344 | tf_op jit(solution)/shard_map/all_to_all | solution.py:191
  55.8 9.1 %collective-permute-start = (f32[200,128]{1,0:T(8,128)S(1)}, f32[200,128]{1,0:T(8,128)S(1)}, u32[]{:S(2)}, u32[]{:S(2)}) collective-permute-start(f32[200,128]{1,0:T(8,128)S(1)} %pad_maximum_fusion.refs_0_), channel_id=1, source_target_pairs={{0,192},{192,384},{384,576},{576,0},{1,193},{193,385},{385,577},{5... | collective-permute-start | bytes 307208 | tf_op jit(solution)/shard_map/ppermute | solution.py:196
  64.9 10.3 %collective-permute-start.1 = (f32[200,128]{1,0:T(8,128)S(1)}, f32[200,128]{1,0:T(8,128)S(1)}, u32[]{:S(2)}, u32[]{:S(2)}) collective-permute-start(f32[200,128]{1,0:T(8,128)S(1)} %pad_maximum_fusion.refs_0_), channel_id=1, source_target_pairs={{0,384},{192,576},{384,0},{576,192},{1,385},{193,577},{385,1},{577... | collective-permute-start | bytes 307208 | tf_op jit(solution)/shard_map/ppermute | solution.py:196
  75.2 3.0 %collective-permute-start.2 = (f32[200,128]{1,0:T(8,128)S(1)}, f32[200,128]{1,0:T(8,128)S(1)}, u32[]{:S(2)}, u32[]{:S(2)}) collective-permute-start(f32[200,128]{1,0:T(8,128)S(1)} %pad_maximum_fusion.refs_0_), channel_id=1, source_target_pairs={{0,576},{192,0},{384,192},{576,384},{1,577},{193,1},{385,193},{577... | collective-permute-start | bytes 307208 | tf_op jit(solution)/shard_map/ppermute | solution.py:196
  78.3 0.5 tokens.1
  78.7 0.0 collective-permute-done.refs_1_
  78.8 4.4 %collective-permute-done.1.refs_2_ = f32[200,128]{1,0:T(8,128)S(1)} collective-permute-done((f32[200,128]{1,0:T(8,128)S(1)}, f32[200,128]{1,0:T(8,128)S(1)}, u32[]{:S(2)}, u32[]{:S(2)}) %collective-permute-start.1) | collective-permute-done | bytes 102432 | tf_op jit(solution)/shard_map/ppermute | solution.py:196
  83.2 4.7 %collective-permute-done.2.refs_3_ = f32[200,128]{1,0:T(8,128)S(1)} collective-permute-done((f32[200,128]{1,0:T(8,128)S(1)}, f32[200,128]{1,0:T(8,128)S(1)}, u32[]{:S(2)}, u32[]{:S(2)}) %collective-permute-start.2) | collective-permute-done | bytes 102432 | tf_op jit(solution)/shard_map/ppermute | solution.py:196
  87.9 0.0 all-to-all-done.1
  87.9 0.1 convert_reduce_fusion.1
  88.0 0.7 broadcast_in_dim.2
  88.7 6.9 %all-to-all-start.2 = ((f16[4,264,128]{2,1,0:T(8,128)(2,1)}), f16[4,264,128]{2,1,0:T(8,128)(2,1)S(1)}, u32[]{:S(2)}, u32[]{:S(2)}) async-start(f16[4,264,128]{2,1,0:T(8,128)(2,1)} %broadcast_in_dim.2), calls=%async_computation.2 | async-start | bytes 540672 | tf_op jit(solution)/shard_map/all_to_all | solution.py:191
  95.6 0.8 slice_bitcast_fusion
  96.4 2.5 %collective-permute-start.3 = (bf16[64,2176]{1,0:T(8,128)(2,1)}, bf16[64,2176]{1,0:T(8,128)(2,1)S(1)}, u32[]{:S(2)}, u32[]{:S(2)}) collective-permute-start(bf16[64,2176]{1,0:T(8,128)(2,1)} %get-tuple-element.57), channel_id=1, source_target_pairs={{0,6},{6,12},{12,18},{18,0},{1,7},{7,13},{13,19},{19,1},{2,8},{8,1... | collective-permute-start | bytes 835592 | tf_op jit(solution)/shard_map/ppermute | solution.py:196
  98.9 4.0 %collective-permute-start.4 = (bf16[64,2176]{1,0:T(8,128)(2,1)S(1)}, bf16[64,2176]{1,0:T(8,128)(2,1)S(1)}, u32[]{:S(2)}, u32[]{:S(2)}) collective-permute-start(bf16[64,2176]{1,0:T(8,128)(2,1)S(1)} %get-tuple-element.56), channel_id=1, source_target_pairs={{0,12},{6,18},{12,0},{18,6},{1,13},{7,19},{13,1},{19,7},{2,14},{8,... | collective-permute-start | bytes 835592 | tf_op jit(solution)/shard_map/ppermute | solution.py:196
  102.9 2.6 %collective-permute-start.5 = (bf16[64,2176]{1,0:T(8,128)(2,1)S(1)}, bf16[64,2176]{1,0:T(8,128)(2,1)S(1)}, u32[]{:S(2)}, u32[]{:S(2)}) collective-permute-start(bf16[64,2176]{1,0:T(8,128)(2,1)S(1)} %get-tuple-element.55), channel_id=1, source_target_pairs={{0,18},{6,0},{12,6},{18,12},{1,19},{7,1},{13,7},{19,13},{2,20},{8,... | collective-permute-start | bytes 835592 | tf_op jit(solution)/shard_map/ppermute | solution.py:196
  105.5 4.0 %all-to-all-done.2 = f16[4,264,128]{2,1,0:T(8,128)(2,1)S(1)} async-done(((f16[4,264,128]{2,1,0:T(8,128)(2,1)}), f16[4,264,128]{2,1,0:T(8,128)(2,1)S(1)}, u32[]{:S(2)}, u32[]{:S(2)}) %all-to-all-start.2) | async-done | bytes 270368 | tf_op jit(solution)/shard_map/all_to_all | solution.py:191
  109.5 0.7 sum_zh.1
  110.2 3.3 %all-to-all-start.3 = ((f32[6,16,128]{2,1,0:T(8,128)}), f32[6,16,128]{2,1,0:T(8,128)S(1)}, u32[]{:S(2)}, u32[]{:S(2)}) async-start(f32[6,16,128]{2,1,0:T(8,128)} %get-tuple-element.34), calls=%async_computation.3 | async-start | bytes 98304 | tf_op jit(solution)/shard_map/all_to_all | solution.py:191
  113.5 0.5 collective-permute-done.3.refs_1_
  114.0 0.0 collective-permute-done.4.refs_2_
  114.0 2.3 %collective-permute-done.5.refs_3_ = bf16[64,2176]{1,0:T(8,128)(2,1)S(1)} collective-permute-done((bf16[64,2176]{1,0:T(8,128)(2,1)S(1)}, bf16[64,2176]{1,0:T(8,128)(2,1)S(1)}, u32[]{:S(2)}, u32[]{:S(2)}) %collective-permute-start.5) | collective-permute-done | bytes 278560 | tf_op jit(solution)/shard_map/ppermute | solution.py:196
  116.3 0.5 all-to-all-done.3.parts
  116.8 0.7 sum_heads.1
  117.5 8.9 %all-to-all-start.4 = ((f32[32,1,128]{2,1,0:T(1,128)}), f32[32,1,128]{2,1,0:T(1,128)S(1)}, u32[]{:S(2)}, u32[]{:S(2)}) async-start(f32[32,1,128]{2,1,0:T(1,128)} %get-tuple-element.41), calls=%async_computation.4 | async-start | bytes 32768 | tf_op jit(solution)/shard_map/all_to_all | solution.py:191
  126.5 9.7 %all-to-all-done.4.norm = f32[32,1,128]{2,1,0:T(1,128)S(1)} async-done(((f32[32,1,128]{2,1,0:T(1,128)}), f32[32,1,128]{2,1,0:T(1,128)S(1)}, u32[]{:S(2)}, u32[]{:S(2)}) %all-to-all-start.4) | async-done | bytes 16416 | tf_op jit(solution)/shard_map/all_to_all | solution.py:191
  136.1 0.7 update.1
  136.8 19.6 %all_to_all.35.refs_4_ = bf16[8,272,128]{2,1,0:T(8,128)(2,1)S(1)} all-to-all(bf16[8,272,128]{2,1,0:T(8,128)(2,1)S(1)} %get-tuple-element.48), channel_id=1, replica_groups=mesh['zh'=4,'y'=8,'x'=4,'zl'=3,'core'=2] {'y'}, dimensions={0} | all-to-all | bytes 1114112 | tf_op jit(solution)/shard_map/all_to_all | solution.py:191
  156.4 1.3 keys.1
  157.7 3.3 %all-to-all-start.6 = ((f32[4,64,128]{2,1,0:T(8,128)}), f32[4,64,128]{2,1,0:T(8,128)S(1)}, u32[]{:S(2)}, u32[]{:S(2)}) async-start(f32[4,64,128]{2,1,0:T(8,128)} %keys.1), calls=%async_computation.6 | async-start | bytes 262144 | tf_op jit(solution)/shard_map/all_to_all | solution.py:191
  161.0 0.6 dynamic_slice.10
  161.6 0.6 dynamic_slice.11
  162.2 0.6 dynamic_slice.9
  162.8 4.2 %all-to-all-done.6 = f32[4,64,128]{2,1,0:T(8,128)S(1)} async-done(((f32[4,64,128]{2,1,0:T(8,128)}), f32[4,64,128]{2,1,0:T(8,128)S(1)}, u32[]{:S(2)}, u32[]{:S(2)}) %all-to-all-start.6) | async-done | bytes 131104 | tf_op jit(solution)/shard_map/all_to_all | solution.py:191
  167.0 0.6 reduce_sum.29
  (12 shorter events, 0.1 us)
Async XLA Ops:
  15.9 4.5 %copy-start.4 = (f32[64]{0:T(128)S(1)}, f32[64]{0:T(128)}, u32[]{:S(2)}) copy-start(f32[64]{0:T(128)} %param.20) | copy-start | bytes 772
  15.9 4.5 %copy-start.5 = (f32[64]{0:T(128)S(1)}, f32[64]{0:T(128)}, u32[]{:S(2)}) copy-start(f32[64]{0:T(128)} %param.19) | copy-start | bytes 772
  15.9 4.5 %copy-start.6 = (f32[64]{0:T(128)S(1)}, f32[64]{0:T(128)}, u32[]{:S(2)}) copy-start(f32[64]{0:T(128)} %param.18) | copy-start | bytes 772
  15.9 4.5 %copy-start.1 = (f32[64,128]{1,0:T(8,128)S(1)}, f32[64,128]{1,0:T(8,128)}, u32[]{:S(2)}) copy-start(f32[64,128]{1,0:T(8,128)} %param.17) | copy-start | bytes 98308
  15.9 4.5 %copy-start.2 = (f32[64,128]{1,0:T(8,128)S(1)}, f32[64,128]{1,0:T(8,128)}, u32[]{:S(2)}) copy-start(f32[64,128]{1,0:T(8,128)} %param.16) | copy-start | bytes 98308
  15.9 4.5 %copy-start.3 = (f32[64,128]{1,0:T(8,128)S(1)}, f32[64,128]{1,0:T(8,128)}, u32[]{:S(2)}) copy-start(f32[64,128]{1,0:T(8,128)} %param.15) | copy-start | bytes 98308
  16.0 31.5 %all-to-all-start = ((f16[4,8,264,128]{3,2,1,0:T(8,128)(2,1)}), f16[4,8,264,128]{3,2,1,0:T(8,128)(2,1)S(1)}, u32[]{:S(2)}, u32[]{:S(2)}) async-start(f16[4,8,264,128]{3,2,1,0:T(8,128)(2,1)} %convert_element_type.27), calls=%async_computation | async-start | bytes 4325376 | tf_op jit(solution)/shard_map/all_to_all | solution.py:191
  47.7 30.5 %copy-start = (bf16[64,8192]{1,0:T(8,128)(2,1)S(1)}, bf16[64,8192]{1,0:T(8,128)(2,1)}, u32[]{:S(2)}) copy-start(bf16[64,8192]{1,0:T(8,128)(2,1)} %tokens.2) | copy-start | bytes 3145732
  48.7 39.2 %all-to-all-start.1 = ((f16[8,264,128]{2,1,0:T(8,128)(2,1)}), f16[8,264,128]{2,1,0:T(8,128)(2,1)S(1)}, u32[]{:S(2)}, u32[]{:S(2)}) async-start(f16[8,264,128]{2,1,0:T(8,128)(2,1)} %multiply_convert_fusion), calls=%async_computation.1 | async-start | bytes 1081344 | tf_op jit(solution)/shard_map/all_to_all | solution.py:191
  55.8 23.0 %collective-permute-start = (f32[200,128]{1,0:T(8,128)S(1)}, f32[200,128]{1,0:T(8,128)S(1)}, u32[]{:S(2)}, u32[]{:S(2)}) collective-permute-start(f32[200,128]{1,0:T(8,128)S(1)} %pad_maximum_fusion.refs_0_), channel_id=1, source_target_pairs={{0,192},{192,384},{384,576},{576,0},{1,193},{193,385},{385,577},{5... | collective-permute-start | bytes 307208 | tf_op jit(solution)/shard_map/ppermute | solution.py:196
  64.9 18.3 %collective-permute-start.1 = (f32[200,128]{1,0:T(8,128)S(1)}, f32[200,128]{1,0:T(8,128)S(1)}, u32[]{:S(2)}, u32[]{:S(2)}) collective-permute-start(f32[200,128]{1,0:T(8,128)S(1)} %pad_maximum_fusion.refs_0_), channel_id=1, source_target_pairs={{0,384},{192,576},{384,0},{576,192},{1,385},{193,577},{385,1},{577... | collective-permute-start | bytes 307208 | tf_op jit(solution)/shard_map/ppermute | solution.py:196
  75.2 12.7 %collective-permute-start.2 = (f32[200,128]{1,0:T(8,128)S(1)}, f32[200,128]{1,0:T(8,128)S(1)}, u32[]{:S(2)}, u32[]{:S(2)}) collective-permute-start(f32[200,128]{1,0:T(8,128)S(1)} %pad_maximum_fusion.refs_0_), channel_id=1, source_target_pairs={{0,576},{192,0},{384,192},{576,384},{1,577},{193,1},{385,193},{577... | collective-permute-start | bytes 307208 | tf_op jit(solution)/shard_map/ppermute | solution.py:196
  88.7 20.7 %all-to-all-start.2 = ((f16[4,264,128]{2,1,0:T(8,128)(2,1)}), f16[4,264,128]{2,1,0:T(8,128)(2,1)S(1)}, u32[]{:S(2)}, u32[]{:S(2)}) async-start(f16[4,264,128]{2,1,0:T(8,128)(2,1)} %broadcast_in_dim.2), calls=%async_computation.2 | async-start | bytes 540672 | tf_op jit(solution)/shard_map/all_to_all | solution.py:191
  96.4 17.6 %collective-permute-start.3 = (bf16[64,2176]{1,0:T(8,128)(2,1)}, bf16[64,2176]{1,0:T(8,128)(2,1)S(1)}, u32[]{:S(2)}, u32[]{:S(2)}) collective-permute-start(bf16[64,2176]{1,0:T(8,128)(2,1)} %get-tuple-element.57), channel_id=1, source_target_pairs={{0,6},{6,12},{12,18},{18,0},{1,7},{7,13},{13,19},{19,1},{2,8},{8,1... | collective-permute-start | bytes 835592 | tf_op jit(solution)/shard_map/ppermute | solution.py:196
  98.9 15.1 %collective-permute-start.4 = (bf16[64,2176]{1,0:T(8,128)(2,1)S(1)}, bf16[64,2176]{1,0:T(8,128)(2,1)S(1)}, u32[]{:S(2)}, u32[]{:S(2)}) collective-permute-start(bf16[64,2176]{1,0:T(8,128)(2,1)S(1)} %get-tuple-element.56), channel_id=1, source_target_pairs={{0,12},{6,18},{12,0},{18,6},{1,13},{7,19},{13,1},{19,7},{2,14},{8,... | collective-permute-start | bytes 835592 | tf_op jit(solution)/shard_map/ppermute | solution.py:196
  102.9 13.4 %collective-permute-start.5 = (bf16[64,2176]{1,0:T(8,128)(2,1)S(1)}, bf16[64,2176]{1,0:T(8,128)(2,1)S(1)}, u32[]{:S(2)}, u32[]{:S(2)}) collective-permute-start(bf16[64,2176]{1,0:T(8,128)(2,1)S(1)} %get-tuple-element.55), channel_id=1, source_target_pairs={{0,18},{6,0},{12,6},{18,12},{1,19},{7,1},{13,7},{19,13},{2,20},{8,... | collective-permute-start | bytes 835592 | tf_op jit(solution)/shard_map/ppermute | solution.py:196
  110.2 6.6 %all-to-all-start.3 = ((f32[6,16,128]{2,1,0:T(8,128)}), f32[6,16,128]{2,1,0:T(8,128)S(1)}, u32[]{:S(2)}, u32[]{:S(2)}) async-start(f32[6,16,128]{2,1,0:T(8,128)} %get-tuple-element.34), calls=%async_computation.3 | async-start | bytes 98304 | tf_op jit(solution)/shard_map/all_to_all | solution.py:191
  117.5 18.6 %all-to-all-start.4 = ((f32[32,1,128]{2,1,0:T(1,128)}), f32[32,1,128]{2,1,0:T(1,128)S(1)}, u32[]{:S(2)}, u32[]{:S(2)}) async-start(f32[32,1,128]{2,1,0:T(1,128)} %get-tuple-element.41), calls=%async_computation.4 | async-start | bytes 32768 | tf_op jit(solution)/shard_map/all_to_all | solution.py:191
  157.7 9.3 %all-to-all-start.6 = ((f32[4,64,128]{2,1,0:T(8,128)}), f32[4,64,128]{2,1,0:T(8,128)S(1)}, u32[]{:S(2)}, u32[]{:S(2)}) async-start(f32[4,64,128]{2,1,0:T(8,128)} %keys.1), calls=%async_computation.6 | async-start | bytes 262144 | tf_op jit(solution)/shard_map/all_to_all | solution.py:191

commit v6 on v4

--- a/solution.py
+++ b/solution.py
@@ -119,11 +119,11 @@
 def update_kernel(norm, grad, gain, states, param, *outs):
     total = jnp.sum(norm[...], axis=0)
     clip = jnp.minimum(1.0, 1.0 / (jnp.sqrt(total) + 1e-06))
-    wide = jnp.broadcast_to(clip[None], (ROWS // 8, 8, 128)).reshape(ROWS, 128)
     for z in range(ZH):
         span = slice(z * ROWS, (z + 1) * ROWS)
-        new = adam_update(wide * grad[span], *[states[z, i * ROWS : (i + 1) * ROWS] for i in range(3)], 0.1)
-        param[span] = new[0].astype(BF16)
+        new = adam_update(clip * grad[span], *[states[z, i * ROWS : (i + 1) * ROWS] for i in range(3)], 0.1)
+        for y in range(Y):
+            param[y, span] = new[0].astype(BF16)
         for i in range(3):
             outs[i][span] = new[i]
     state = []
@@ -132,8 +132,10 @@
         part = [states[z, row : row + 1, :ROWS] for z in range(ZH)]
         pairs = [jnp.concatenate(part[j : j + 2], axis=1) for j in (0, 2)]
         state.append(jnp.concatenate(pairs, axis=0))
-    new = adam_update(clip[:2] * gain[:2], *state, 0.0)
-    param[GROUP:] = jnp.concatenate([new[0], jnp.zeros((14, 128), F32)], axis=0).astype(BF16)
+    new = adam_update(clip * gain[:2], *state, 0.0)
+    tile = jnp.concatenate([new[0], jnp.zeros((14, 128), F32)], axis=0).astype(BF16)
+    for y in range(Y):
+        param[y, GROUP:] = tile
     for i in range(3):
         outs[3 + i][...] = new[i]
 
@@ -204,15 +206,16 @@
     grads = exchange(grads.astype(F16), "x")
     me = lax.axis_index("x").astype(jnp.int32).reshape(1)
     specs = [pl.BlockSpec(memory_space=pltpu.SMEM), pl.BlockSpec(memory_space=pltpu.VMEM)]
+    grads, states = lax.optimization_barrier((grads, states))
+    grads = (jnp.sum(grads.astype(F32), axis=0) * SUM_SCALE).astype(F16)
+    grads, next_input = lax.optimization_barrier((exchange(grads, "y"), next_input))
     (tokens,) = whole(
         tokens_kernel, ((X, ROWS, WIDTH + 128), BF16), name="tokens", in_specs=specs
     )(me, next_input)
-    grads, tokens, states = lax.optimization_barrier((grads, tokens, states))
     tokens = [tokens[0]] + [
         lax.ppermute(tokens[k], "x", [(i, (i + k) % X) for i in range(X)]) for k in range(1, X)
     ]
-    grads = (jnp.sum(grads.astype(F32), axis=0) * SUM_SCALE).astype(F16)
-    grads = jnp.sum(exchange(grads, "y").astype(F32), axis=0) * LAST_SCALE
+    grads = jnp.sum(grads.astype(F32), axis=0) * LAST_SCALE
     grads = jnp.broadcast_to(grads.astype(F16)[None], (ZH,) + grads.shape)
     grads = exchange(grads, "zh").astype(F32)
     heads = ZL * CORE
@@ -222,18 +225,18 @@
 
     shared, *tokens = lax.optimization_barrier((exchange(shared, TENSOR), *tokens))
     gain_grad, norm = whole(
-        sum_heads_kernel, ((8, 128), F32), ((Y * X, 8, 128), F32), name="sum_heads"
+        sum_heads_kernel, ((8, 128), F32), ((Y * X, 1, 128), F32), name="sum_heads"
     )(shared)
     norm = exchange(norm, ("y", "x"))
     param, *news = whole(
         update_kernel,
-        ((PADDED, 128), BF16),
+        ((Y, PADDED, 128), BF16),
         *[((GROUP, 128), F32)] * 3,
         *[((2, 128), F32)] * 3,
         name="update",
     )(norm, key_grad, gain_grad, states)
 
-    param = lax.all_gather(param, "y", axis=0, tiled=False)
+    param = exchange(param, "y")
     specs = [pl.BlockSpec(memory_space=pltpu.SMEM)] + [pl.BlockSpec(memory_space=pltpu.VMEM)] * (X + 1)
     (keys,) = whole(keys_kernel, ((X, ROWS, 128), F32), name="keys", in_specs=specs)(
         me, *tokens, param

time: 165 us -> 157 us (0.952)
  blocking collectives: 66.6 us -> 31.1 us
  waiting for transfers between devices: 19.4 us -> 43.7 us
  starting transfers between devices: 51.2 us -> 55.6 us
    all_gather x1 -> x0, blocking collectives: 25.6 us -> none  [local(): param = lax.all_gather(param, 'y', axis=0, tiled=False)]
    all_to_all x5 -> x6, waiting for transfers between devices: 19.3 us -> 43.7 us  [exchange(): return lax.all_to_all(array, axes, 0, 0, tiled=True)]
    all_to_all x1, blocking collectives: 23.1 us -> 13.1 us  [exchange(): return lax.all_to_all(array, axes, 0, 0, tiled=True)]
    all_to_all x5 -> x6, starting transfers between devices: 41.4 us -> 45.8 us  [exchange(): return lax.all_to_all(array, axes, 0, 0, tiled=True)]
    reduce_sum x1, other arithmetic: 2.05 us -> 0.29 us  [local(): grads = (jnp.sum(grads.astype(F32), axis=0) * SUM_SCALE).astype(F16)]
  transfers between devices with their start and end apart: 8 -> 9, of which waited for: 4 -> 5; matrix products, arithmetic and copies ran while one was open for 2% -> 2% of each run, Pallas kernels for 1% -> 1%
where the time goes in v6:
time: 157 us; the launch traced here: 156 us
  starting transfers between devices  55.6 us (35%)
  waiting for transfers between devices  43.7 us (28%)
  blocking collectives  31.1 us (20%)
  Pallas kernels  13.6 us (9%)
  other arithmetic  5.85 us (4%)
  local copies, waits for them, and re-layouts  5.21 us (3%)
    all_to_all x6, starting transfers between devices, exchange(): return lax.all_to_all(array, axes, 0, 0, tiled=True)  45.8 us
    all_to_all x6, waiting for transfers between devices, exchange(): return lax.all_to_all(array, axes, 0, 0, tiled=True)  43.7 us
    all_gather x1, blocking collectives, local(): states = lax.all_gather(state, 'zh', axis=0, tiled=False)  18 us
    all_to_all x1, blocking collectives, exchange(): return lax.all_to_all(array, axes, 0, 0, tiled=True)  13.1 us
    pallas_call x1, Pallas kernels, gradients(): pl.pallas_call(gradient_kernel, grid=(Y,), in_specs=[*[pl.BlockSpec((toke...  10.1 us
    ppermute x3, starting transfers between devices, local(): lax.ppermute(tokens[k], 'x', [(i, (i + k) % X) for i in range(X)])  9.82 us
    convert_element_type x1, other arithmetic, local(): grads = exchange(grads.astype(F16), 'x')  3.88 us
  transfers between devices with their start and end apart: 9, of which 5 were waited for; matrix products, arithmetic and copies ran while one was open for 2% of the time, Pallas kernels for 1%

profile of v6, /device:TPU:2, one launch (start us, length us, event | category | flops | bytes accessed | tf_op | source)
XLA Modules:
  0.0 155.9 jit_solution(13380873472758850516)
XLA Ops:
  0.6 1.4 reshape.34.refs_4_.refs_5_.refs_6_.refs_7_
  2.0 10.1 %gradients.1 = f32[4,8,264,128]{3,2,1,0:T(8,128)} custom-call(bf16[512,8192]{1,0:T(8,128)(2,1)} %refs_3_.1, bf16[512,8192]{1,0:T(8,128)(2,1)} %refs_3_.1, bf16[512,8192]{1,0:T(8,128)(2,1)} %refs_3_.1, bf16[512,8192]{1,0:T(8,128)(2,1)} %refs_3_.1, bf16[1,8192]{1,0:T(2,128)(2,1)} %reshape.34.refs_4_.refs_5_.refs_6_.refs_7_, ...), custom_call_target="tpu_custom_call" | custom-call | flops 2147483648 | bytes 14680064 | tf_op jit(solution)/shard_map/gradients/pallas_call | solution.py:67
  12.1 3.9 %convert_element_type.27 = f16[4,8,264,128]{3,2,1,0:T(8,128)(2,1)} convert(f32[4,8,264,128]{3,2,1,0:T(8,128)} %gradients.1) | non-fusion elementwise | flops 1081344 | bytes 6488064 | tf_op jit(solution)/shard_map/convert_element_type | solution.py:206
  16.0 0.0 copy-start.2
  16.0 0.0 copy-start.3
  16.0 13.3 %all-to-all-start = ((f16[4,8,264,128]{3,2,1,0:T(8,128)(2,1)}), f16[4,8,264,128]{3,2,1,0:T(8,128)(2,1)S(1)}, u32[]{:S(2)}, u32[]{:S(2)}) async-start(f16[4,8,264,128]{3,2,1,0:T(8,128)(2,1)} %convert_element_type.27), calls=%async_computation | async-start | bytes 4325376 | tf_op jit(solution)/shard_map/all_to_all | solution.py:182
  29.3 0.0 copy-done.4
  29.3 0.0 copy-done.5
  29.3 0.0 copy-done.6
  29.3 0.0 copy-done.1
  29.3 0.0 copy-done.2
  29.3 0.0 copy-done.3
  29.3 18.0 %all-gather = f32[800,128]{1,0:T(8,128)S(1)} all-gather(f32[200,128]{1,0:T(8,128)S(1)} %pad_maximum_fusion), channel_id=2, replica_groups=mesh['zh'=4,'y'=8,'x'=4,'zl'=3,'core'=2] {'zh'}, dimensions={0}, use_global_device_ids=true | all-gather | bytes 512000 | tf_op jit(solution)/shard_map/all_gather | solution.py:203
  47.4 0.0 all-to-all-done
  47.4 0.3 convert_reduce_fusion
  47.7 0.9 multiply_convert_fusion
  48.6 7.3 %all-to-all-start.1 = ((f16[8,264,128]{2,1,0:T(8,128)(2,1)}), f16[8,264,128]{2,1,0:T(8,128)(2,1)S(1)}, u32[]{:S(2)}, u32[]{:S(2)}) async-start(f16[8,264,128]{2,1,0:T(8,128)(2,1)} %multiply_convert_fusion), calls=%async_computation.1 | async-start | bytes 1081344 | tf_op jit(solution)/shard_map/all_to_all | solution.py:182
  55.9 16.5 %all-to-all-done.1 = f16[8,264,128]{2,1,0:T(8,128)(2,1)S(1)} async-done(((f16[8,264,128]{2,1,0:T(8,128)(2,1)}), f16[8,264,128]{2,1,0:T(8,128)(2,1)S(1)}, u32[]{:S(2)}, u32[]{:S(2)}) %all-to-all-start.1) | async-done | bytes 540704 | tf_op jit(solution)/shard_map/all_to_all | solution.py:182
  72.4 0.1 convert_reduce_fusion.1
  72.5 0.7 broadcast_in_dim.2
  73.2 13.6 %all-to-all-start.2 = ((f16[4,264,128]{2,1,0:T(8,128)(2,1)}), f16[4,264,128]{2,1,0:T(8,128)(2,1)S(1)}, u32[]{:S(2)}, u32[]{:S(2)}) async-start(f16[4,264,128]{2,1,0:T(8,128)(2,1)} %broadcast_in_dim.2), calls=%async_computation.2 | async-start | bytes 540672 | tf_op jit(solution)/shard_map/all_to_all | solution.py:182
  86.8 0.0 copy-done
  86.8 0.5 tokens.1
  87.3 0.1 slice_bitcast_fusion
  87.4 1.9 %collective-permute-start = (bf16[64,2176]{1,0:T(8,128)(2,1)S(1)}, bf16[64,2176]{1,0:T(8,128)(2,1)S(1)}, u32[]{:S(2)}, u32[]{:S(2)}) collective-permute-start(bf16[64,2176]{1,0:T(8,128)(2,1)S(1)} %get-tuple-element.49), channel_id=1, source_target_pairs={{0,6},{6,12},{12,18},{18,0},{1,7},{7,13},{13,19},{19,1},{2,8},{8,1... | collective-permute-start | bytes 835592 | tf_op jit(solution)/shard_map/ppermute | solution.py:216
  89.4 5.4 %collective-permute-start.1 = (bf16[64,2176]{1,0:T(8,128)(2,1)S(1)}, bf16[64,2176]{1,0:T(8,128)(2,1)S(1)}, u32[]{:S(2)}, u32[]{:S(2)}) collective-permute-start(bf16[64,2176]{1,0:T(8,128)(2,1)S(1)} %get-tuple-element.48), channel_id=1, source_target_pairs={{0,12},{6,18},{12,0},{18,6},{1,13},{7,19},{13,1},{19,7},{2,14},{8,... | collective-permute-start | bytes 835592 | tf_op jit(solution)/shard_map/ppermute | solution.py:216
  94.8 2.5 %collective-permute-start.2 = (bf16[64,2176]{1,0:T(8,128)(2,1)S(1)}, bf16[64,2176]{1,0:T(8,128)(2,1)S(1)}, u32[]{:S(2)}, u32[]{:S(2)}) collective-permute-start(bf16[64,2176]{1,0:T(8,128)(2,1)S(1)} %get-tuple-element.47), channel_id=1, source_target_pairs={{0,18},{6,0},{12,6},{18,12},{1,19},{7,1},{13,7},{19,13},{2,20},{8,... | collective-permute-start | bytes 835592 | tf_op jit(solution)/shard_map/ppermute | solution.py:216
  97.2 4.0 %all-to-all-done.2 = f16[4,264,128]{2,1,0:T(8,128)(2,1)S(1)} async-done(((f16[4,264,128]{2,1,0:T(8,128)(2,1)}), f16[4,264,128]{2,1,0:T(8,128)(2,1)S(1)}, u32[]{:S(2)}, u32[]{:S(2)}) %all-to-all-start.2) | async-done | bytes 270368 | tf_op jit(solution)/shard_map/all_to_all | solution.py:182
  101.2 0.7 sum_zh.1
  101.9 3.3 %all-to-all-start.3 = ((f32[6,16,128]{2,1,0:T(8,128)}), f32[6,16,128]{2,1,0:T(8,128)S(1)}, u32[]{:S(2)}, u32[]{:S(2)}) async-start(f32[6,16,128]{2,1,0:T(8,128)} %get-tuple-element.29), calls=%async_computation.3 | async-start | bytes 98304 | tf_op jit(solution)/shard_map/all_to_all | solution.py:182
  105.3 0.0 collective-permute-done.refs_1_
  105.3 0.0 collective-permute-done.1.refs_2_
  105.3 0.0 collective-permute-done.2.refs_3_
  105.3 4.9 %all-to-all-done.3.parts = f32[6,16,128]{2,1,0:T(8,128)S(1)} async-done(((f32[6,16,128]{2,1,0:T(8,128)}), f32[6,16,128]{2,1,0:T(8,128)S(1)}, u32[]{:S(2)}, u32[]{:S(2)}) %all-to-all-start.3) | async-done | bytes 49184 | tf_op jit(solution)/shard_map/all_to_all | solution.py:182
  110.2 0.1 sum_heads.1
  110.4 13.1 %all_to_all.35.norm = f32[32,1,128]{2,1,0:T(1,128)S(1)} all-to-all(f32[32,1,128]{2,1,0:T(1,128)S(1)} %get-tuple-element.36), channel_id=1, replica_groups=mesh['zh'=4,'y'=8,'x'=4,'zl'=3,'core'=2] {'y','x'}, dimensions={0} | all-to-all | bytes 32768 | tf_op jit(solution)/shard_map/all_to_all | solution.py:182
  123.4 1.0 update.1
  124.4 3.5 %all-to-all-start.5 = ((bf16[8,272,128]{2,1,0:T(8,128)(2,1)}), bf16[8,272,128]{2,1,0:T(8,128)(2,1)S(1)}, u32[]{:S(2)}, u32[]{:S(2)}) async-start(bf16[8,272,128]{2,1,0:T(8,128)(2,1)} %get-tuple-element.40), calls=%async_computation.5 | async-start | bytes 1114112 | tf_op jit(solution)/shard_map/all_to_all | solution.py:182
  128.0 0.6 dynamic_slice.21
  128.6 0.6 dynamic_slice.22
  129.2 0.6 dynamic_slice.23
  129.7 0.6 constant_dynamic-slice_fusion
  130.4 14.4 %all-to-all-done.5.refs_4_ = bf16[8,272,128]{2,1,0:T(8,128)(2,1)S(1)} async-done(((bf16[8,272,128]{2,1,0:T(8,128)(2,1)}), bf16[8,272,128]{2,1,0:T(8,128)(2,1)S(1)}, u32[]{:S(2)}, u32[]{:S(2)}) %all-to-all-start.5) | async-done | bytes 557088 | tf_op jit(solution)/shard_map/all_to_all | solution.py:182
  144.8 1.3 keys.1
  146.0 4.7 %all-to-all-start.6 = ((f32[4,64,128]{2,1,0:T(8,128)}), f32[4,64,128]{2,1,0:T(8,128)S(1)}, u32[]{:S(2)}, u32[]{:S(2)}) async-start(f32[4,64,128]{2,1,0:T(8,128)} %keys.1), calls=%async_computation.6 | async-start | bytes 262144 | tf_op jit(solution)/shard_map/all_to_all | solution.py:182
  150.8 0.6 constant_dynamic-slice_fusion.2
  151.4 3.9 %all-to-all-done.6 = f32[4,64,128]{2,1,0:T(8,128)S(1)} async-done(((f32[4,64,128]{2,1,0:T(8,128)}), f32[4,64,128]{2,1,0:T(8,128)S(1)}, u32[]{:S(2)}, u32[]{:S(2)}) %all-to-all-start.6) | async-done | bytes 131104 | tf_op jit(solution)/shard_map/all_to_all | solution.py:182
  155.3 0.6 reduce_sum.29
  (9 shorter events, 0.1 us)
Async XLA Ops:
  15.9 13.3 %copy-start.4 = (f32[64]{0:T(128)S(1)}, f32[64]{0:T(128)}, u32[]{:S(2)}) copy-start(f32[64]{0:T(128)} %param.20) | copy-start | bytes 772
  15.9 13.3 %copy-start.5 = (f32[64]{0:T(128)S(1)}, f32[64]{0:T(128)}, u32[]{:S(2)}) copy-start(f32[64]{0:T(128)} %param.19) | copy-start | bytes 772
  15.9 13.3 %copy-start.6 = (f32[64]{0:T(128)S(1)}, f32[64]{0:T(128)}, u32[]{:S(2)}) copy-start(f32[64]{0:T(128)} %param.18) | copy-start | bytes 772
  16.0 13.3 %copy-start.1 = (f32[64,128]{1,0:T(8,128)S(1)}, f32[64,128]{1,0:T(8,128)}, u32[]{:S(2)}) copy-start(f32[64,128]{1,0:T(8,128)} %param.17) | copy-start | bytes 98308
  16.0 13.3 %copy-start.2 = (f32[64,128]{1,0:T(8,128)S(1)}, f32[64,128]{1,0:T(8,128)}, u32[]{:S(2)}) copy-start(f32[64,128]{1,0:T(8,128)} %param.16) | copy-start | bytes 98308
  16.0 13.3 %copy-start.3 = (f32[64,128]{1,0:T(8,128)S(1)}, f32[64,128]{1,0:T(8,128)}, u32[]{:S(2)}) copy-start(f32[64,128]{1,0:T(8,128)} %param.15) | copy-start | bytes 98308
  16.0 31.4 %all-to-all-start = ((f16[4,8,264,128]{3,2,1,0:T(8,128)(2,1)}), f16[4,8,264,128]{3,2,1,0:T(8,128)(2,1)S(1)}, u32[]{:S(2)}, u32[]{:S(2)}) async-start(f16[4,8,264,128]{3,2,1,0:T(8,128)(2,1)} %convert_element_type.27), calls=%async_computation | async-start | bytes 4325376 | tf_op jit(solution)/shard_map/all_to_all | solution.py:182
  48.6 23.8 %all-to-all-start.1 = ((f16[8,264,128]{2,1,0:T(8,128)(2,1)}), f16[8,264,128]{2,1,0:T(8,128)(2,1)S(1)}, u32[]{:S(2)}, u32[]{:S(2)}) async-start(f16[8,264,128]{2,1,0:T(8,128)(2,1)} %multiply_convert_fusion), calls=%async_computation.1 | async-start | bytes 1081344 | tf_op jit(solution)/shard_map/all_to_all | solution.py:182
  55.9 31.0 %copy-start = (bf16[64,8192]{1,0:T(8,128)(2,1)S(1)}, bf16[64,8192]{1,0:T(8,128)(2,1)}, u32[]{:S(2)}) copy-start(bf16[64,8192]{1,0:T(8,128)(2,1)} %tokens.2) | copy-start | bytes 3145732
  73.2 27.9 %all-to-all-start.2 = ((f16[4,264,128]{2,1,0:T(8,128)(2,1)}), f16[4,264,128]{2,1,0:T(8,128)(2,1)S(1)}, u32[]{:S(2)}, u32[]{:S(2)}) async-start(f16[4,264,128]{2,1,0:T(8,128)(2,1)} %broadcast_in_dim.2), calls=%async_computation.2 | async-start | bytes 540672 | tf_op jit(solution)/shard_map/all_to_all | solution.py:182
  87.4 17.9 %collective-permute-start = (bf16[64,2176]{1,0:T(8,128)(2,1)S(1)}, bf16[64,2176]{1,0:T(8,128)(2,1)S(1)}, u32[]{:S(2)}, u32[]{:S(2)}) collective-permute-start(bf16[64,2176]{1,0:T(8,128)(2,1)S(1)} %get-tuple-element.49), channel_id=1, source_target_pairs={{0,6},{6,12},{12,18},{18,0},{1,7},{7,13},{13,19},{19,1},{2,8},{8,1... | collective-permute-start | bytes 835592 | tf_op jit(solution)/shard_map/ppermute | solution.py:216
  89.4 15.9 %collective-permute-start.1 = (bf16[64,2176]{1,0:T(8,128)(2,1)S(1)}, bf16[64,2176]{1,0:T(8,128)(2,1)S(1)}, u32[]{:S(2)}, u32[]{:S(2)}) collective-permute-start(bf16[64,2176]{1,0:T(8,128)(2,1)S(1)} %get-tuple-element.48), channel_id=1, source_target_pairs={{0,12},{6,18},{12,0},{18,6},{1,13},{7,19},{13,1},{19,7},{2,14},{8,... | collective-permute-start | bytes 835592 | tf_op jit(solution)/shard_map/ppermute | solution.py:216
  94.8 10.5 %collective-permute-start.2 = (bf16[64,2176]{1,0:T(8,128)(2,1)S(1)}, bf16[64,2176]{1,0:T(8,128)(2,1)S(1)}, u32[]{:S(2)}, u32[]{:S(2)}) collective-permute-start(bf16[64,2176]{1,0:T(8,128)(2,1)S(1)} %get-tuple-element.47), channel_id=1, source_target_pairs={{0,18},{6,0},{12,6},{18,12},{1,19},{7,1},{13,7},{19,13},{2,20},{8,... | collective-permute-start | bytes 835592 | tf_op jit(solution)/shard_map/ppermute | solution.py:216
  101.9 8.3 %all-to-all-start.3 = ((f32[6,16,128]{2,1,0:T(8,128)}), f32[6,16,128]{2,1,0:T(8,128)S(1)}, u32[]{:S(2)}, u32[]{:S(2)}) async-start(f32[6,16,128]{2,1,0:T(8,128)} %get-tuple-element.29), calls=%async_computation.3 | async-start | bytes 98304 | tf_op jit(solution)/shard_map/all_to_all | solution.py:182
  124.4 20.3 %all-to-all-start.5 = ((bf16[8,272,128]{2,1,0:T(8,128)(2,1)}), bf16[8,272,128]{2,1,0:T(8,128)(2,1)S(1)}, u32[]{:S(2)}, u32[]{:S(2)}) async-start(bf16[8,272,128]{2,1,0:T(8,128)(2,1)} %get-tuple-element.40), calls=%async_computation.5 | async-start | bytes 1114112 | tf_op jit(solution)/shard_map/all_to_all | solution.py:182
  146.0 9.3 %all-to-all-start.6 = ((f32[4,64,128]{2,1,0:T(8,128)}), f32[4,64,128]{2,1,0:T(8,128)S(1)}, u32[]{:S(2)}, u32[]{:S(2)}) async-start(f32[4,64,128]{2,1,0:T(8,128)} %keys.1), calls=%async_computation.6 | async-start | bytes 262144 | tf_op jit(solution)/shard_map/all_to_all | solution.py:182

commit v7 on v6

--- a/solution.py
+++ b/solution.py
@@ -44,7 +44,8 @@
     gains = []
     for z in range(ZH):
         saved = normed[z][...].astype(F32)
-        scaled = (saved * gain[z][...].astype(F32)).astype(BF16)
+        pair = gain[z][0].astype(F32)
+        scaled = (saved * jnp.concatenate([pair[0:1], pair[1:2]], axis=1)).astype(BF16)
         both = [scaled, normed[z][...]]
         term, inner = [
             lax.dot_general(cot, rows, (((0,), (0,)), ((), ())), preferred_element_type=F32)
@@ -63,13 +64,13 @@
 
 def gradients(normed, key_cot, key_weight, norm_gain):
     tokens = normed.shape[0]
-    gain = norm_gain.reshape(1, -1)
+    gain = norm_gain.reshape(-1, 2, 128)
     return pl.pallas_call(
         gradient_kernel,
         grid=(Y,),
         in_specs=[
             *[pl.BlockSpec((tokens, GROUP), lambda y, z=z: (0, z * Y + y)) for z in range(ZH)],
-            *[pl.BlockSpec((1, GROUP), lambda y, z=z: (0, z * Y + y)) for z in range(ZH)],
+            *[pl.BlockSpec((1, 2, 128), lambda y, z=z: (z * Y + y, 0, 0)) for z in range(ZH)],
             *[pl.BlockSpec((GROUP, 128), lambda y, z=z: (z * Y + y, 0)) for z in range(ZH)],
             pl.BlockSpec((tokens, 128), lambda y: (0, 0)),
         ],
@@ -208,22 +209,23 @@
     specs = [pl.BlockSpec(memory_space=pltpu.SMEM), pl.BlockSpec(memory_space=pltpu.VMEM)]
     grads, states = lax.optimization_barrier((grads, states))
     grads = (jnp.sum(grads.astype(F32), axis=0) * SUM_SCALE).astype(F16)
-    grads, next_input = lax.optimization_barrier((exchange(grads, "y"), next_input))
+    grads, next_input = lax.optimization_barrier((grads, next_input))
     (tokens,) = whole(
         tokens_kernel, ((X, ROWS, WIDTH + 128), BF16), name="tokens", in_specs=specs
     )(me, next_input)
     tokens = [tokens[0]] + [
         lax.ppermute(tokens[k], "x", [(i, (i + k) % X) for i in range(X)]) for k in range(1, X)
     ]
-    grads = jnp.sum(grads.astype(F32), axis=0) * LAST_SCALE
-    grads = jnp.broadcast_to(grads.astype(F16)[None], (ZH,) + grads.shape)
-    grads = exchange(grads, "zh").astype(F32)
+    grads = jnp.sum(exchange(grads, "y").astype(F32), axis=0) * LAST_SCALE
+    grads = lax.all_gather(grads.astype(F16), "zh", axis=0, tiled=False)
+    grads, *tokens = lax.optimization_barrier((grads, *tokens))
+    grads = grads.astype(F32)
     heads = ZL * CORE
     key_grad, shared = whole(
         sum_zh_kernel, ((GROUP, 128), F32), ((heads, 16, 128), F32), name="sum_zh"
     )(grads)
 
-    shared, *tokens = lax.optimization_barrier((exchange(shared, TENSOR), *tokens))
+    shared = exchange(shared, TENSOR)
     gain_grad, norm = whole(
         sum_heads_kernel, ((8, 128), F32), ((Y * X, 1, 128), F32), name="sum_heads"
     )(shared)

time: 157 us -> 154 us (0.981)
  blocking collectives: 31.1 us -> 65.4 us
  waiting for transfers between devices: 43.7 us -> 23.6 us
  starting transfers between devices: 55.6 us -> 39.8 us
  local copies, waits for them, and re-layouts: 5.21 us -> 3.11 us
  other arithmetic: 5.85 us -> 7.6 us
    all_gather x0 -> x1, blocking collectives: none -> 24.9 us  [local(): grads = lax.all_gather(grads.astype(F16), 'zh', axis=0, tiled=False)]
    all_to_all x6 -> x4, waiting for transfers between devices: 43.7 us -> 23.6 us  [exchange(): return lax.all_to_all(array, axes, 0, 0, tiled=True)]
    all_to_all x6 -> x4, starting transfers between devices: 45.8 us -> 29.3 us  [exchange(): return lax.all_to_all(array, axes, 0, 0, tiled=True)]
    all_to_all x1 -> x2, blocking collectives: 13.1 us -> 22.4 us  [exchange(): return lax.all_to_all(array, axes, 0, 0, tiled=True)]
    reduce_sum x1, other arithmetic: 0.29 us -> 2.05 us  [local(): grads = (jnp.sum(grads.astype(F32), axis=0) * SUM_SCALE).astype(F16)]
  transfers between devices with their start and end apart: 9 -> 7, of which waited for: 5 -> 3; matrix products, arithmetic and copies ran while one was open for 2% -> 2% of each run, Pallas kernels for 1% -> 0%
where the time goes in v7:
time: 154 us; the launch traced here: 153 us
  blocking collectives  65.4 us (42%)
  starting transfers between devices  39.8 us (26%)
  waiting for transfers between devices  23.6 us (15%)
  Pallas kernels  13.1 us (9%)
  other arithmetic  7.6 us (5%)
  local copies, waits for them, and re-layouts  3.11 us (2%)
    all_to_all x4, starting transfers between devices, exchange(): return lax.all_to_all(array, axes, 0, 0, tiled=True)  29.3 us
    all_gather x1, blocking collectives, local(): grads = lax.all_gather(grads.astype(F16), 'zh', axis=0, tiled=False)  24.9 us
    all_to_all x4, waiting for transfers between devices, exchange(): return lax.all_to_all(array, axes, 0, 0, tiled=True)  23.6 us
    all_to_all x2, blocking collectives, exchange(): return lax.all_to_all(array, axes, 0, 0, tiled=True)  22.4 us
    all_gather x1, blocking collectives, local(): states = lax.all_gather(state, 'zh', axis=0, tiled=False)  18 us
    ppermute x3, starting transfers between devices, local(): lax.ppermute(tokens[k], 'x', [(i, (i + k) % X) for i in range(X)])  10.4 us
    pallas_call x1, Pallas kernels, gradients(): pl.pallas_call(gradient_kernel, grid=(Y,), in_specs=[*[pl.BlockSpec((toke...  10.2 us
    convert_element_type x1, other arithmetic, local(): grads = exchange(grads.astype(F16), 'x')  3.89 us
  transfers between devices with their start and end apart: 7, of which 3 were waited for; matrix products, arithmetic and copies ran while one was open for 2% of the time, Pallas kernels for 0%

profile of v7, /device:TPU:2, one launch (start us, length us, event | category | flops | bytes accessed | tf_op | source)
XLA Modules:
  0.0 153.3 jit_solution(3789173436080056461)
XLA Ops:
  0.6 10.2 %gradients.1 = f32[4,8,264,128]{3,2,1,0:T(8,128)} custom-call(bf16[512,8192]{1,0:T(8,128)(2,1)} %refs_3_.1, bf16[512,8192]{1,0:T(8,128)(2,1)} %refs_3_.1, bf16[512,8192]{1,0:T(8,128)(2,1)} %refs_3_.1, bf16[512,8192]{1,0:T(8,128)(2,1)} %refs_3_.1, bf16[32,2,128]{2,1,0:T(2,128)(2,1)} %bitcast.23, bf16[32,2,128]{2,1,0:T(2,128)(2,1)} %bitcast.24, ...), custom_call_target="tpu_custom_call" | custom-call | flops 2147483648 | bytes 14680064 | tf_op jit(solution)/shard_map/gradients/pallas_call | solution.py:68
  10.8 3.9 %convert_element_type.33 = f16[4,8,264,128]{3,2,1,0:T(8,128)(2,1)} convert(f32[4,8,264,128]{3,2,1,0:T(8,128)} %gradients.1) | non-fusion elementwise | flops 1081344 | bytes 6488064 | tf_op jit(solution)/shard_map/convert_element_type | solution.py:207
  14.7 0.0 copy-start.4
  14.7 0.0 copy-start.5
  14.7 0.0 copy-start.6
  14.7 0.0 copy-start.1
  14.7 0.0 copy-start.2
  14.7 0.0 copy-start.3
  14.7 14.1 %all-to-all-start = ((f16[4,8,264,128]{3,2,1,0:T(8,128)(2,1)}), f16[4,8,264,128]{3,2,1,0:T(8,128)(2,1)}, u32[]{:S(2)}, u32[]{:S(2)}) async-start(f16[4,8,264,128]{3,2,1,0:T(8,128)(2,1)} %convert_element_type.33), calls=%async_computation | async-start | bytes 4325376 | tf_op jit(solution)/shard_map/all_to_all | solution.py:183
  28.8 0.0 copy-done.4
  28.8 0.0 copy-done.5
  28.8 0.0 copy-done.6
  28.9 0.0 copy-done.1
  28.9 0.0 copy-done.2
  28.9 0.0 copy-done.3
  28.9 18.0 %all-gather = f32[800,128]{1,0:T(8,128)S(1)} all-gather(f32[200,128]{1,0:T(8,128)S(1)} %pad_maximum_fusion), channel_id=2, replica_groups=mesh['zh'=4,'y'=8,'x'=4,'zl'=3,'core'=2] {'zh'}, dimensions={0}, use_global_device_ids=true | all-gather | bytes 512000 | tf_op jit(solution)/shard_map/all_gather | solution.py:204
  46.9 0.0 all-to-all-done
  46.9 2.0 %convert_reduce_fusion = f32[8,264,128]{2,1,0:T(8,128)S(1)} fusion(f16[4,8,264,128]{3,2,1,0:T(8,128)(2,1)} %all-to-all-done), kind=kLoop, calls=%fused_computation | loop fusion | flops 1892352 | bytes 3244032 | tf_op jit(solution)/shard_map/reduce_sum | solution.py:211
  49.0 0.0 copy-start
  49.0 0.9 multiply_convert_fusion
  49.9 7.0 %all-to-all-start.1 = ((f16[8,264,128]{2,1,0:T(8,128)(2,1)}), f16[8,264,128]{2,1,0:T(8,128)(2,1)S(1)}, u32[]{:S(2)}, u32[]{:S(2)}) async-start(f16[8,264,128]{2,1,0:T(8,128)(2,1)} %multiply_convert_fusion), calls=%async_computation.1 | async-start | bytes 1081344 | tf_op jit(solution)/shard_map/all_to_all | solution.py:183
  56.9 0.0 copy-done
  56.9 0.5 tokens.1
  57.4 0.1 slice_bitcast_fusion
  57.5 3.4 %collective-permute-start = (bf16[64,2176]{1,0:T(8,128)(2,1)S(1)}, bf16[64,2176]{1,0:T(8,128)(2,1)S(1)}, u32[]{:S(2)}, u32[]{:S(2)}) collective-permute-start(bf16[64,2176]{1,0:T(8,128)(2,1)S(1)} %get-tuple-element.49), channel_id=1, source_target_pairs={{0,6},{6,12},{12,18},{18,0},{1,7},{7,13},{13,19},{19,1},{2,8},{8,1... | collective-permute-start | bytes 835592 | tf_op jit(solution)/shard_map/ppermute | solution.py:217
  60.8 2.9 %collective-permute-start.1 = (bf16[64,2176]{1,0:T(8,128)(2,1)S(1)}, bf16[64,2176]{1,0:T(8,128)(2,1)S(1)}, u32[]{:S(2)}, u32[]{:S(2)}) collective-permute-start(bf16[64,2176]{1,0:T(8,128)(2,1)S(1)} %get-tuple-element.48), channel_id=1, source_target_pairs={{0,12},{6,18},{12,0},{18,6},{1,13},{7,19},{13,1},{19,7},{2,14},{8,... | collective-permute-start | bytes 835592 | tf_op jit(solution)/shard_map/ppermute | solution.py:217
  63.8 4.1 %collective-permute-start.2 = (bf16[64,2176]{1,0:T(8,128)(2,1)S(1)}, bf16[64,2176]{1,0:T(8,128)(2,1)S(1)}, u32[]{:S(2)}, u32[]{:S(2)}) collective-permute-start(bf16[64,2176]{1,0:T(8,128)(2,1)S(1)} %get-tuple-element.47), channel_id=1, source_target_pairs={{0,18},{6,0},{12,6},{18,12},{1,19},{7,1},{13,7},{19,13},{2,20},{8,... | collective-permute-start | bytes 835592 | tf_op jit(solution)/shard_map/ppermute | solution.py:217
  67.9 5.3 %all-to-all-done.1 = f16[8,264,128]{2,1,0:T(8,128)(2,1)S(1)} async-done(((f16[8,264,128]{2,1,0:T(8,128)(2,1)}), f16[8,264,128]{2,1,0:T(8,128)(2,1)S(1)}, u32[]{:S(2)}, u32[]{:S(2)}) %all-to-all-start.1) | async-done | bytes 540704 | tf_op jit(solution)/shard_map/all_to_all | solution.py:183
  73.2 0.1 convert_reduce_fusion.1
  73.3 24.9 %all-gather.1 = f16[1056,128]{1,0:T(8,128)(2,1)S(1)} all-gather(f16[264,128]{1,0:T(8,128)(2,1)S(1)} %multiply_convert_fusion.1), channel_id=3, replica_groups=mesh['zh'=4,'y'=8,'x'=4,'zl'=3,'core'=2] {'zh'}, dimensions={0}, use_global_device_ids=true | all-gather | bytes 337920 | tf_op jit(solution)/shard_map/all_gather | solution.py:220
  98.2 0.0 collective-permute-done.refs_1_
  98.2 0.0 collective-permute-done.1.refs_2_
  98.2 0.0 collective-permute-done.2.refs_3_
  98.3 8.8 %all_to_all.30.parts = f32[6,16,128]{2,1,0:T(8,128)S(1)} all-to-all(f32[6,16,128]{2,1,0:T(8,128)S(1)} %get-tuple-element.35), channel_id=1, replica_groups=mesh['zh'=4,'y'=8,'x'=4,'zl'=3,'core'=2] {'zl','core'}, dimensions={0} | all-to-all | bytes 98304 | tf_op jit(solution)/shard_map/all_to_all | solution.py:183
  107.1 0.1 sum_heads.1
  107.3 13.6 %all_to_all.31.norm = f32[32,1,128]{2,1,0:T(1,128)S(1)} all-to-all(f32[32,1,128]{2,1,0:T(1,128)S(1)} %get-tuple-element.36), channel_id=1, replica_groups=mesh['zh'=4,'y'=8,'x'=4,'zl'=3,'core'=2] {'y','x'}, dimensions={0} | all-to-all | bytes 32768 | tf_op jit(solution)/shard_map/all_to_all | solution.py:183
  120.9 1.0 update.1
  121.9 3.5 %all-to-all-start.4 = ((bf16[8,272,128]{2,1,0:T(8,128)(2,1)}), bf16[8,272,128]{2,1,0:T(8,128)(2,1)S(1)}, u32[]{:S(2)}, u32[]{:S(2)}) async-start(bf16[8,272,128]{2,1,0:T(8,128)(2,1)} %get-tuple-element.40), calls=%async_computation.4 | async-start | bytes 1114112 | tf_op jit(solution)/shard_map/all_to_all | solution.py:183
  125.4 0.6 dynamic_slice.21
  126.0 0.6 dynamic_slice.22
  126.6 0.6 dynamic_slice.23
  127.2 0.6 constant_dynamic-slice_fusion
  127.8 14.4 %all-to-all-done.4.refs_4_ = bf16[8,272,128]{2,1,0:T(8,128)(2,1)S(1)} async-done(((bf16[8,272,128]{2,1,0:T(8,128)(2,1)}), bf16[8,272,128]{2,1,0:T(8,128)(2,1)S(1)}, u32[]{:S(2)}, u32[]{:S(2)}) %all-to-all-start.4) | async-done | bytes 557088 | tf_op jit(solution)/shard_map/all_to_all | solution.py:183
  142.2 1.3 keys.1
  143.5 4.7 %all-to-all-start.5 = ((f32[4,64,128]{2,1,0:T(8,128)}), f32[4,64,128]{2,1,0:T(8,128)S(1)}, u32[]{:S(2)}, u32[]{:S(2)}) async-start(f32[4,64,128]{2,1,0:T(8,128)} %keys.1), calls=%async_computation.5 | async-start | bytes 262144 | tf_op jit(solution)/shard_map/all_to_all | solution.py:183
  148.2 0.6 constant_dynamic-slice_fusion.2
  148.8 3.9 %all-to-all-done.5 = f32[4,64,128]{2,1,0:T(8,128)S(1)} async-done(((f32[4,64,128]{2,1,0:T(8,128)}), f32[4,64,128]{2,1,0:T(8,128)S(1)}, u32[]{:S(2)}, u32[]{:S(2)}) %all-to-all-start.5) | async-done | bytes 131104 | tf_op jit(solution)/shard_map/all_to_all | solution.py:183
  152.7 0.6 reduce_sum.29
  (5 shorter events, 0.1 us)
Async XLA Ops:
  14.7 14.1 %copy-start.4 = (f32[64]{0:T(128)S(1)}, f32[64]{0:T(128)}, u32[]{:S(2)}) copy-start(f32[64]{0:T(128)} %param.20) | copy-start | bytes 772
  14.7 14.1 %copy-start.5 = (f32[64]{0:T(128)S(1)}, f32[64]{0:T(128)}, u32[]{:S(2)}) copy-start(f32[64]{0:T(128)} %param.19) | copy-start | bytes 772
  14.7 14.1 %copy-start.6 = (f32[64]{0:T(128)S(1)}, f32[64]{0:T(128)}, u32[]{:S(2)}) copy-start(f32[64]{0:T(128)} %param.18) | copy-start | bytes 772
  14.7 14.2 %copy-start.1 = (f32[64,128]{1,0:T(8,128)S(1)}, f32[64,128]{1,0:T(8,128)}, u32[]{:S(2)}) copy-start(f32[64,128]{1,0:T(8,128)} %param.17) | copy-start | bytes 98308
  14.7 14.2 %copy-start.2 = (f32[64,128]{1,0:T(8,128)S(1)}, f32[64,128]{1,0:T(8,128)}, u32[]{:S(2)}) copy-start(f32[64,128]{1,0:T(8,128)} %param.16) | copy-start | bytes 98308
  14.7 14.2 %copy-start.3 = (f32[64,128]{1,0:T(8,128)S(1)}, f32[64,128]{1,0:T(8,128)}, u32[]{:S(2)}) copy-start(f32[64,128]{1,0:T(8,128)} %param.15) | copy-start | bytes 98308
  14.7 32.2 %all-to-all-start = ((f16[4,8,264,128]{3,2,1,0:T(8,128)(2,1)}), f16[4,8,264,128]{3,2,1,0:T(8,128)(2,1)}, u32[]{:S(2)}, u32[]{:S(2)}) async-start(f16[4,8,264,128]{3,2,1,0:T(8,128)(2,1)} %convert_element_type.33), calls=%async_computation | async-start | bytes 4325376 | tf_op jit(solution)/shard_map/all_to_all | solution.py:183
  49.0 7.9 %copy-start = (bf16[64,8192]{1,0:T(8,128)(2,1)S(1)}, bf16[64,8192]{1,0:T(8,128)(2,1)}, u32[]{:S(2)}) copy-start(bf16[64,8192]{1,0:T(8,128)(2,1)} %tokens.2) | copy-start | bytes 3145732
  49.9 23.3 %all-to-all-start.1 = ((f16[8,264,128]{2,1,0:T(8,128)(2,1)}), f16[8,264,128]{2,1,0:T(8,128)(2,1)S(1)}, u32[]{:S(2)}, u32[]{:S(2)}) async-start(f16[8,264,128]{2,1,0:T(8,128)(2,1)} %multiply_convert_fusion), calls=%async_computation.1 | async-start | bytes 1081344 | tf_op jit(solution)/shard_map/all_to_all | solution.py:183
  57.5 40.7 %collective-permute-start = (bf16[64,2176]{1,0:T(8,128)(2,1)S(1)}, bf16[64,2176]{1,0:T(8,128)(2,1)S(1)}, u32[]{:S(2)}, u32[]{:S(2)}) collective-permute-start(bf16[64,2176]{1,0:T(8,128)(2,1)S(1)} %get-tuple-element.49), channel_id=1, source_target_pairs={{0,6},{6,12},{12,18},{18,0},{1,7},{7,13},{13,19},{19,1},{2,8},{8,1... | collective-permute-start | bytes 835592 | tf_op jit(solution)/shard_map/ppermute | solution.py:217
  60.8 37.4 %collective-permute-start.1 = (bf16[64,2176]{1,0:T(8,128)(2,1)S(1)}, bf16[64,2176]{1,0:T(8,128)(2,1)S(1)}, u32[]{:S(2)}, u32[]{:S(2)}) collective-permute-start(bf16[64,2176]{1,0:T(8,128)(2,1)S(1)} %get-tuple-element.48), channel_id=1, source_target_pairs={{0,12},{6,18},{12,0},{18,6},{1,13},{7,19},{13,1},{19,7},{2,14},{8,... | collective-permute-start | bytes 835592 | tf_op jit(solution)/shard_map/ppermute | solution.py:217
  63.8 34.4 %collective-permute-start.2 = (bf16[64,2176]{1,0:T(8,128)(2,1)S(1)}, bf16[64,2176]{1,0:T(8,128)(2,1)S(1)}, u32[]{:S(2)}, u32[]{:S(2)}) collective-permute-start(bf16[64,2176]{1,0:T(8,128)(2,1)S(1)} %get-tuple-element.47), channel_id=1, source_target_pairs={{0,18},{6,0},{12,6},{18,12},{1,19},{7,1},{13,7},{19,13},{2,20},{8,... | collective-permute-start | bytes 835592 | tf_op jit(solution)/shard_map/ppermute | solution.py:217
  121.9 20.3 %all-to-all-start.4 = ((bf16[8,272,128]{2,1,0:T(8,128)(2,1)}), bf16[8,272,128]{2,1,0:T(8,128)(2,1)S(1)}, u32[]{:S(2)}, u32[]{:S(2)}) async-start(bf16[8,272,128]{2,1,0:T(8,128)(2,1)} %get-tuple-element.40), calls=%async_computation.4 | async-start | bytes 1114112 | tf_op jit(solution)/shard_map/all_to_all | solution.py:183
  143.5 9.3 %all-to-all-start.5 = ((f32[4,64,128]{2,1,0:T(8,128)}), f32[4,64,128]{2,1,0:T(8,128)S(1)}, u32[]{:S(2)}, u32[]{:S(2)}) async-start(f32[4,64,128]{2,1,0:T(8,128)} %keys.1), calls=%async_computation.5 | async-start | bytes 262144 | tf_op jit(solution)/shard_map/all_to_all | solution.py:183

commit v8 on v7

--- a/solution.py
+++ b/solution.py
@@ -24,6 +24,7 @@
 SUM_SCALE = 2.0**-2
 LAST_SCALE = 2.0**-3
 WIDTH = Y * GROUP
+STEP = 4
 F32 = jnp.float32
 BF16 = jnp.bfloat16
 F16 = jnp.float16
@@ -41,40 +42,45 @@
 def gradient_kernel(*refs):
     normed, gain, weight = refs[0:4], refs[4:8], refs[8:12]
     cot, out = refs[12][...], refs[13]
-    gains = []
-    for z in range(ZH):
-        saved = normed[z][...].astype(F32)
-        pair = gain[z][0].astype(F32)
-        scaled = (saved * jnp.concatenate([pair[0:1], pair[1:2]], axis=1)).astype(BF16)
-        both = [scaled, normed[z][...]]
-        term, inner = [
-            lax.dot_general(cot, rows, (((0,), (0,)), ((), ())), preferred_element_type=F32)
-            for rows in both
-        ]
-        term = term.T
+    for y in range(STEP):
+        span = slice(y * GROUP, (y + 1) * GROUP)
+        gains = []
+        for z in range(ZH):
+            saved = normed[z][:, span]
+            pair = gain[z][y].astype(F32)
+            row = jnp.concatenate([pair[0:1], pair[1:2]], axis=1)
+            scaled = (saved.astype(F32) * row).astype(BF16)
+            term, inner = [
+                lax.dot_general(cot, rows, (((0,), (0,)), ((), ())), preferred_element_type=F32)
+                for rows in (scaled, saved)
+            ]
+            term = term.T
+            for x in range(X):
+                out[x, y, z * ROWS : (z + 1) * ROWS, :] = term[x * ROWS : (x + 1) * ROWS]
+            products = weight[z][span].astype(F32).T * inner
+            gains.append(jnp.sum(products, axis=0, keepdims=True))
         for x in range(X):
-            out[x, 0, z * ROWS : (z + 1) * ROWS, :] = term[x * ROWS : (x + 1) * ROWS]
-        gains.append(jnp.sum(weight[z][...].astype(F32).T * inner, axis=0, keepdims=True))
-    for x in range(X):
-        part = [g[:, x * ROWS : (x + 1) * ROWS] for g in gains]
-        pairs = [jnp.concatenate(part[i : i + 2], axis=1) for i in (0, 2)]
-        rows = jnp.concatenate([*pairs, jnp.zeros((6, 128), F32)], axis=0)
-        out[x, 0, GROUP:, :] = rows * GAIN_SCALE
+            part = [g[:, x * ROWS : (x + 1) * ROWS] for g in gains]
+            pairs = [jnp.concatenate(part[i : i + 2], axis=1) for i in (0, 2)]
+            rows = jnp.concatenate([*pairs, jnp.zeros((6, 128), F32)], axis=0)
+            out[x, y, GROUP:, :] = rows * GAIN_SCALE
 
 
 def gradients(normed, key_cot, key_weight, norm_gain):
     tokens = normed.shape[0]
     gain = norm_gain.reshape(-1, 2, 128)
+    steps = Y // STEP
+    blocks = [lambda y, z=z: z * steps + y for z in range(ZH)]
     return pl.pallas_call(
         gradient_kernel,
-        grid=(Y,),
+        grid=(steps,),
         in_specs=[
-            *[pl.BlockSpec((tokens, GROUP), lambda y, z=z: (0, z * Y + y)) for z in range(ZH)],
-            *[pl.BlockSpec((1, 2, 128), lambda y, z=z: (z * Y + y, 0, 0)) for z in range(ZH)],
-            *[pl.BlockSpec((GROUP, 128), lambda y, z=z: (z * Y + y, 0)) for z in range(ZH)],
+            *[pl.BlockSpec((tokens, STEP * GROUP), lambda y, b=b: (0, b(y))) for b in blocks],
+            *[pl.BlockSpec((STEP, 2, 128), lambda y, b=b: (b(y), 0, 0)) for b in blocks],
+            *[pl.BlockSpec((STEP * GROUP, 128), lambda y, b=b: (b(y), 0)) for b in blocks],
             pl.BlockSpec((tokens, 128), lambda y: (0, 0)),
         ],
-        out_specs=pl.BlockSpec((X, 1, SUMMED, 128), lambda y: (0, y, 0, 0)),
+        out_specs=pl.BlockSpec((X, STEP, SUMMED, 128), lambda y: (0, y, 0, 0)),
         out_shape=jax.ShapeDtypeStruct((X, Y, SUMMED, 128), F32),
         compiler_params=pltpu.CompilerParams(vmem_limit_bytes=56 << 20),
         cost_estimate=pl.CostEstimate(
@@ -102,18 +108,17 @@
     weight = total[:GROUP] * (1.0 / (SUM_SCALE * LAST_SCALE))
     gain = total[GROUP:] * (1.0 / (SUM_SCALE * LAST_SCALE * GAIN_SCALE))
     grad[...] = weight
-    squares = jnp.sum((weight * weight).reshape(-1, 8, 128), axis=0)
+    squares = jnp.sum(weight * weight, axis=0, keepdims=True)
     for t in range(ZL * CORE):
-        shared[t, :8] = gain
-        shared[t, 8:] = squares
+        shared[t] = jnp.concatenate([gain[:2], squares, gain[2:3]], axis=0)
 
 
 def sum_heads_kernel(parts, gain, norm):
     total = parts[0]
     for t in range(1, ZL * CORE):
         total += parts[t]
-    gain[...] = total[:8]
-    square = jnp.sum(total[:8] * total[:8] + total[8:])
+    gain[...] = total
+    square = jnp.sum(total[:2] * total[:2]) + jnp.sum(total[2:3])
     norm[...] = jnp.broadcast_to(square, norm.shape)
 
 
@@ -222,12 +227,12 @@
     grads = grads.astype(F32)
     heads = ZL * CORE
     key_grad, shared = whole(
-        sum_zh_kernel, ((GROUP, 128), F32), ((heads, 16, 128), F32), name="sum_zh"
+        sum_zh_kernel, ((GROUP, 128), F32), ((heads, 4, 128), F32), name="sum_zh"
     )(grads)
 
     shared = exchange(shared, TENSOR)
     gain_grad, norm = whole(
-        sum_heads_kernel, ((8, 128), F32), ((Y * X, 1, 128), F32), name="sum_heads"
+        sum_heads_kernel, ((4, 128), F32), ((Y * X, 1, 128), F32), name="sum_heads"
     )(shared)
     norm = exchange(norm, ("y", "x"))
     param, *news = whole(

time: 154 us -> 151 us (0.981)
  the two profiles are of different devices: /device:TPU:2 before, /device:TPU:192 now
where the time goes in v8:
time: 151 us; the launch traced here: 150 us
  blocking collectives  71.6 us (47%)
  waiting for transfers between devices  28.6 us (19%)
  starting transfers between devices  28.3 us (19%)
  Pallas kernels  10.2 us (7%)
  other arithmetic  7.6 us (5%)
  local copies, waits for them, and re-layouts  3.12 us (2%)
    all_to_all x4, waiting for transfers between devices, exchange(): return lax.all_to_all(array, axes, 0, 0, tiled=True)  28.6 us
    all_gather x1, blocking collectives, local(): states = lax.all_gather(state, 'zh', axis=0, tiled=False)  25.2 us
    all_to_all x2, blocking collectives, exchange(): return lax.all_to_all(array, axes, 0, 0, tiled=True)  23.5 us
    all_gather x1, blocking collectives, local(): grads = lax.all_gather(grads.astype(F16), 'zh', axis=0, tiled=False)  22.9 us
    all_to_all x4, starting transfers between devices, exchange(): return lax.all_to_all(array, axes, 0, 0, tiled=True)  18.6 us
    ppermute x3, starting transfers between devices, local(): lax.ppermute(tokens[k], 'x', [(i, (i + k) % X) for i in range(X)])  9.73 us
    pallas_call x1, Pallas kernels, gradients(): pl.pallas_call(gradient_kernel, grid=(steps,), in_specs=[*[pl.BlockSpec((...  7.29 us
    convert_element_type x1, other arithmetic, local(): grads = exchange(grads.astype(F16), 'x')  3.89 us
  transfers between devices with their start and end apart: 7, of which 4 were waited for; matrix products, arithmetic and copies ran while one was open for 2% of the time, Pallas kernels for 0%

profile of v8, /device:TPU:192, one launch (start us, length us, event | category | flops | bytes accessed | tf_op | source)
XLA Modules:
  0.0 150.3 jit_solution(2342763739901433447)
XLA Ops:
  0.6 7.3 %gradients.1 = f32[4,8,264,128]{3,2,1,0:T(8,128)} custom-call(bf16[512,8192]{1,0:T(8,128)(2,1)} %refs_3_.1, bf16[512,8192]{1,0:T(8,128)(2,1)} %refs_3_.1, bf16[512,8192]{1,0:T(8,128)(2,1)} %refs_3_.1, bf16[512,8192]{1,0:T(8,128)(2,1)} %refs_3_.1, bf16[32,2,128]{2,1,0:T(2,128)(2,1)} %bitcast.23, bf16[32,2,128]{2,1,0:T(2,128)(2,1)} %bitcast.24, ...), custom_call_target="tpu_custom_call" | custom-call | flops 2147483648 | bytes 14680064 | tf_op jit(solution)/shard_map/gradients/pallas_call | solution.py:74
  7.9 3.9 %convert_element_type.33 = f16[4,8,264,128]{3,2,1,0:T(8,128)(2,1)} convert(f32[4,8,264,128]{3,2,1,0:T(8,128)} %gradients.1) | non-fusion elementwise | flops 1081344 | bytes 6488064 | tf_op jit(solution)/shard_map/convert_element_type | solution.py:212
  11.8 0.0 copy-start.4
  11.8 0.0 copy-start.5
  11.8 0.0 copy-start.6
  11.8 0.0 copy-start.2
  11.8 0.0 copy-start.3
  11.9 4.6 %all-to-all-start = ((f16[4,8,264,128]{3,2,1,0:T(8,128)(2,1)}), f16[4,8,264,128]{3,2,1,0:T(8,128)(2,1)}, u32[]{:S(2)}, u32[]{:S(2)}) async-start(f16[4,8,264,128]{3,2,1,0:T(8,128)(2,1)} %convert_element_type.33), calls=%async_computation | async-start | bytes 4325376 | tf_op jit(solution)/shard_map/all_to_all | solution.py:188
  16.5 0.0 copy-done.4
  16.5 0.0 copy-done.5
  16.5 0.0 copy-done.6
  16.5 0.0 copy-done.1
  16.5 0.0 copy-done.2
  16.5 0.0 copy-done.3
  16.5 25.2 %all-gather = f32[800,128]{1,0:T(8,128)S(1)} all-gather(f32[200,128]{1,0:T(8,128)S(1)} %pad_maximum_fusion), channel_id=2, replica_groups=mesh['zh'=4,'y'=8,'x'=4,'zl'=3,'core'=2] {'zh'}, dimensions={0}, use_global_device_ids=true | all-gather | bytes 512000 | tf_op jit(solution)/shard_map/all_gather | solution.py:209
  41.7 2.1 %all-to-all-done = f16[4,8,264,128]{3,2,1,0:T(8,128)(2,1)} async-done(((f16[4,8,264,128]{3,2,1,0:T(8,128)(2,1)}), f16[4,8,264,128]{3,2,1,0:T(8,128)(2,1)}, u32[]{:S(2)}, u32[]{:S(2)}) %all-to-all-start) | async-done | bytes 2162720 | tf_op jit(solution)/shard_map/all_to_all | solution.py:188
  43.8 2.0 %convert_reduce_fusion = f32[8,264,128]{2,1,0:T(8,128)S(1)} fusion(f16[4,8,264,128]{3,2,1,0:T(8,128)(2,1)} %all-to-all-done), kind=kLoop, calls=%fused_computation | loop fusion | flops 1892352 | bytes 3244032 | tf_op jit(solution)/shard_map/reduce_sum | solution.py:216
  45.9 0.0 copy-start
  45.9 0.9 multiply_convert_fusion
  46.8 7.1 %all-to-all-start.1 = ((f16[8,264,128]{2,1,0:T(8,128)(2,1)}), f16[8,264,128]{2,1,0:T(8,128)(2,1)S(1)}, u32[]{:S(2)}, u32[]{:S(2)}) async-start(f16[8,264,128]{2,1,0:T(8,128)(2,1)} %multiply_convert_fusion), calls=%async_computation.1 | async-start | bytes 1081344 | tf_op jit(solution)/shard_map/all_to_all | solution.py:188
  53.9 0.0 copy-done
  53.9 0.5 tokens.1
  54.4 0.1 slice_bitcast_fusion
  54.5 2.5 %collective-permute-start = (bf16[64,2176]{1,0:T(8,128)(2,1)S(1)}, bf16[64,2176]{1,0:T(8,128)(2,1)S(1)}, u32[]{:S(2)}, u32[]{:S(2)}) collective-permute-start(bf16[64,2176]{1,0:T(8,128)(2,1)S(1)} %get-tuple-element.49), channel_id=1, source_target_pairs={{0,6},{6,12},{12,18},{18,0},{1,7},{7,13},{13,19},{19,1},{2,8},{8,1... | collective-permute-start | bytes 835592 | tf_op jit(solution)/shard_map/ppermute | solution.py:222
  56.9 4.0 %collective-permute-start.1 = (bf16[64,2176]{1,0:T(8,128)(2,1)S(1)}, bf16[64,2176]{1,0:T(8,128)(2,1)S(1)}, u32[]{:S(2)}, u32[]{:S(2)}) collective-permute-start(bf16[64,2176]{1,0:T(8,128)(2,1)S(1)} %get-tuple-element.48), channel_id=1, source_target_pairs={{0,12},{6,18},{12,0},{18,6},{1,13},{7,19},{13,1},{19,7},{2,14},{8,... | collective-permute-start | bytes 835592 | tf_op jit(solution)/shard_map/ppermute | solution.py:222
  60.9 3.3 %collective-permute-start.2 = (bf16[64,2176]{1,0:T(8,128)(2,1)S(1)}, bf16[64,2176]{1,0:T(8,128)(2,1)S(1)}, u32[]{:S(2)}, u32[]{:S(2)}) collective-permute-start(bf16[64,2176]{1,0:T(8,128)(2,1)S(1)} %get-tuple-element.47), channel_id=1, source_target_pairs={{0,18},{6,0},{12,6},{18,12},{1,19},{7,1},{13,7},{19,13},{2,20},{8,... | collective-permute-start | bytes 835592 | tf_op jit(solution)/shard_map/ppermute | solution.py:222
  64.2 6.7 %all-to-all-done.1 = f16[8,264,128]{2,1,0:T(8,128)(2,1)S(1)} async-done(((f16[8,264,128]{2,1,0:T(8,128)(2,1)}), f16[8,264,128]{2,1,0:T(8,128)(2,1)S(1)}, u32[]{:S(2)}, u32[]{:S(2)}) %all-to-all-start.1) | async-done | bytes 540704 | tf_op jit(solution)/shard_map/all_to_all | solution.py:188
  70.9 0.1 convert_reduce_fusion.1
  71.0 22.9 %all-gather.1 = f16[1056,128]{1,0:T(8,128)(2,1)S(1)} all-gather(f16[264,128]{1,0:T(8,128)(2,1)S(1)} %multiply_convert_fusion.1), channel_id=3, replica_groups=mesh['zh'=4,'y'=8,'x'=4,'zl'=3,'core'=2] {'zh'}, dimensions={0}, use_global_device_ids=true | all-gather | bytes 337920 | tf_op jit(solution)/shard_map/all_gather | solution.py:225
  93.9 0.0 collective-permute-done.refs_1_
  93.9 0.0 collective-permute-done.1.refs_2_
  93.9 0.0 collective-permute-done.2.refs_3_
  93.9 0.1 sum_zh.1
  94.0 10.5 %all_to_all.30.parts = f32[6,4,128]{2,1,0:T(4,128)S(1)} all-to-all(f32[6,4,128]{2,1,0:T(4,128)S(1)} %get-tuple-element.35), channel_id=1, replica_groups=mesh['zh'=4,'y'=8,'x'=4,'zl'=3,'core'=2] {'zl','core'}, dimensions={0} | all-to-all | bytes 24576 | tf_op jit(solution)/shard_map/all_to_all | solution.py:188
  104.5 0.1 sum_heads.1
  104.7 13.0 %all_to_all.31.norm = f32[32,1,128]{2,1,0:T(1,128)S(1)} all-to-all(f32[32,1,128]{2,1,0:T(1,128)S(1)} %get-tuple-element.36), channel_id=1, replica_groups=mesh['zh'=4,'y'=8,'x'=4,'zl'=3,'core'=2] {'y','x'}, dimensions={0} | all-to-all | bytes 32768 | tf_op jit(solution)/shard_map/all_to_all | solution.py:188
  117.7 1.0 update.1
  118.7 3.5 %all-to-all-start.4 = ((bf16[8,272,128]{2,1,0:T(8,128)(2,1)}), bf16[8,272,128]{2,1,0:T(8,128)(2,1)S(1)}, u32[]{:S(2)}, u32[]{:S(2)}) async-start(bf16[8,272,128]{2,1,0:T(8,128)(2,1)} %get-tuple-element.40), calls=%async_computation.4 | async-start | bytes 1114112 | tf_op jit(solution)/shard_map/all_to_all | solution.py:188
  122.2 0.6 dynamic_slice.21
  122.8 0.6 dynamic_slice.22
  123.4 0.6 dynamic_slice.23
  124.0 0.6 constant_dynamic-slice_fusion
  124.6 14.5 %all-to-all-done.4.refs_4_ = bf16[8,272,128]{2,1,0:T(8,128)(2,1)S(1)} async-done(((bf16[8,272,128]{2,1,0:T(8,128)(2,1)}), bf16[8,272,128]{2,1,0:T(8,128)(2,1)S(1)}, u32[]{:S(2)}, u32[]{:S(2)}) %all-to-all-start.4) | async-done | bytes 557088 | tf_op jit(solution)/shard_map/all_to_all | solution.py:188
  139.1 1.3 keys.1
  140.4 3.3 %all-to-all-start.5 = ((f32[4,64,128]{2,1,0:T(8,128)}), f32[4,64,128]{2,1,0:T(8,128)S(1)}, u32[]{:S(2)}, u32[]{:S(2)}) async-start(f32[4,64,128]{2,1,0:T(8,128)} %keys.1), calls=%async_computation.5 | async-start | bytes 262144 | tf_op jit(solution)/shard_map/all_to_all | solution.py:188
  143.7 0.6 constant_dynamic-slice_fusion.2
  144.3 5.3 %all-to-all-done.5 = f32[4,64,128]{2,1,0:T(8,128)S(1)} async-done(((f32[4,64,128]{2,1,0:T(8,128)}), f32[4,64,128]{2,1,0:T(8,128)S(1)}, u32[]{:S(2)}, u32[]{:S(2)}) %all-to-all-start.5) | async-done | bytes 131104 | tf_op jit(solution)/shard_map/all_to_all | solution.py:188
  149.6 0.6 reduce_sum.29
  (5 shorter events, 0.1 us)
Async XLA Ops:
  11.8 4.6 %copy-start.4 = (f32[64]{0:T(128)S(1)}, f32[64]{0:T(128)}, u32[]{:S(2)}) copy-start(f32[64]{0:T(128)} %param.20) | copy-start | bytes 772
  11.8 4.6 %copy-start.5 = (f32[64]{0:T(128)S(1)}, f32[64]{0:T(128)}, u32[]{:S(2)}) copy-start(f32[64]{0:T(128)} %param.19) | copy-start | bytes 772
  11.8 4.7 %copy-start.6 = (f32[64]{0:T(128)S(1)}, f32[64]{0:T(128)}, u32[]{:S(2)}) copy-start(f32[64]{0:T(128)} %param.18) | copy-start | bytes 772
  11.8 4.7 %copy-start.1 = (f32[64,128]{1,0:T(8,128)S(1)}, f32[64,128]{1,0:T(8,128)}, u32[]{:S(2)}) copy-start(f32[64,128]{1,0:T(8,128)} %param.17) | copy-start | bytes 98308
  11.8 4.7 %copy-start.2 = (f32[64,128]{1,0:T(8,128)S(1)}, f32[64,128]{1,0:T(8,128)}, u32[]{:S(2)}) copy-start(f32[64,128]{1,0:T(8,128)} %param.16) | copy-start | bytes 98308
  11.8 4.7 %copy-start.3 = (f32[64,128]{1,0:T(8,128)S(1)}, f32[64,128]{1,0:T(8,128)}, u32[]{:S(2)}) copy-start(f32[64,128]{1,0:T(8,128)} %param.15) | copy-start | bytes 98308
  11.9 32.0 %all-to-all-start = ((f16[4,8,264,128]{3,2,1,0:T(8,128)(2,1)}), f16[4,8,264,128]{3,2,1,0:T(8,128)(2,1)}, u32[]{:S(2)}, u32[]{:S(2)}) async-start(f16[4,8,264,128]{3,2,1,0:T(8,128)(2,1)} %convert_element_type.33), calls=%async_computation | async-start | bytes 4325376 | tf_op jit(solution)/shard_map/all_to_all | solution.py:188
  45.9 8.0 %copy-start = (bf16[64,8192]{1,0:T(8,128)(2,1)S(1)}, bf16[64,8192]{1,0:T(8,128)(2,1)}, u32[]{:S(2)}) copy-start(bf16[64,8192]{1,0:T(8,128)(2,1)} %tokens.2) | copy-start | bytes 3145732
  46.8 24.1 %all-to-all-start.1 = ((f16[8,264,128]{2,1,0:T(8,128)(2,1)}), f16[8,264,128]{2,1,0:T(8,128)(2,1)S(1)}, u32[]{:S(2)}, u32[]{:S(2)}) async-start(f16[8,264,128]{2,1,0:T(8,128)(2,1)} %multiply_convert_fusion), calls=%async_computation.1 | async-start | bytes 1081344 | tf_op jit(solution)/shard_map/all_to_all | solution.py:188
  54.5 39.4 %collective-permute-start = (bf16[64,2176]{1,0:T(8,128)(2,1)S(1)}, bf16[64,2176]{1,0:T(8,128)(2,1)S(1)}, u32[]{:S(2)}, u32[]{:S(2)}) collective-permute-start(bf16[64,2176]{1,0:T(8,128)(2,1)S(1)} %get-tuple-element.49), channel_id=1, source_target_pairs={{0,6},{6,12},{12,18},{18,0},{1,7},{7,13},{13,19},{19,1},{2,8},{8,1... | collective-permute-start | bytes 835592 | tf_op jit(solution)/shard_map/ppermute | solution.py:222
  56.9 36.9 %collective-permute-start.1 = (bf16[64,2176]{1,0:T(8,128)(2,1)S(1)}, bf16[64,2176]{1,0:T(8,128)(2,1)S(1)}, u32[]{:S(2)}, u32[]{:S(2)}) collective-permute-start(bf16[64,2176]{1,0:T(8,128)(2,1)S(1)} %get-tuple-element.48), channel_id=1, source_target_pairs={{0,12},{6,18},{12,0},{18,6},{1,13},{7,19},{13,1},{19,7},{2,14},{8,... | collective-permute-start | bytes 835592 | tf_op jit(solution)/shard_map/ppermute | solution.py:222
  60.9 33.0 %collective-permute-start.2 = (bf16[64,2176]{1,0:T(8,128)(2,1)S(1)}, bf16[64,2176]{1,0:T(8,128)(2,1)S(1)}, u32[]{:S(2)}, u32[]{:S(2)}) collective-permute-start(bf16[64,2176]{1,0:T(8,128)(2,1)S(1)} %get-tuple-element.47), channel_id=1, source_target_pairs={{0,18},{6,0},{12,6},{18,12},{1,19},{7,1},{13,7},{19,13},{2,20},{8,... | collective-permute-start | bytes 835592 | tf_op jit(solution)/shard_map/ppermute | solution.py:222
  118.7 20.4 %all-to-all-start.4 = ((bf16[8,272,128]{2,1,0:T(8,128)(2,1)}), bf16[8,272,128]{2,1,0:T(8,128)(2,1)S(1)}, u32[]{:S(2)}, u32[]{:S(2)}) async-start(bf16[8,272,128]{2,1,0:T(8,128)(2,1)} %get-tuple-element.40), calls=%async_computation.4 | async-start | bytes 1114112 | tf_op jit(solution)/shard_map/all_to_all | solution.py:188
  140.4 9.3 %all-to-all-start.5 = ((f32[4,64,128]{2,1,0:T(8,128)}), f32[4,64,128]{2,1,0:T(8,128)S(1)}, u32[]{:S(2)}, u32[]{:S(2)}) async-start(f32[4,64,128]{2,1,0:T(8,128)} %keys.1), calls=%async_computation.5 | async-start | bytes 262144 | tf_op jit(solution)/shard_map/all_to_all | solution.py:188
